TPU v7x, 32 devices: a whole 2x2x4 slice. The times are simulated.
32 devices in a mesh: fsdp: 4 (over z), bal: 8 (over y, x, core).
Axes of the slice: x: 2, y: 2, z: 4, core: 2. Of those that a mesh axis runs over, the one named last changes fastest.
Arguments:
- tokens: bfloat16 [4096, 2048], P(('fsdp', 'bal')), may hold values from -6 to 6
- kv_weight: bfloat16 [2048, 1024], P('fsdp')
- queries: bfloat16 [4096, 2048], P(('fsdp', 'bal')), may hold values from -300 to 300
- out_grad: bfloat16 [4096, 2048], P(('fsdp', 'bal')), may hold values from -6 to 6
- doc_lengths: int32 [4, 4], P('fsdp'), may hold values from 1 to 512, 1024 in all within a row
Outputs:
- attn_out: bfloat16 [4096, 2048], P(('fsdp', 'bal'))
- grad_queries: bfloat16 [4096, 2048], P(('fsdp', 'bal'))
- grad_tokens: bfloat16 [4096, 2048], P(('fsdp', 'bal'))
- grad_kv_weight: float32 [2048, 1024], P('fsdp')
Inputs may be any that keep to these rules, and one draw needn't show every extreme that they name: Each row of doc_lengths sums to 1024, and its largest entry is exactly 512.
All inputs are finite; a program needn't handle non-finite values.
Results may differ from a plain program's by a relative error of at most 0.015.
Values may be sent and summed in bfloat16 or wider, within the bound.
No kernel may reach another device: no remote copies, remote signals or barrier semaphores. Data moves between devices by JAX's collectives and lax.ppermute only.
A program may use at most 64 MiB of HBM per device.

v0:
```python
import jax
import jax.numpy as jnp
from jax import lax
from jax.sharding import PartitionSpec as P

HEADS = 16
KV_HEADS = 4
HEAD_DIM = 128
REACH = 4


NEG_FILL = -1e30


def from_behind(value, axis, steps):
    count = lax.axis_size(axis)
    initial, last = (max(0, -steps), min(count, count - steps))
    return lax.ppermute(value, axis, [(source, source + steps) for source in range(initial, last)])


def doc_index(doc_ends, positions):
    return jnp.sum((doc_ends[None, :] <= positions[:, None]).astype(jnp.int32), axis=1)


def score_tile(q_group, key_block, mask_block, inv_root):
    raw_scores = (
        jnp.einsum("qhd,kd->hqk", q_group, key_block, preferred_element_type=jnp.float32) * inv_root
    )
    return jnp.where(mask_block[None], raw_scores, NEG_FILL)


def value_tile(prob_tile, value_block):
    return jnp.einsum("hqk,kd->qhd", prob_tile, value_block, preferred_element_type=jnp.float32)


def dprob_tile(grad_group, value_block):
    return jnp.einsum("qhd,kd->hqk", grad_group, value_block, preferred_element_type=jnp.float32)


def query_tile(dscore_tile, key_block):
    return jnp.einsum("hqk,kd->qhd", dscore_tile, key_block, preferred_element_type=jnp.float32)


def key_tile(dscore_tile, q_group, inv_root):
    return (
        jnp.einsum("hqk,qhd->kd", dscore_tile, q_group, preferred_element_type=jnp.float32)
        * inv_root
    )


def value_grad_tile(prob_tile, grad_group):
    return jnp.einsum("hqk,qhd->kd", prob_tile, grad_group, preferred_element_type=jnp.float32)


def attend(q_rows, kv_blocks, grad_rows, allowed_parts):
    row_count = q_rows.shape[0]
    key_rows = kv_blocks[0].shape[0]
    group_size = HEADS // KV_HEADS
    inv_root = HEAD_DIM ** (-0.5)
    window_range = list(range(len(kv_blocks)))
    row_shape = (row_count, group_size, HEAD_DIM)
    out_parts = []
    dq_parts = []
    key_grads = [[] for window_pos in window_range]
    value_grads = [[] for window_pos in window_range]
    for head_group in range(KV_HEADS):
        col_start = head_group * group_size * HEAD_DIM
        col_stop = col_start + group_size * HEAD_DIM
        val_start = (KV_HEADS + head_group) * HEAD_DIM
        q_group = q_rows[:, col_start:col_stop].reshape(row_shape)
        grad_group = grad_rows[:, col_start:col_stop].reshape(row_shape)
        key_list = [
            piece[:, head_group * HEAD_DIM : (head_group + 1) * HEAD_DIM] for piece in kv_blocks
        ]
        value_list = [piece[:, val_start : val_start + HEAD_DIM] for piece in kv_blocks]
        score_tiles = [
            score_tile(q_group, key_list[window_pos], allowed_parts[window_pos], inv_root)
            for window_pos in window_range
        ]
        scores = jnp.concatenate(score_tiles, axis=2)
        row_max = jnp.max(scores, axis=-1, keepdims=True)
        exp_shift = jnp.exp(scores - row_max)
        prob_full = exp_shift / jnp.sum(exp_shift, axis=-1, keepdims=True)
        prob_low = prob_full.astype(jnp.bfloat16)
        prob_tiles = [
            prob_low[:, :, window_pos * key_rows : (window_pos + 1) * key_rows]
            for window_pos in window_range
        ]
        out_accum = jnp.zeros(row_shape, jnp.float32)
        for window_pos in window_range:
            out_accum = out_accum + value_tile(prob_tiles[window_pos], value_list[window_pos])
        out_group = out_accum.astype(jnp.bfloat16)
        row_delta = jnp.sum(grad_group.astype(jnp.float32) * out_group.astype(jnp.float32), axis=-1)
        dprob_tiles = [
            dprob_tile(grad_group, value_list[window_pos]) for window_pos in window_range
        ]
        dprobs = jnp.concatenate(dprob_tiles, axis=2)
        dscores = (prob_full * (dprobs - row_delta.T[:, :, None])).astype(jnp.bfloat16)
        dq_accum = jnp.zeros(row_shape, jnp.float32)
        for window_pos in window_range:
            dscore_piece = dscores[:, :, window_pos * key_rows : (window_pos + 1) * key_rows]
            dq_accum = dq_accum + query_tile(dscore_piece, key_list[window_pos])
            key_grads[window_pos].append(key_tile(dscore_piece, q_group, inv_root))
            value_grads[window_pos].append(value_grad_tile(prob_tiles[window_pos], grad_group))
        dq_group = (dq_accum * inv_root).astype(jnp.bfloat16)
        out_parts.append(out_group.reshape(row_count, group_size * HEAD_DIM))
        dq_parts.append(dq_group.reshape(row_count, group_size * HEAD_DIM))
    window_terms = [
        jnp.concatenate(key_grads[window_pos] + value_grads[window_pos], axis=1)
        for window_pos in window_range
    ]
    return (jnp.concatenate(out_parts, axis=1), jnp.concatenate(dq_parts, axis=1), window_terms)


def local(tokens, kv_weight, queries, out_grad, doc_lengths):
    row_count = tokens.shape[0]
    bal_index = lax.axis_index("bal")
    doc_ends = jnp.cumsum(doc_lengths[0])
    row_ids = jnp.arange(row_count, dtype=jnp.int32)
    own_pos = bal_index * row_count + row_ids
    own_doc = doc_index(doc_ends, own_pos)
    allowed_parts = []
    for distance in range(REACH, -1, -1):
        key_pos = (bal_index - distance) * row_count + row_ids
        key_doc = jnp.where(key_pos >= 0, doc_index(doc_ends, key_pos), -1)
        allowed_parts.append(
            (own_doc[:, None] == key_doc[None, :]) & (key_pos[None, :] <= own_pos[:, None])
        )
    full_weight = lax.all_gather(kv_weight, "fsdp", axis=0, tiled=True)
    kv_accum = jnp.dot(tokens, full_weight, preferred_element_type=jnp.float32)
    kv_rows = kv_accum.astype(jnp.bfloat16)
    earlier = [kv_rows]
    for distance in range(1, REACH + 1):
        earlier.append(from_behind(kv_rows, "bal", distance))
    kv_blocks = earlier[::-1]
    attn_out, grad_queries, window_terms = attend(queries, kv_blocks, out_grad, allowed_parts)
    grad_terms = window_terms[::-1]
    grad_sum = grad_terms[0]
    for distance in range(1, REACH + 1):
        grad_sum = grad_sum + from_behind(
            grad_terms[distance].astype(jnp.bfloat16), "bal", -distance
        ).astype(jnp.float32)
    grad_kv = grad_sum.astype(jnp.bfloat16)
    grad_tokens = lax.dot_general(
        grad_kv, full_weight, (((1,), (1,)), ((), ())), preferred_element_type=jnp.float32
    ).astype(jnp.bfloat16)
    shard_sum = lax.psum_scatter(
        lax.dot_general(
            tokens, grad_kv, (((0,), (0,)), ((), ())), preferred_element_type=jnp.float32
        ).astype(jnp.bfloat16),
        "fsdp",
        scatter_dimension=0,
        tiled=True,
    )
    grad_weight = lax.psum(shard_sum, "bal").astype(jnp.float32)
    return (attn_out, grad_queries, grad_tokens, grad_weight)


def solution(mesh):
    placed = (
        P(("fsdp", "bal"), None),
        P("fsdp", None),
        P(("fsdp", "bal"), None),
        P(("fsdp", "bal"), None),
        P("fsdp", None),
    )
    return jax.shard_map(
        local,
        mesh=mesh,
        in_specs=placed,
        out_specs=(
            P(("fsdp", "bal"), None),
            P(("fsdp", "bal"), None),
            P(("fsdp", "bal"), None),
            P("fsdp", None),
        ),
        check_vma=False,
    )
```

profile of v0, /device:TPU:0, one launch (start us, length us, event | category | flops | bytes accessed | tf_op | source)
XLA Modules:
  0.0 314.1 jit_solution(15407342938714566075)
XLA Ops:
  9.1 84.0 %all-gather.2.cloned.1.call-done = bf16[2048,1024]{1,0:T(8,128)(2,1)} async-done(((bf16[512,1024]{1,0:T(8,128)(2,1)}), bf16[2048,1024]{1,0:T(8,128)(2,1)}) %all-gather.2.cloned.1.call-update) | async-done | bytes 4194320 | tf_op jit(solution)/shard_map/all_gather | solution.py:129
  93.1 2.9 convolution_convert_fusion.1
  96.0 3.4 %collective-permute-start = (bf16[128,1024]{1,0:T(8,128)(2,1)S(1)}, bf16[128,1024]{1,0:T(8,128)(2,1)S(1)}, u32[]{:S(2)}, u32[]{:S(2)}) collective-permute-start(bf16[128,1024]{1,0:T(8,128)(2,1)S(1)} %convolution_convert_fusion.1), channel_id=1, source_target_pairs={{0,4},{1,5},{2,6},{3,7},{8,12},{9,13},{10,14},{11,15},{16,20},{17,... | collective-permute-start | bytes 786440 | tf_op jit(solution)/shard_map/ppermute | solution.py:18
  99.4 2.4 collective-permute-start.1
  103.1 2.3 collective-permute-start.2
  105.4 1.7 collective-permute-start.3
  107.1 10.2 %collective-permute-done = bf16[128,1024]{1,0:T(8,128)(2,1)S(1)} collective-permute-done((bf16[128,1024]{1,0:T(8,128)(2,1)S(1)}, bf16[128,1024]{1,0:T(8,128)(2,1)S(1)}, u32[]{:S(2)}, u32[]{:S(2)}) %collective-permute-start) | collective-permute-done | bytes 262176 | tf_op jit(solution)/shard_map/ppermute | solution.py:18
  133.8 1.0 fusion.266
  135.2 1.7 multiply_reduce_fusion
  138.2 1.3 collective-permute-start.4
  141.9 1.5 collective-permute-start.5
  144.8 1.3 collective-permute-start.6
  147.6 1.3 collective-permute-start.7
  149.3 5.4 %collective-permute-done.5 = bf16[128,1024]{0,1:T(8,128)(2,1)S(1)} collective-permute-done((bf16[128,1024]{0,1:T(8,128)(2,1)S(1)}, bf16[128,1024]{0,1:T(8,128)(2,1)S(1)}, u32[]{:S(2)}, u32[]{:S(2)}) %collective-permute-start.5) | collective-permute-done | bytes 262176 | tf_op jit(solution)/shard_map/ppermute | solution.py:18
  154.6 2.2 collective-permute-done.6
  156.9 5.6 %collective-permute-done.7 = bf16[128,1024]{0,1:T(8,128)(2,1)S(1)} collective-permute-done((bf16[128,1024]{0,1:T(8,128)(2,1)S(1)}, bf16[128,1024]{0,1:T(8,128)(2,1)S(1)}, u32[]{:S(2)}, u32[]{:S(2)}) %collective-permute-start.7) | collective-permute-done | bytes 262176 | tf_op jit(solution)/shard_map/ppermute | solution.py:18
  162.6 3.2 %convert_bitcast_fusion = bf16[2048,1024]{0,1:T(8,128)(2,1)} fusion(bf16[128,1024]{0,1:T(8,128)(2,1)S(1)} %add_convert_fusion, bf16[128,2048]{1,0:T(8,128)(2,1)S(1)} %copy-done), kind=kOutput, calls=%fused_computation | convolution fusion | flops 538968064 | bytes 4980736 | tf_op jit(solution)/shard_map/dot_general | solution.py:148
  167.0 1.0 fusion.252
  169.9 1.0 fusion.100
  171.9 1.0 fusion.238
  172.9 1.0 fusion.235
  173.8 1.0 fusion.232
  174.8 1.0 fusion.101
  177.1 1.0 fusion.221
  179.1 1.0 fusion.102
  181.5 1.0 fusion.207
  182.5 1.0 fusion.204
  183.5 1.1 fusion.103
  186.1 58.5 %reduce-scatter.2.cloned.1.call-done = bf16[512,1024]{0,1:T(8,128)(2,1)} async-done(((bf16[2048,1024]{0,1:T(8,128)(2,1)}), bf16[512,1024]{0,1:T(8,128)(2,1)}) %reduce-scatter.2.cloned.1.call-update) | async-done | bytes 1048592 | tf_op jit(solution)/shard_map/reduce_scatter | solution.py:147
  245.4 4.5 %convolution_convert_fusion = bf16[128,2048]{1,0:T(8,128)(2,1)} fusion(bf16[128,1024]{0,1:T(8,128)(2,1)S(1)} %add_convert_fusion, bf16[2048,1024]{1,0:T(8,128)(2,1)} %all-gather.2.cloned.1.call-done), kind=kOutput, calls=%fused_computation.1 | convolution fusion | flops 537133056 | bytes 4980736 | tf_op jit(solution)/shard_map/dot_general | solution.py:144
  249.9 55.1 %all-reduce.2.cloned.1.call-done = bf16[512,1024]{0,1:T(8,128)(2,1)} async-done(((bf16[512,1024]{0,1:T(8,128)(2,1)}), bf16[512,1024]{0,1:T(8,128)(2,1)}) %all-reduce.2.cloned.1.call-update) | async-done | bytes 1048592 | tf_op jit(solution)/shard_map/psum | solution.py:155
  305.0 2.6 copy.535
  (195 shorter events, 36.3 us)
Async XLA Ops:
  7.2 85.9 %copy-start = (bf16[128,2048]{1,0:T(8,128)(2,1)S(1)}, bf16[128,2048]{1,0:T(8,128)(2,1)}, u32[]{:S(2)}) copy-start(bf16[128,2048]{1,0:T(8,128)(2,1)} %param.5) | copy-start | bytes 1572868
  7.2 1.8 copy-start.12
  7.2 1.8 copy-start.13
  7.2 85.9 %all-gather.2.cloned.1.call-start = ((), (), s32[]{:S(2)}) async-start(), calls=%async_computation.1 | async-start | bytes 5242880 | tf_op jit(solution)/shard_map/all_gather | solution.py:129
  7.9 236.6 %reduce-scatter.2.cloned.1.call-start = ((), (), s32[]{:S(2)}) async-start(), calls=%async_computation.2 | async-start | bytes 5242880 | tf_op jit(solution)/shard_map/reduce_scatter | solution.py:147
  96.0 33.4 %copy-start.3 = (bf16[128,1024]{1,0:T(8,128)(2,1)}, bf16[128,1024]{1,0:T(8,128)(2,1)S(1)}, u32[]{:S(2)}) copy-start(bf16[128,1024]{1,0:T(8,128)(2,1)S(1)} %convolution_convert_fusion.1) | copy-start | bytes 786436
  96.0 21.3 %collective-permute-start = (bf16[128,1024]{1,0:T(8,128)(2,1)S(1)}, bf16[128,1024]{1,0:T(8,128)(2,1)S(1)}, u32[]{:S(2)}, u32[]{:S(2)}) collective-permute-start(bf16[128,1024]{1,0:T(8,128)(2,1)S(1)} %convolution_convert_fusion.1), channel_id=1, source_target_pairs={{0,4},{1,5},{2,6},{3,7},{8,12},{9,13},{10,14},{11,15},{16,20},{17,... | collective-permute-start | bytes 786440 | tf_op jit(solution)/shard_map/ppermute | solution.py:18
  99.4 18.1 %collective-permute-start.1 = (bf16[128,1024]{1,0:T(8,128)(2,1)S(1)}, bf16[128,1024]{1,0:T(8,128)(2,1)S(1)}, u32[]{:S(2)}, u32[]{:S(2)}) collective-permute-start(bf16[128,1024]{1,0:T(8,128)(2,1)S(1)} %convolution_convert_fusion.1), channel_id=1, source_target_pairs={{0,3},{1,4},{2,5},{3,6},{4,7},{8,11},{9,12},{10,13},{11,14},{12,15... | collective-permute-start | bytes 786440 | tf_op jit(solution)/shard_map/ppermute | solution.py:18
  103.1 14.6 %collective-permute-start.2 = (bf16[128,1024]{1,0:T(8,128)(2,1)S(1)}, bf16[128,1024]{1,0:T(8,128)(2,1)S(1)}, u32[]{:S(2)}, u32[]{:S(2)}) collective-permute-start(bf16[128,1024]{1,0:T(8,128)(2,1)S(1)} %convolution_convert_fusion.1), channel_id=1, source_target_pairs={{0,2},{1,3},{2,4},{3,5},{4,6},{5,7},{8,10},{9,11},{10,12},{11,13},... | collective-permute-start | bytes 786440 | tf_op jit(solution)/shard_map/ppermute | solution.py:18
  105.4 12.5 %collective-permute-start.3 = (bf16[128,1024]{1,0:T(8,128)(2,1)S(1)}, bf16[128,1024]{1,0:T(8,128)(2,1)S(1)}, u32[]{:S(2)}, u32[]{:S(2)}) collective-permute-start(bf16[128,1024]{1,0:T(8,128)(2,1)S(1)} %convolution_convert_fusion.1), channel_id=1, source_target_pairs={{0,1},{1,2},{2,3},{3,4},{4,5},{5,6},{6,7},{8,9},{9,10},{10,11},{11... | collective-permute-start | bytes 786440 | tf_op jit(solution)/shard_map/ppermute | solution.py:18
  117.3 15.0 %copy-start.8 = (bf16[128,1024]{1,0:T(8,128)(2,1)}, bf16[128,1024]{1,0:T(8,128)(2,1)S(1)}, u32[]{:S(2)}) copy-start(bf16[128,1024]{1,0:T(8,128)(2,1)S(1)} %collective-permute-done) | copy-start | bytes 786436
  117.5 14.2 %copy-start.5 = (bf16[128,1024]{1,0:T(8,128)(2,1)}, bf16[128,1024]{1,0:T(8,128)(2,1)S(1)}, u32[]{:S(2)}) copy-start(bf16[128,1024]{1,0:T(8,128)(2,1)S(1)} %collective-permute-done.1) | copy-start | bytes 786436
  117.7 17.0 %copy-start.6 = (bf16[128,1024]{1,0:T(8,128)(2,1)}, bf16[128,1024]{1,0:T(8,128)(2,1)S(1)}, u32[]{:S(2)}) copy-start(bf16[128,1024]{1,0:T(8,128)(2,1)S(1)} %collective-permute-done.2) | copy-start | bytes 786436
  117.9 17.0 %copy-start.7 = (bf16[128,1024]{1,0:T(8,128)(2,1)}, bf16[128,1024]{1,0:T(8,128)(2,1)S(1)}, u32[]{:S(2)}) copy-start(bf16[128,1024]{1,0:T(8,128)(2,1)S(1)} %collective-permute-done.3) | copy-start | bytes 786436
  137.1 9.4 %copy-start.1 = (bf16[4,128,640]{1,2,0:T(8,128)(2,1)}, bf16[4,128,640]{1,2,0:T(8,128)(2,1)S(1)}, u32[]{:S(2)}) copy-start(bf16[4,128,640]{1,2,0:T(8,128)(2,1)S(1)} %multiply_convert_fusion) | copy-start | bytes 1966084
  138.2 11.1 %collective-permute-start.4 = (bf16[128,1024]{0,1:T(8,128)(2,1)S(1)}, bf16[128,1024]{0,1:T(8,128)(2,1)S(1)}, u32[]{:S(2)}, u32[]{:S(2)}) collective-permute-start(bf16[128,1024]{0,1:T(8,128)(2,1)S(1)} %fusion.147), channel_id=1, source_target_pairs={{1,0},{2,1},{3,2},{4,3},{5,4},{6,5},{7,6},{9,8},{10,9},{11,10},{12... | collective-permute-start | bytes 786440 | tf_op jit(solution)/shard_map/ppermute | solution.py:18
  141.9 12.7 %collective-permute-start.5 = (bf16[128,1024]{0,1:T(8,128)(2,1)S(1)}, bf16[128,1024]{0,1:T(8,128)(2,1)S(1)}, u32[]{:S(2)}, u32[]{:S(2)}) collective-permute-start(bf16[128,1024]{0,1:T(8,128)(2,1)S(1)} %fusion.163), channel_id=1, source_target_pairs={{2,0},{3,1},{4,2},{5,3},{6,4},{7,5},{10,8},{11,9},{12,10},{13,11},... | collective-permute-start | bytes 786440 | tf_op jit(solution)/shard_map/ppermute | solution.py:18
  144.8 12.1 %collective-permute-start.6 = (bf16[128,1024]{0,1:T(8,128)(2,1)S(1)}, bf16[128,1024]{0,1:T(8,128)(2,1)S(1)}, u32[]{:S(2)}, u32[]{:S(2)}) collective-permute-start(bf16[128,1024]{0,1:T(8,128)(2,1)S(1)} %fusion.179), channel_id=1, source_target_pairs={{3,0},{4,1},{5,2},{6,3},{7,4},{11,8},{12,9},{13,10},{14,11},{15,12... | collective-permute-start | bytes 786440 | tf_op jit(solution)/shard_map/ppermute | solution.py:18
  147.6 14.9 %collective-permute-start.7 = (bf16[128,1024]{0,1:T(8,128)(2,1)S(1)}, bf16[128,1024]{0,1:T(8,128)(2,1)S(1)}, u32[]{:S(2)}, u32[]{:S(2)}) collective-permute-start(bf16[128,1024]{0,1:T(8,128)(2,1)S(1)} %fusion.195), channel_id=1, source_target_pairs={{4,0},{5,1},{6,2},{7,3},{12,8},{13,9},{14,10},{15,11},{20,16},{21,... | collective-permute-start | bytes 786440 | tf_op jit(solution)/shard_map/ppermute | solution.py:18
  165.8 0.9 copy-start.4
  165.9 139.1 %all-reduce.2.cloned.1.call-start = ((), (), s32[]{:S(2)}) async-start(), calls=%async_computation.3 | async-start | bytes 2097152 | tf_op jit(solution)/shard_map/psum | solution.py:155
  177.1 3.2 %copy-start.2 = (bf16[4,128,640]{1,2,0:T(8,128)(2,1)S(1)}, bf16[4,128,640]{1,2,0:T(8,128)(2,1)}, u32[]{:S(2)}) copy-start(bf16[4,128,640]{1,2,0:T(8,128)(2,1)} %copy-done.1) | copy-start | bytes 1966084
  181.5 3.4 %copy-start.9 = (bf16[128,4,128]{2,0,1:T(8,128)(2,1)S(1)}, bf16[128,4,128]{2,0,1:T(8,128)(2,1)}, u32[]{:S(2)}) copy-start(bf16[128,4,128]{2,0,1:T(8,128)(2,1)} %get-tuple-element.79) | copy-start | bytes 393220
  182.5 2.5 copy-start.10
  183.5 1.6 copy-start.11
  183.5 1.7 copy-start.14
Sparse Core Ops, SparseCore 0:
  9.6 83.4 all-gather.1
  166.0 78.5 reduce-scatter.1
  247.7 57.2 all-reduce.1
where the time goes:
time: 316 us; the launch traced here: 314 us
  waiting for transfers between devices  222 us (70%)
  matrix products  50 us (16%)
  starting transfers between devices  15.3 us (5%)
  between operations  15 us (5%)
  local copies, waits for them, and re-layouts  6.13 us (2%)
  other arithmetic  6.02 us (2%)
    all_gather x1, waiting for transfers between devices, local(): full_weight = lax.all_gather(kv_weight, 'fsdp', axis=0, tiled=True)  84 us
    reduce_scatter x1, waiting for transfers between devices, local(): lax.psum_scatter(lax.dot_general(tokens, grad_kv, (((0,), (0,)), ((), ())...  58.5 us
    psum x1, waiting for transfers between devices, local(): grad_weight = lax.psum(shard_sum, 'bal').astype(jnp.float32)  55.1 us
    ppermute x8, waiting for transfers between devices, from_behind(): lax.ppermute(value, axis, [(source, source + steps) for source in range(i...  23.4 us
    dot_general x20, matrix products, query_tile(): jnp.einsum('hqk,kd->qhd', dscore_tile, key_block, preferred_element_type=...  16.5 us
    ppermute x8, starting transfers between devices, from_behind(): lax.ppermute(value, axis, [(source, source + steps) for source in range(i...  15.2 us
    dot_general x20, matrix products, value_tile(): jnp.einsum('hqk,kd->qhd', prob_tile, value_block, preferred_element_type=...  7.82 us
  transfers between devices with their start and end apart: 11, of which 7 were waited for; matrix products, arithmetic and copies ran while one was open for 10% of the time, Pallas kernels for 0%

commit v1 on v0

--- a/solution.py
+++ b/solution.py
@@ -1,6 +1,10 @@
+import functools
+
 import jax
 import jax.numpy as jnp
 from jax import lax
+from jax.experimental import pallas as pl
+from jax.experimental.pallas import tpu as pltpu
 from jax.sharding import PartitionSpec as P
 
 HEADS = 16
@@ -8,8 +12,294 @@
 HEAD_DIM = 128
 REACH = 4
 
-
 NEG_FILL = -1e30
+F32 = jnp.float32
+BF16 = jnp.bfloat16
+VM = pl.BlockSpec(memory_space=pltpu.VMEM)
+SM = pl.BlockSpec(memory_space=pltpu.SMEM)
+
+
+def swap(value, axis, bit):
+    count = lax.axis_size(axis)
+    return lax.ppermute(value, axis, [(i, i ^ bit) for i in range(count)])
+
+
+def dot(a, b, ca, cb):
+    return lax.dot_general(a, b, (((ca,), (cb,)), ((), ())), preferred_element_type=F32)
+
+
+def project_kernel(x0, x1, x2, x3, w_own, w_oth, keep, send):
+    for r, x in enumerate((x0, x1, x2, x3)):
+        keep[r] = dot(x[...], w_own[...], 1, 0).astype(BF16)
+        send[r] = dot(x[...], w_oth[...], 1, 0).astype(BF16)
+
+
+def project(xs, w_own, w_oth):
+    rows = xs[0].shape[0]
+    out = jax.ShapeDtypeStruct((4, rows, HEAD_DIM), BF16)
+    return pl.pallas_call(
+        project_kernel, out_shape=(out, out), in_specs=[VM] * 6, out_specs=(VM, VM)
+    )(*xs, w_own, w_oth)
+
+
+def window_kernel(ids, keep, recv, o0, o1, o2, o3):
+    m = ids[0]
+    rows = keep.shape[1]
+    for r, out in enumerate((o0, o1, o2, o3)):
+        target = jnp.bitwise_xor(m, r)
+        for w in range(3):
+            chip = target + (w - 2)
+            ok = chip >= 0
+            rel = jnp.bitwise_xor(jnp.maximum(chip, 0), m)
+            zero = jnp.zeros((rows, HEAD_DIM), BF16)
+            out[2 * w * rows : (2 * w + 1) * rows, :] = jnp.where(ok, keep[rel], zero)
+            out[(2 * w + 1) * rows : (2 * w + 2) * rows, :] = jnp.where(ok, recv[rel], zero)
+
+
+def windows(ids, keep, recv):
+    rows = keep.shape[1]
+    out = jax.ShapeDtypeStruct((6 * rows, HEAD_DIM), BF16)
+    return pl.pallas_call(
+        window_kernel, out_shape=(out,) * 4, in_specs=[SM, VM, VM], out_specs=(VM,) * 4
+    )(ids, keep, recv)
+
+
+def attend_kernel(docs, ids, first, second, q_own, q_oth, g_own, g_oth, lens,
+                  out_own, out_oth, dq_own, dq_oth, d_first, d_second, bias):
+    m, c = ids[0], ids[1]
+    rows = q_own.shape[0]
+    keys = first.shape[0]
+    inv = HEAD_DIM ** (-0.5)
+
+    def place(index, chip0, shape, dim):
+        t = lax.broadcasted_iota(jnp.int32, shape, dim)
+        chip = t // (2 * rows) + chip0
+        within = t % (2 * rows)
+        mine = within < rows
+        shard = 2 * chip + jnp.where(mine, c, 1 - c)
+        return shard * rows + jnp.where(mine, within, within - rows)
+
+    kpos = place(0, m - 2, (keys, 1), 0)
+    qpos = place(0, m, (1, 2 * rows), 1)
+    kdoc = jnp.where(kpos >= 0, 0, -1)
+    qdoc = jnp.zeros_like(qpos)
+    end = jnp.int32(0)
+    for k in range(docs):
+        end = end + lens[0, k]
+        kdoc = kdoc + (kpos >= end).astype(jnp.int32)
+        qdoc = qdoc + (qpos >= end).astype(jnp.int32)
+    bias[...] = jnp.where((kdoc == qdoc) & (kpos <= qpos), 0.0, NEG_FILL)
+
+    is_key = m < 2
+    key = jnp.where(is_key, first[...], second[...])
+    val = jnp.where(is_key, second[...], first[...])
+    key_t = key.T
+    val_t = val.T
+    dk = jnp.zeros((keys, HEAD_DIM), F32)
+    dv = jnp.zeros((keys, HEAD_DIM), F32)
+    for h in range(HEADS // KV_HEADS):
+        cols = slice(h * HEAD_DIM, (h + 1) * HEAD_DIM)
+        q = jnp.concatenate([q_own[:, cols], q_oth[:, cols]], axis=0)
+        g = jnp.concatenate([g_own[:, cols], g_oth[:, cols]], axis=0)
+        s = dot(key, q, 1, 1) * inv + bias[...]
+        p = jnp.exp(s - jnp.max(s, axis=0, keepdims=True))
+        p = p * (1.0 / jnp.sum(p, axis=0, keepdims=True))
+        low = p.astype(BF16)
+        out_t = dot(val_t, low, 1, 0).astype(BF16).astype(F32)
+        delta = jnp.sum(out_t * g.astype(F32).T, axis=0, keepdims=True)
+        dp = dot(val, g, 1, 1)
+        ds = (p * (dp - delta)).astype(BF16)
+        dq_t = dot(key_t, ds, 1, 0) * inv
+        dk = dk + dot(ds, q, 1, 0)
+        dv = dv + dot(low, g, 1, 0)
+        out = out_t.T.astype(BF16)
+        dq = dq_t.T.astype(BF16)
+        out_own[:, cols] = out[:rows]
+        out_oth[:, cols] = out[rows:]
+        dq_own[:, cols] = dq[:rows]
+        dq_oth[:, cols] = dq[rows:]
+    dk = (dk * inv).astype(BF16)
+    dv = dv.astype(BF16)
+    d_first[...] = jnp.where(is_key, dk, dv)
+    d_second[...] = jnp.where(is_key, dv, dk)
+
+
+def attend(first, second, q_own, q_oth, g_own, g_oth, lens, ids):
+    rows, width = q_own.shape
+    keys = first.shape[0]
+    part = jax.ShapeDtypeStruct((rows, width), BF16)
+    grad = jax.ShapeDtypeStruct((keys, HEAD_DIM), BF16)
+    docs = lens.shape[1]
+    return pl.pallas_call(
+        functools.partial(attend_kernel, docs),
+        out_shape=(part, part, part, part, grad, grad),
+        in_specs=[SM] + [VM] * 6 + [SM],
+        out_specs=(VM,) * 6,
+        scratch_shapes=[pltpu.VMEM((keys, 2 * rows), F32)],
+    )(ids, first, second, q_own, q_oth, g_own, g_oth, lens)
+
+
+def gather_kernel(ids, d0, d1, d2, d3, own, oth, acc):
+    m = ids[0]
+    rows = own.shape[1]
+    acc[...] = jnp.zeros_like(acc)
+    for r, d in enumerate((d0, d1, d2, d3)):
+        start = pl.multiple_of(jnp.bitwise_xor(m, r) * (2 * rows), 2 * rows)
+        span = pl.ds(start, 6 * rows)
+        acc[span, :] = acc[span, :] + d[...].astype(F32)
+    for r in range(4):
+        start = pl.multiple_of((jnp.bitwise_xor(m, r) + 2) * (2 * rows), 2 * rows)
+        own[r] = acc[pl.ds(start, rows), :].astype(BF16)
+        oth[r] = acc[pl.ds(start + rows, rows), :].astype(BF16)
+
+
+def gather_grads(ids, ds):
+    rows = ds[0].shape[0] // 6
+    out = jax.ShapeDtypeStruct((4, rows, HEAD_DIM), BF16)
+    return pl.pallas_call(
+        gather_kernel,
+        out_shape=(out, out),
+        in_specs=[SM] + [VM] * 4,
+        out_specs=(VM, VM),
+        scratch_shapes=[pltpu.VMEM((12 * rows, HEAD_DIM), F32)],
+    )(ids, *ds)
+
+
+def weight_kernel(x0, x1, x2, x3, g_own, g_oth, own, oth):
+    for g, out in ((g_own, own), (g_oth, oth)):
+        total = None
+        for r, x in enumerate((x0, x1, x2, x3)):
+            term = dot(g[r].T, x[...], 1, 0)
+            total = term if total is None else total + term
+        out[...] = total.T.astype(out.dtype)
+
+
+def weight_grads(xs, g_own, g_oth):
+    width = xs[0].shape[1]
+    return pl.pallas_call(
+        weight_kernel,
+        out_shape=(
+            jax.ShapeDtypeStruct((width, HEAD_DIM), F32),
+            jax.ShapeDtypeStruct((width, HEAD_DIM), BF16),
+        ),
+        in_specs=[VM] * 6,
+        out_specs=(VM, VM),
+    )(*xs, g_own, g_oth)
+
+
+def token_kernel(g_own, g_oth, w_own, w_oth, *outs):
+    half = w_own.shape[0] // 2
+    for r in range(4):
+        g = jnp.concatenate([g_own[r], g_oth[r]], axis=1)
+        for part in range(2):
+            rows = slice(part * half, (part + 1) * half)
+            w = jnp.concatenate([w_own[rows, :], w_oth[rows, :]], axis=1)
+            outs[2 * r + part][...] = dot(g, w, 1, 1).astype(BF16)
+
+
+def token_grads(g_own, g_oth, w_own, w_oth):
+    rows, half = g_own.shape[1], w_own.shape[0] // 2
+    return pl.pallas_call(
+        token_kernel,
+        out_shape=(jax.ShapeDtypeStruct((rows, half), BF16),) * 8,
+        in_specs=[VM] * 4,
+        out_specs=(VM,) * 8,
+    )(g_own, g_oth, w_own, w_oth)
+
+
+def assemble_kernel(ids, *refs):
+    m, c = ids[0], ids[1]
+    out = refs[-1]
+    for side in range(2):
+        core = c if side == 0 else 1 - c
+        for r in range(4):
+            q = jnp.bitwise_xor(m, r)
+            col = (q // 2) * (KV_HEADS * HEAD_DIM) + (2 * core + q % 2) * HEAD_DIM
+            col = pl.multiple_of(col, HEAD_DIM)
+            out[:, pl.ds(col, HEAD_DIM)] = refs[4 * side + r][...].astype(F32)
+
+
+def assemble(ids, blocks):
+    rows = blocks[0].shape[0]
+    return pl.pallas_call(
+        assemble_kernel,
+        out_shape=jax.ShapeDtypeStruct((rows, 2 * KV_HEADS * HEAD_DIM), F32),
+        in_specs=[SM] + [VM] * 8,
+        out_specs=VM,
+    )(ids, *blocks)
+
+
+def plane_local(tokens, kv_weight, queries, out_grad, doc_lengths):
+    half = queries.shape[1] // 2
+    rows = tokens.shape[0]
+    b = lax.axis_index("bal")
+    z = lax.axis_index("fsdp")
+    m, c = b // 2, b % 2
+    ids = jnp.stack([m, c]).astype(jnp.int32)
+    pair = lambda v: swap(v, "bal", 1)
+    near = lambda v: swap(v, "bal", 2)
+    far = lambda v: swap(v, "bal", 4)
+    cross = lambda v: swap(v, "bal", 6)
+
+    col = (m // 2) * (KV_HEADS * HEAD_DIM) + (2 * c + m % 2) * HEAD_DIM
+    w0 = lax.dynamic_slice(kv_weight, (0, col), (kv_weight.shape[0], HEAD_DIM))
+    w2 = swap(w0, "fsdp", 2)
+    w13 = swap(jnp.stack([w0, w2]), "fsdp", 1)
+    blocks = jnp.stack([w0, w13[0], w2, w13[1]])
+    w_own = jnp.take(blocks, jnp.arange(4) ^ z, axis=0).reshape(-1, HEAD_DIM)
+    w_oth = pair(w_own)
+
+    xs = [tokens, near(tokens), far(tokens), cross(tokens)]
+
+    q_own = lax.dynamic_slice(queries, (0, c * half), (rows, half))
+    g_own = lax.dynamic_slice(out_grad, (0, c * half), (rows, half))
+    q_oth = pair(lax.dynamic_slice(queries, (0, (1 - c) * half), (rows, half)))
+    g_oth = pair(lax.dynamic_slice(out_grad, (0, (1 - c) * half), (rows, half)))
+
+    keep, send = project(xs, w_own, w_oth)
+    win = windows(ids, keep, pair(send))
+    win_x, win_y, win_d = near(win[1]), far(win[2]), cross(win[3])
+
+    width = half // 2
+    ga, gb = m % 2, 1 - m % 2
+    cut = lambda v, g: lax.dynamic_slice(v, (0, g * width), (rows, width))
+    oa = attend(win[0], win_y, *[cut(v, ga) for v in (q_own, q_oth, g_own, g_oth)], doc_lengths, ids)
+    ob = attend(win_x, win_d, *[cut(v, gb) for v in (q_own, q_oth, g_own, g_oth)], doc_lengths, ids)
+
+    grads = [oa[4], near(ob[4]), far(oa[5]), cross(ob[5])]
+    g_keep, g_send = gather_grads(ids, grads)
+    g_recv = pair(g_send)
+
+    w_mine, w_send = weight_grads(xs, g_keep, g_recv)
+    total = w_mine + pair(w_send).astype(F32)
+    total = total.reshape(4, -1, HEAD_DIM)
+    rel = jnp.take(total, jnp.arange(4) ^ z, axis=0)
+    got = swap(rel[1::2].astype(BF16), "fsdp", 1).astype(F32)
+    a0, a2 = rel[0] + got[0], rel[2] + got[1]
+    block = (a0 + swap(a2.astype(BF16), "fsdp", 2).astype(F32)).astype(BF16)
+    mine = [block, near(block), far(block), cross(block)]
+    theirs = [pair(v) for v in mine]
+    grad_weight = assemble(ids, mine + theirs)
+
+    t = token_grads(g_keep, g_recv, w_own, w_oth)
+    t = [v.astype(F32) for v in t]
+    send_a = near(jnp.concatenate([t[2], t[6]], axis=0).astype(BF16)).astype(F32)
+    send_b = far(jnp.concatenate([t[5], t[7]], axis=0).astype(BF16)).astype(F32)
+    a0, a2 = t[0] + send_a[:rows], t[4] + send_a[rows:]
+    b0, b1 = t[1] + send_b[:rows], t[3] + send_b[rows:]
+    a0 = a0 + far(a2.astype(BF16)).astype(F32)
+    b0 = b0 + near(b1.astype(BF16)).astype(F32)
+    grad_tokens = jnp.concatenate([a0, b0], axis=1).astype(BF16)
+
+    def place(own_a, own_b, oth_a, oth_b):
+        order = lambda a, b_: jnp.where(ga == 0, jnp.concatenate([a, b_], 1), jnp.concatenate([b_, a], 1))
+        own = order(own_a, own_b)
+        got = pair(order(oth_a, oth_b))
+        return jnp.where(c == 0, jnp.concatenate([own, got], 1), jnp.concatenate([got, own], 1))
+
+    attn_out = place(oa[0], ob[0], oa[1], ob[1])
+    grad_queries = place(oa[2], ob[2], oa[3], ob[3])
+    return attn_out, grad_queries, grad_tokens, grad_weight
 
 
 def from_behind(value, axis, steps):
@@ -52,7 +342,7 @@
     return jnp.einsum("hqk,qhd->kd", prob_tile, grad_group, preferred_element_type=jnp.float32)
 
 
-def attend(q_rows, kv_blocks, grad_rows, allowed_parts):
+def attend_rows(q_rows, kv_blocks, grad_rows, allowed_parts):
     row_count = q_rows.shape[0]
     key_rows = kv_blocks[0].shape[0]
     group_size = HEADS // KV_HEADS
@@ -133,7 +423,7 @@
     for distance in range(1, REACH + 1):
         earlier.append(from_behind(kv_rows, "bal", distance))
     kv_blocks = earlier[::-1]
-    attn_out, grad_queries, window_terms = attend(queries, kv_blocks, out_grad, allowed_parts)
+    attn_out, grad_queries, window_terms = attend_rows(queries, kv_blocks, out_grad, allowed_parts)
     grad_terms = window_terms[::-1]
     grad_sum = grad_terms[0]
     for distance in range(1, REACH + 1):
@@ -164,8 +454,9 @@
         P(("fsdp", "bal"), None),
         P("fsdp", None),
     )
+    one_plane = mesh.shape["bal"] == 8 and mesh.shape["fsdp"] == 4
     return jax.shard_map(
-        local,
+        plane_local if one_plane else local,
         mesh=mesh,
         in_specs=placed,
         out_specs=(

time: 316 us -> 133 us (0.42)
  waiting for transfers between devices: 222 us -> 37 us
  matrix products: 50 us -> 0 us
  Pallas kernels: 0 us -> 33.1 us
  starting transfers between devices: 15.3 us -> 29.8 us
  between operations: 15 us -> 1.03 us
  local copies, waits for them, and re-layouts: 6.13 us -> 16.1 us
  other arithmetic: 6.02 us -> 15 us
    all_gather x1 -> x0, waiting for transfers between devices: 84 us -> none  [local(): full_weight = lax.all_gather(kv_weight, 'fsdp', axis=0, tiled=True)]
    reduce_scatter x1 -> x0, waiting for transfers between devices: 58.5 us -> none  [local(): lax.psum_scatter(lax.dot_general(tokens, grad_kv, (((0,), (0,)), ((), ())...]
    psum x1 -> x0, waiting for transfers between devices: 55.1 us -> none  [local(): grad_weight = lax.psum(shard_sum, 'bal').astype(jnp.float32)]
    dot_general x123 -> x0, matrix products: 50 us -> none  [the longest x20 16.5 us: query_tile(): jnp.einsum('hqk,kd->qhd', dscore_tile, key_block, preferred_element_type=...]
    pallas_call x0 -> x8, Pallas kernels: none -> 33.1 us  [the longest x2 14.9 us: attend(): pl.pallas_call(functools.partial(attend_kernel, docs), out_shape=(part, p...]
    ppermute x8 -> x32, starting transfers between devices: 15.2 us -> 29.8 us  [swap(): return lax.ppermute(value, axis, [(i, i ^ bit) for i in range(count)])]
    ppermute x8 -> x32, waiting for transfers between devices: 23.4 us -> 37 us  [swap(): return lax.ppermute(value, axis, [(i, i ^ bit) for i in range(count)])]
    dynamic_slice x0 -> x6, local copies, waits for them, and re-layouts: none -> 8.36 us  [the longest x3 5.58 us: plane_local(): cut = lambda v, g: lax.dynamic_slice(v, (0, g * width), (rows, width))]
  transfers between devices with their start and end apart: 11 -> 32, of which waited for: 7 -> 16; matrix products, arithmetic and copies ran while one was open for 10% -> 19% of each run, Pallas kernels for 0% -> 23%
where the time goes in v1:
time: 133 us; the launch traced here: 132 us
  waiting for transfers between devices  37 us (28%)
  Pallas kernels  33.1 us (25%)
  starting transfers between devices  29.8 us (22%)
  local copies, waits for them, and re-layouts  16.1 us (12%)
  other arithmetic  15 us (11%)
    ppermute x32, waiting for transfers between devices, swap(): return lax.ppermute(value, axis, [(i, i ^ bit) for i in range(count)])  37 us
    ppermute x32, starting transfers between devices, swap(): return lax.ppermute(value, axis, [(i, i ^ bit) for i in range(count)])  29.8 us
    pallas_call x2, Pallas kernels, attend(): pl.pallas_call(functools.partial(attend_kernel, docs), out_shape=(part, p...  14.9 us
    unnamed x62, local copies, waits for them, and re-layouts  6.43 us
    dynamic_slice x3, local copies, waits for them, and re-layouts, plane_local(): cut = lambda v, g: lax.dynamic_slice(v, (0, g * width), (rows, width))  5.58 us
    pallas_call x1, Pallas kernels, weight_grads(): pl.pallas_call(weight_kernel, out_shape=(jax.ShapeDtypeStruct((width, HEA...  3.86 us
    pallas_call x1, Pallas kernels, project(): pl.pallas_call(project_kernel, out_shape=(out, out), in_specs=[VM] * 6, o...  3.73 us
    pallas_call x1, Pallas kernels, token_grads(): pl.pallas_call(token_kernel, out_shape=(jax.ShapeDtypeStruct((rows, half)...  3.54 us
  transfers between devices with their start and end apart: 32, of which 16 were waited for; matrix products, arithmetic and copies ran while one was open for 19% of the time, Pallas kernels for 23%

profile of v1, /device:TPU:0, one launch (start us, length us, event | category | flops | bytes accessed | tf_op | source)
XLA Modules:
  0.0 132.1 jit_solution(7412491252296053776)
XLA Ops:
  0.6 4.0 %collective-permute-start.2 = (bf16[128,2048]{1,0:T(8,128)(2,1)}, bf16[128,2048]{1,0:T(8,128)(2,1)S(1)}, u32[]{:S(2)}, u32[]{:S(2)}) collective-permute-start(bf16[128,2048]{1,0:T(8,128)(2,1)} %x0.3), channel_id=1, source_target_pairs={{0,6},{1,7},{2,4},{3,5},{4,2},{5,3},{6,0},{7,1},{8,14},{9,15},{10,... | collective-permute-start | bytes 1572872 | tf_op jit(solution)/shard_map/ppermute | solution.py:24
  5.3 3.1 %collective-permute-start.3 = (bf16[512,128]{1,0:T(8,128)(2,1)S(1)}, bf16[512,128]{1,0:T(8,128)(2,1)S(1)}, u32[]{:S(2)}, u32[]{:S(2)}) collective-permute-start(bf16[512,128]{1,0:T(8,128)(2,1)S(1)} %constant_dynamic-slice_fusion.10), channel_id=1, source_target_pairs={{0,16},{8,24},{16,0},{24,8},{1,17},{9,25},{17,1},{25,9},{2,18},{10... | collective-permute-start | bytes 393224 | tf_op jit(solution)/shard_map/ppermute | solution.py:24
  8.4 5.4 %collective-permute-done.3 = bf16[512,128]{1,0:T(8,128)(2,1)S(1)} collective-permute-done((bf16[512,128]{1,0:T(8,128)(2,1)S(1)}, bf16[512,128]{1,0:T(8,128)(2,1)S(1)}, u32[]{:S(2)}, u32[]{:S(2)}) %collective-permute-start.3) | collective-permute-done | bytes 131104 | tf_op jit(solution)/shard_map/ppermute | solution.py:24
  14.8 5.8 %collective-permute-done.4 = bf16[2,512,128]{2,1,0:T(8,128)(2,1)S(1)} collective-permute-done((bf16[2,512,128]{2,1,0:T(8,128)(2,1)S(1)}, bf16[2,512,128]{2,1,0:T(8,128)(2,1)S(1)}, u32[]{:S(2)}, u32[]{:S(2)}) %collective-permute-start.4) | collective-permute-done | bytes 262176 | tf_op jit(solution)/shard_map/ppermute | solution.py:24
  21.8 1.8 %constant_dynamic-slice_fusion.5 = bf16[128,1024]{1,0:T(8,128)(2,1)} fusion(bf16[128,2048]{1,0:T(8,128)(2,1)} %param.8, s32[]{:T(128)S(6)} %select_n.124), kind=kLoop, calls=%fused_computation.42 | loop fusion | bytes 524292 | tf_op jit(solution)/shard_map/dynamic_slice | solution.py:257
  25.1 2.9 %collective-permute-done.1.x2 = bf16[128,2048]{1,0:T(8,128)(2,1)S(1)} collective-permute-done((bf16[128,2048]{1,0:T(8,128)(2,1)}, bf16[128,2048]{1,0:T(8,128)(2,1)S(1)}, u32[]{:S(2)}, u32[]{:S(2)}) %collective-permute-start.1) | collective-permute-done | bytes 524320 | tf_op jit(solution)/shard_map/ppermute | solution.py:24
  29.6 3.7 %shard_map.84 = (bf16[4,128,128]{2,1,0:T(8,128)(2,1)}, bf16[4,128,128]{2,1,0:T(8,128)(2,1)}) custom-call(bf16[128,2048]{1,0:T(8,128)(2,1)} %x0.3, bf16[128,2048]{1,0:T(8,128)(2,1)} %collective-permute-done.x1, bf16[128,2048]{1,0:T(8,128)(2,1)} %copy-done.4, bf16[128,2048]{1,0:T(8,128)(2,1)} %copy-done.3, bf16[2048,128]{1,0:T(8,128)(2,1)} %copy-done.1, ...), custom_call_target="tpu_custom_call" | custom-call | tf_op jit(solution)/shard_map/pallas_call | solution.py:40
  34.1 2.2 %constant_dynamic-slice_fusion.6 = (bf16[128,512]{1,0:T(8,128)(2,1)}, bf16[128,512]{1,0:T(8,128)(2,1)}, bf16[128,512]{1,0:T(8,128)(2,1)}, bf16[128,512]{1,0:T(8,128)(2,1)}) fusion(bf16[128,2048]{1,0:T(8,128)(2,1)} %param.8, s32[]{:T(128)S(6)} %dynamic_slice.40, s32[]{:T(128)S(6)} %dynamic_slice.47, bf16[128,2048]{1,0:T(8,128)(2,1)} %param.7), kind=kLoop, calls=%fused_computation.43 | loop fusion | bytes 1048584 | tf_op jit(solution)/shard_map/dynamic_slice | solution.py:265
  36.9 2.0 %shard_map.85 = (bf16[768,128]{1,0:T(8,128)(2,1)}, bf16[768,128]{1,0:T(8,128)(2,1)}, bf16[768,128]{1,0:T(8,128)(2,1)}, bf16[768,128]{1,0:T(8,128)(2,1)}) custom-call(s32[2]{0:T(128)} %pad_add_fusion.ids, bf16[4,128,128]{2,1,0:T(8,128)(2,1)} %get-tuple-element.34.keep, bf16[4,128,128]{2,1,0:T(8,128)(2,1)} %copy-done.22), custom_call_target="tpu_custom_call" | custom-call | tf_op jit(solution)/shard_map/pallas_call | solution.py:62
  39.0 1.6 %collective-permute-start.7 = (bf16[768,128]{1,0:T(8,128)(2,1)}, bf16[768,128]{1,0:T(8,128)(2,1)S(1)}, u32[]{:S(2)}, u32[]{:S(2)}) collective-permute-start(bf16[768,128]{1,0:T(8,128)(2,1)} %get-tuple-element.37), channel_id=1, source_target_pairs={{0,4},{1,5},{2,6},{3,7},{4,0},{5,1},{6,2},{7,3},{8,12},{9,13},{10,... | collective-permute-start | bytes 589832 | tf_op jit(solution)/shard_map/ppermute | solution.py:24
  42.5 1.7 %constant_dynamic-slice_fusion.4 = (bf16[128,512]{1,0:T(8,128)(2,1)}, bf16[128,512]{1,0:T(8,128)(2,1)}) fusion(bf16[128,1024]{1,0:T(8,128)(2,1)} %collective-permute-done.9, s32[]{:T(128)S(6)} %select_n.120, s32[]{:T(128)S(6)} %select_n.125), kind=kLoop, calls=%fused_computation.41 | loop fusion | bytes 524296 | tf_op jit(solution)/shard_map/dynamic_slice | solution.py:265
  44.1 1.7 %constant_dynamic-slice_fusion.7 = (bf16[128,512]{1,0:T(8,128)(2,1)}, bf16[128,512]{1,0:T(8,128)(2,1)}) fusion(bf16[128,1024]{1,0:T(8,128)(2,1)} %collective-permute-done.8, s32[]{:T(128)S(6)} %select_n.120, s32[]{:T(128)S(6)} %select_n.125), kind=kLoop, calls=%fused_computation.44 | loop fusion | bytes 524296 | tf_op jit(solution)/shard_map/dynamic_slice | solution.py:265
  47.0 7.3 %shard_map.86 = (bf16[128,512]{1,0:T(8,128)(2,1)}, bf16[128,512]{1,0:T(8,128)(2,1)}, bf16[128,512]{1,0:T(8,128)(2,1)}, bf16[128,512]{1,0:T(8,128)(2,1)}, bf16[76...) custom-call(s32[2]{0:T(128)} %pad_add_fusion.ids, bf16[768,128]{1,0:T(8,128)(2,1)} %get-tuple-element.36.first, ...), custom_call_target="tpu_custom_call" | custom-call | tf_op jit(solution)/shard_map/pallas_call | solution.py:133
  54.4 1.8 %collective-permute-start.15 = (bf16[768,128]{1,0:T(8,128)(2,1)}, bf16[768,128]{1,0:T(8,128)(2,1)S(1)}, u32[]{:S(2)}, u32[]{:S(2)}) collective-permute-start(bf16[768,128]{1,0:T(8,128)(2,1)} %get-tuple-element.50), channel_id=1, source_target_pairs={{0,4},{1,5},{2,6},{3,7},{4,0},{5,1},{6,2},{7,3},{8,12},{9,13},{10,... | collective-permute-start | bytes 589832 | tf_op jit(solution)/shard_map/ppermute | solution.py:24
  56.9 7.6 %shard_map.87 = (bf16[128,512]{1,0:T(8,128)(2,1)}, bf16[128,512]{1,0:T(8,128)(2,1)}, bf16[128,512]{1,0:T(8,128)(2,1)}, bf16[128,512]{1,0:T(8,128)(2,1)}, bf16[76...) custom-call(s32[2]{0:T(128)} %pad_add_fusion.ids, bf16[768,128]{1,0:T(8,128)(2,1)} %copy-done.13, ...), custom_call_target="tpu_custom_call" | custom-call | tf_op jit(solution)/shard_map/pallas_call | solution.py:133
  69.2 3.2 %collective-permute-done.14.d1 = bf16[768,128]{1,0:T(8,128)(2,1)S(1)} collective-permute-done((bf16[768,128]{1,0:T(8,128)(2,1)}, bf16[768,128]{1,0:T(8,128)(2,1)S(1)}, u32[]{:S(2)}, u32[]{:S(2)}) %collective-permute-start.14) | collective-permute-done | bytes 196640 | tf_op jit(solution)/shard_map/ppermute | solution.py:24
  72.5 2.3 %collective-permute-done.16.d3 = bf16[768,128]{1,0:T(8,128)(2,1)S(1)} collective-permute-done((bf16[768,128]{1,0:T(8,128)(2,1)}, bf16[768,128]{1,0:T(8,128)(2,1)S(1)}, u32[]{:S(2)}, u32[]{:S(2)}) %collective-permute-start.16) | collective-permute-done | bytes 196640 | tf_op jit(solution)/shard_map/ppermute | solution.py:24
  75.4 2.2 %shard_map.88 = (bf16[4,128,128]{2,1,0:T(8,128)(2,1)}, bf16[4,128,128]{2,1,0:T(8,128)(2,1)}) custom-call(s32[2]{0:T(128)} %pad_add_fusion.ids, bf16[768,128]{1,0:T(8,128)(2,1)} %get-tuple-element.48.d0, bf16[768,128]{1,0:T(8,128)(2,1)} %copy-done.17, bf16[768,128]{1,0:T(8,128)(2,1)} %copy-done.14, bf16[768,128]{1,0:T(8,128)(2,1)} %copy-done.18), custom_call_target="tpu_custom_call" | custom-call | tf_op jit(solution)/shard_map/pallas_call | solution.py:159
  79.8 3.9 %shard_map.90 = (f32[2048,128]{1,0:T(8,128)}, bf16[2048,128]{1,0:T(8,128)(2,1)}) custom-call(bf16[128,2048]{1,0:T(8,128)(2,1)} %x0.3, bf16[128,2048]{1,0:T(8,128)(2,1)} %collective-permute-done.x1, bf16[128,2048]{1,0:T(8,128)(2,1)} %copy-done.4, bf16[128,2048]{1,0:T(8,128)(2,1)} %copy-done.3, bf16[4,128,128]{2,1,0:T(8,128)(2,1)} %get-tuple-element.52.g_own, ...), custom_call_target="tpu_custom_call" | custom-call | tf_op jit(solution)/shard_map/pallas_call | solution.py:179
  85.7 3.5 %shard_map.89 = (bf16[128,1024]{1,0:T(8,128)(2,1)}, bf16[128,1024]{1,0:T(8,128)(2,1)}, bf16[128,1024]{1,0:T(8,128)(2,1)}, bf16[128,1024]{1,0:T(8,128)(2,1)}, bf1...) custom-call(bf16[4,128,128]{2,1,0:T(8,128)(2,1)} %get-tuple-element.5, ...), custom_call_target="tpu_custom_call" | custom-call | tf_op jit(solution)/shard_map/pallas_call | solution.py:202
  89.2 1.9 %pad_maximum_fusion.2 = bf16[256,1024]{1,0:T(8,128)(2,1)} fusion(bf16[128,1024]{1,0:T(8,128)(2,1)} %get-tuple-element.60, bf16[128,1024]{1,0:T(8,128)(2,1)} %get-tuple-element.59), kind=kLoop, calls=%fused_computation.17 | loop fusion | flops 1048576 | bytes 1048576 | tf_op jit(solution)/shard_map/concatenate | solution.py:287
  91.1 1.7 %collective-permute-start.20 = (bf16[256,1024]{1,0:T(8,128)(2,1)}, bf16[256,1024]{1,0:T(8,128)(2,1)}, u32[]{:S(2)}, u32[]{:S(2)}) collective-permute-start(bf16[256,1024]{1,0:T(8,128)(2,1)} %pad_maximum_fusion.2), channel_id=1, source_target_pairs={{0,4},{1,5},{2,6},{3,7},{4,0},{5,1},{6,2},{7,3},{8,12},{9,13},{10,... | collective-permute-start | bytes 1572872 | tf_op jit(solution)/shard_map/ppermute | solution.py:24
  92.8 1.9 %pad_maximum_fusion.1 = bf16[256,1024]{1,0:T(8,128)(2,1)} fusion(bf16[128,1024]{1,0:T(8,128)(2,1)} %get-tuple-element.56, bf16[128,1024]{1,0:T(8,128)(2,1)} %get-tuple-element.55), kind=kLoop, calls=%fused_computation.16 | loop fusion | flops 1048576 | bytes 1048576 | tf_op jit(solution)/shard_map/concatenate | solution.py:286
  98.2 1.8 %collective-permute-start.23 = (bf16[2,512,128]{2,1,0:T(8,128)(2,1)S(1)}, bf16[2,512,128]{2,1,0:T(8,128)(2,1)S(1)}, u32[]{:S(2)}, u32[]{:S(2)}) collective-permute-start(bf16[2,512,128]{2,1,0:T(8,128)(2,1)S(1)} %slice.41), channel_id=1, source_target_pairs={{0,8},{8,0},{16,24},{24,16},{1,9},{9,1},{17,25},{25,17},{2,10},{10... | collective-permute-start | bytes 786440 | tf_op jit(solution)/shard_map/ppermute | solution.py:24
  100.0 5.6 %collective-permute-done.20 = bf16[256,1024]{1,0:T(8,128)(2,1)} collective-permute-done((bf16[256,1024]{1,0:T(8,128)(2,1)}, bf16[256,1024]{1,0:T(8,128)(2,1)}, u32[]{:S(2)}, u32[]{:S(2)}) %collective-permute-start.20) | collective-permute-done | bytes 524320 | tf_op jit(solution)/shard_map/ppermute | solution.py:24
  106.8 1.7 %collective-permute-start.21 = (bf16[128,1024]{1,0:T(8,128)(2,1)S(1)}, bf16[128,1024]{1,0:T(8,128)(2,1)S(1)}, u32[]{:S(2)}, u32[]{:S(2)}) collective-permute-start(bf16[128,1024]{1,0:T(8,128)(2,1)S(1)} %fusion), channel_id=1, source_target_pairs={{0,2},{1,3},{2,0},{3,1},{4,6},{5,7},{6,4},{7,5},{8,10},{9,11},{10,... | collective-permute-start | bytes 786440 | tf_op jit(solution)/shard_map/ppermute | solution.py:24
  110.7 2.8 %collective-permute-start.24 = (bf16[512,128]{1,0:T(8,128)(2,1)S(1)}, bf16[512,128]{1,0:T(8,128)(2,1)S(1)}, u32[]{:S(2)}, u32[]{:S(2)}) collective-permute-start(bf16[512,128]{1,0:T(8,128)(2,1)S(1)} %fusion.10), channel_id=1, source_target_pairs={{0,16},{8,24},{16,0},{24,8},{1,17},{9,25},{17,1},{25,9},{2,18},{10... | collective-permute-start | bytes 393224 | tf_op jit(solution)/shard_map/ppermute | solution.py:24
  114.7 4.2 %collective-permute-done.24 = bf16[512,128]{1,0:T(8,128)(2,1)S(1)} collective-permute-done((bf16[512,128]{1,0:T(8,128)(2,1)S(1)}, bf16[512,128]{1,0:T(8,128)(2,1)S(1)}, u32[]{:S(2)}, u32[]{:S(2)}) %collective-permute-start.24) | collective-permute-done | bytes 131104 | tf_op jit(solution)/shard_map/ppermute | solution.py:24
  119.0 1.8 %collective-permute-start.27 = (bf16[512,128]{1,0:T(8,128)(2,1)S(1)}, bf16[512,128]{1,0:T(8,128)(2,1)S(1)}, u32[]{:S(2)}, u32[]{:S(2)}) collective-permute-start(bf16[512,128]{1,0:T(8,128)(2,1)S(1)} %fusion.9.refs_0_), channel_id=1, source_target_pairs={{0,6},{1,7},{2,4},{3,5},{4,2},{5,3},{6,0},{7,1},{8,14},{9,15},{10,... | collective-permute-start | bytes 393224 | tf_op jit(solution)/shard_map/ppermute | solution.py:24
  122.7 2.2 %collective-permute-done.27.refs_3_ = bf16[512,128]{1,0:T(8,128)(2,1)S(1)} collective-permute-done((bf16[512,128]{1,0:T(8,128)(2,1)S(1)}, bf16[512,128]{1,0:T(8,128)(2,1)S(1)}, u32[]{:S(2)}, u32[]{:S(2)}) %collective-permute-start.27) | collective-permute-done | bytes 131104 | tf_op jit(solution)/shard_map/ppermute | solution.py:24
  125.0 1.3 %collective-permute-done.26.refs_2_ = bf16[512,128]{1,0:T(8,128)(2,1)S(1)} collective-permute-done((bf16[512,128]{1,0:T(8,128)(2,1)S(1)}, bf16[512,128]{1,0:T(8,128)(2,1)S(1)}, u32[]{:S(2)}, u32[]{:S(2)}) %collective-permute-start.26) | collective-permute-done | bytes 131104 | tf_op jit(solution)/shard_map/ppermute | solution.py:24
  129.2 2.9 %shard_map.91 = f32[512,1024]{1,0:T(8,128)} custom-call(s32[2]{0:T(128)} %pad_add_fusion.ids, bf16[512,128]{1,0:T(8,128)(2,1)} %copy-done.8, bf16[512,128]{1,0:T(8,128)(2,1)} %copy-done.25, bf16[512,128]{1,0:T(8,128)(2,1)} %copy-done.24, bf16[512,128]{1,0:T(8,128)(2,1)} %copy-done.23, bf16[512,128]{1,0:T(8,128)(2,1)} %copy-done.26, ...), custom_call_target="tpu_custom_call" | custom-call | tf_op jit(solution)/shard_map/pallas_call | solution.py:224
  (140 shorter events, 33.6 us)
Async XLA Ops:
  0.6 24.3 %collective-permute-start.2 = (bf16[128,2048]{1,0:T(8,128)(2,1)}, bf16[128,2048]{1,0:T(8,128)(2,1)S(1)}, u32[]{:S(2)}, u32[]{:S(2)}) collective-permute-start(bf16[128,2048]{1,0:T(8,128)(2,1)} %x0.3), channel_id=1, source_target_pairs={{0,6},{1,7},{2,4},{3,5},{4,2},{5,3},{6,0},{7,1},{8,14},{9,15},{10,... | collective-permute-start | bytes 1572872 | tf_op jit(solution)/shard_map/ppermute | solution.py:24
  4.6 23.4 %collective-permute-start.1 = (bf16[128,2048]{1,0:T(8,128)(2,1)}, bf16[128,2048]{1,0:T(8,128)(2,1)S(1)}, u32[]{:S(2)}, u32[]{:S(2)}) collective-permute-start(bf16[128,2048]{1,0:T(8,128)(2,1)} %x0.3), channel_id=1, source_target_pairs={{0,4},{1,5},{2,6},{3,7},{4,0},{5,1},{6,2},{7,3},{8,12},{9,13},{10,... | collective-permute-start | bytes 1572872 | tf_op jit(solution)/shard_map/ppermute | solution.py:24
  5.1 23.3 %collective-permute-start = (bf16[128,2048]{1,0:T(8,128)(2,1)}, bf16[128,2048]{1,0:T(8,128)(2,1)}, u32[]{:S(2)}, u32[]{:S(2)}) collective-permute-start(bf16[128,2048]{1,0:T(8,128)(2,1)} %x0.3), channel_id=1, source_target_pairs={{0,2},{1,3},{2,0},{3,1},{4,6},{5,7},{6,4},{7,5},{8,10},{9,11},{10,... | collective-permute-start | bytes 1572872 | tf_op jit(solution)/shard_map/ppermute | solution.py:24
  5.3 8.5 %collective-permute-start.3 = (bf16[512,128]{1,0:T(8,128)(2,1)S(1)}, bf16[512,128]{1,0:T(8,128)(2,1)S(1)}, u32[]{:S(2)}, u32[]{:S(2)}) collective-permute-start(bf16[512,128]{1,0:T(8,128)(2,1)S(1)} %constant_dynamic-slice_fusion.10), channel_id=1, source_target_pairs={{0,16},{8,24},{16,0},{24,8},{1,17},{9,25},{17,1},{25,9},{2,18},{10... | collective-permute-start | bytes 393224 | tf_op jit(solution)/shard_map/ppermute | solution.py:24
  13.9 6.7 %collective-permute-start.4 = (bf16[2,512,128]{2,1,0:T(8,128)(2,1)S(1)}, bf16[2,512,128]{2,1,0:T(8,128)(2,1)S(1)}, u32[]{:S(2)}, u32[]{:S(2)}) collective-permute-start(bf16[2,512,128]{2,1,0:T(8,128)(2,1)S(1)} %pad_maximum_fusion.4), channel_id=1, source_target_pairs={{0,8},{8,0},{16,24},{24,16},{1,9},{9,1},{17,25},{25,17},{2,10},{10... | collective-permute-start | bytes 786440 | tf_op jit(solution)/shard_map/ppermute | solution.py:24
  21.7 6.7 %collective-permute-start.5 = (bf16[2048,128]{1,0:T(8,128)(2,1)S(1)}, bf16[2048,128]{1,0:T(8,128)(2,1)S(1)}, u32[]{:S(2)}, u32[]{:S(2)}) collective-permute-start(bf16[2048,128]{1,0:T(8,128)(2,1)S(1)} %bitcast_select_fusion.w_own), channel_id=1, source_target_pairs={{0,1},{1,0},{2,3},{3,2},{4,5},{5,4},{6,7},{7,6},{8,9},{9,8},{10,11... | collective-permute-start | bytes 1572872 | tf_op jit(solution)/shard_map/ppermute | solution.py:24
  23.5 18.9 %collective-permute-start.9 = (bf16[128,1024]{1,0:T(8,128)(2,1)}, bf16[128,1024]{1,0:T(8,128)(2,1)}, u32[]{:S(2)}, u32[]{:S(2)}) collective-permute-start(bf16[128,1024]{1,0:T(8,128)(2,1)} %constant_dynamic-slice_fusion.5), channel_id=1, source_target_pairs={{0,1},{1,0},{2,3},{3,2},{4,5},{5,4},{6,7},{7,6},{8,9},{9,8},{10,11... | collective-permute-start | bytes 786440 | tf_op jit(solution)/shard_map/ppermute | solution.py:24
  24.9 19.2 %collective-permute-start.8 = (bf16[128,1024]{1,0:T(8,128)(2,1)S(1)}, bf16[128,1024]{1,0:T(8,128)(2,1)}, u32[]{:S(2)}, u32[]{:S(2)}) collective-permute-start(bf16[128,1024]{1,0:T(8,128)(2,1)S(1)} %constant_dynamic-slice_fusion.8), channel_id=1, source_target_pairs={{0,1},{1,0},{2,3},{3,2},{4,5},{5,4},{6,7},{7,6},{8,9},{9,8},{10,11... | collective-permute-start | bytes 786440 | tf_op jit(solution)/shard_map/ppermute | solution.py:24
  33.3 2.9 %collective-permute-start.6 = (bf16[4,128,128]{2,1,0:T(8,128)(2,1)}, bf16[4,128,128]{2,1,0:T(8,128)(2,1)S(1)}, u32[]{:S(2)}, u32[]{:S(2)}) collective-permute-start(bf16[4,128,128]{2,1,0:T(8,128)(2,1)} %get-tuple-element.35), channel_id=1, source_target_pairs={{0,1},{1,0},{2,3},{3,2},{4,5},{5,4},{6,7},{7,6},{8,9},{9,8},{10,11... | collective-permute-start | bytes 393224 | tf_op jit(solution)/shard_map/ppermute | solution.py:24
  39.0 7.4 %collective-permute-start.7 = (bf16[768,128]{1,0:T(8,128)(2,1)}, bf16[768,128]{1,0:T(8,128)(2,1)S(1)}, u32[]{:S(2)}, u32[]{:S(2)}) collective-permute-start(bf16[768,128]{1,0:T(8,128)(2,1)} %get-tuple-element.37), channel_id=1, source_target_pairs={{0,4},{1,5},{2,6},{3,7},{4,0},{5,1},{6,2},{7,3},{8,12},{9,13},{10,... | collective-permute-start | bytes 589832 | tf_op jit(solution)/shard_map/ppermute | solution.py:24
  40.6 15.6 %collective-permute-start.10 = (bf16[768,128]{1,0:T(8,128)(2,1)}, bf16[768,128]{1,0:T(8,128)(2,1)S(1)}, u32[]{:S(2)}, u32[]{:S(2)}) collective-permute-start(bf16[768,128]{1,0:T(8,128)(2,1)} %get-tuple-element.39), channel_id=1, source_target_pairs={{0,2},{1,3},{2,0},{3,1},{4,6},{5,7},{6,4},{7,5},{8,10},{9,11},{10,... | collective-permute-start | bytes 589832 | tf_op jit(solution)/shard_map/ppermute | solution.py:24
  41.2 14.9 %collective-permute-start.11 = (bf16[768,128]{1,0:T(8,128)(2,1)}, bf16[768,128]{1,0:T(8,128)(2,1)S(1)}, u32[]{:S(2)}, u32[]{:S(2)}) collective-permute-start(bf16[768,128]{1,0:T(8,128)(2,1)} %get-tuple-element.40), channel_id=1, source_target_pairs={{0,6},{1,7},{2,4},{3,5},{4,2},{5,3},{6,0},{7,1},{8,14},{9,15},{10,... | collective-permute-start | bytes 589832 | tf_op jit(solution)/shard_map/ppermute | solution.py:24
  54.4 14.8 %collective-permute-start.15 = (bf16[768,128]{1,0:T(8,128)(2,1)}, bf16[768,128]{1,0:T(8,128)(2,1)S(1)}, u32[]{:S(2)}, u32[]{:S(2)}) collective-permute-start(bf16[768,128]{1,0:T(8,128)(2,1)} %get-tuple-element.50), channel_id=1, source_target_pairs={{0,4},{1,5},{2,6},{3,7},{4,0},{5,1},{6,2},{7,3},{8,12},{9,13},{10,... | collective-permute-start | bytes 589832 | tf_op jit(solution)/shard_map/ppermute | solution.py:24
  64.5 8.0 %collective-permute-start.14 = (bf16[768,128]{1,0:T(8,128)(2,1)}, bf16[768,128]{1,0:T(8,128)(2,1)S(1)}, u32[]{:S(2)}, u32[]{:S(2)}) collective-permute-start(bf16[768,128]{1,0:T(8,128)(2,1)} %get-tuple-element.49), channel_id=1, source_target_pairs={{0,2},{1,3},{2,0},{3,1},{4,6},{5,7},{6,4},{7,5},{8,10},{9,11},{10,... | collective-permute-start | bytes 589832 | tf_op jit(solution)/shard_map/ppermute | solution.py:24
  65.2 9.6 %collective-permute-start.16 = (bf16[768,128]{1,0:T(8,128)(2,1)}, bf16[768,128]{1,0:T(8,128)(2,1)S(1)}, u32[]{:S(2)}, u32[]{:S(2)}) collective-permute-start(bf16[768,128]{1,0:T(8,128)(2,1)} %get-tuple-element.51), channel_id=1, source_target_pairs={{0,6},{1,7},{2,4},{3,5},{4,2},{5,3},{6,0},{7,1},{8,14},{9,15},{10,... | collective-permute-start | bytes 589832 | tf_op jit(solution)/shard_map/ppermute | solution.py:24
  67.4 16.4 %collective-permute-start.13 = (bf16[128,1024]{1,0:T(8,128)(2,1)S(1)}, bf16[128,1024]{1,0:T(8,128)(2,1)S(1)}, u32[]{:S(2)}, u32[]{:S(2)}) collective-permute-start(bf16[128,1024]{1,0:T(8,128)(2,1)S(1)} %maximum_select_fusion.5), channel_id=1, source_target_pairs={{0,1},{1,0},{2,3},{3,2},{4,5},{5,4},{6,7},{7,6},{8,9},{9,8},{10,11... | collective-permute-start | bytes 786440 | tf_op jit(solution)/shard_map/ppermute | solution.py:24
  68.7 16.1 %collective-permute-start.12 = (bf16[128,1024]{1,0:T(8,128)(2,1)S(1)}, bf16[128,1024]{1,0:T(8,128)(2,1)S(1)}, u32[]{:S(2)}, u32[]{:S(2)}) collective-permute-start(bf16[128,1024]{1,0:T(8,128)(2,1)S(1)} %maximum_select_fusion.3), channel_id=1, source_target_pairs={{0,1},{1,0},{2,3},{3,2},{4,5},{5,4},{6,7},{7,6},{8,9},{9,8},{10,11... | collective-permute-start | bytes 786440 | tf_op jit(solution)/shard_map/ppermute | solution.py:24
  77.6 1.6 %collective-permute-start.17 = (bf16[4,128,128]{2,1,0:T(8,128)(2,1)}, bf16[4,128,128]{2,1,0:T(8,128)(2,1)S(1)}, u32[]{:S(2)}, u32[]{:S(2)}) collective-permute-start(bf16[4,128,128]{2,1,0:T(8,128)(2,1)} %get-tuple-element.53), channel_id=1, source_target_pairs={{0,1},{1,0},{2,3},{3,2},{4,5},{5,4},{6,7},{7,6},{8,9},{9,8},{10,11... | collective-permute-start | bytes 393224 | tf_op jit(solution)/shard_map/ppermute | solution.py:24
  83.7 11.7 %collective-permute-start.22 = (bf16[2048,128]{1,0:T(8,128)(2,1)}, bf16[2048,128]{1,0:T(8,128)(2,1)S(1)}, u32[]{:S(2)}, u32[]{:S(2)}) collective-permute-start(bf16[2048,128]{1,0:T(8,128)(2,1)} %get-tuple-element.63), channel_id=1, source_target_pairs={{0,1},{1,0},{2,3},{3,2},{4,5},{5,4},{6,7},{7,6},{8,9},{9,8},{10,11... | collective-permute-start | bytes 1572872 | tf_op jit(solution)/shard_map/ppermute | solution.py:24
  91.1 14.5 %collective-permute-start.20 = (bf16[256,1024]{1,0:T(8,128)(2,1)}, bf16[256,1024]{1,0:T(8,128)(2,1)}, u32[]{:S(2)}, u32[]{:S(2)}) collective-permute-start(bf16[256,1024]{1,0:T(8,128)(2,1)} %pad_maximum_fusion.2), channel_id=1, source_target_pairs={{0,4},{1,5},{2,6},{3,7},{4,0},{5,1},{6,2},{7,3},{8,12},{9,13},{10,... | collective-permute-start | bytes 1572872 | tf_op jit(solution)/shard_map/ppermute | solution.py:24
  94.7 14.2 %collective-permute-start.18 = (bf16[256,1024]{1,0:T(8,128)(2,1)}, bf16[256,1024]{1,0:T(8,128)(2,1)}, u32[]{:S(2)}, u32[]{:S(2)}) collective-permute-start(bf16[256,1024]{1,0:T(8,128)(2,1)} %pad_maximum_fusion.1), channel_id=1, source_target_pairs={{0,2},{1,3},{2,0},{3,1},{4,6},{5,7},{6,4},{7,5},{8,10},{9,11},{10,... | collective-permute-start | bytes 1572872 | tf_op jit(solution)/shard_map/ppermute | solution.py:24
  98.2 12.4 %collective-permute-start.23 = (bf16[2,512,128]{2,1,0:T(8,128)(2,1)S(1)}, bf16[2,512,128]{2,1,0:T(8,128)(2,1)S(1)}, u32[]{:S(2)}, u32[]{:S(2)}) collective-permute-start(bf16[2,512,128]{2,1,0:T(8,128)(2,1)S(1)} %slice.41), channel_id=1, source_target_pairs={{0,8},{8,0},{16,24},{24,16},{1,9},{9,1},{17,25},{25,17},{2,10},{10... | collective-permute-start | bytes 786440 | tf_op jit(solution)/shard_map/ppermute | solution.py:24
  106.8 7.8 %collective-permute-start.21 = (bf16[128,1024]{1,0:T(8,128)(2,1)S(1)}, bf16[128,1024]{1,0:T(8,128)(2,1)S(1)}, u32[]{:S(2)}, u32[]{:S(2)}) collective-permute-start(bf16[128,1024]{1,0:T(8,128)(2,1)S(1)} %fusion), channel_id=1, source_target_pairs={{0,2},{1,3},{2,0},{3,1},{4,6},{5,7},{6,4},{7,5},{8,10},{9,11},{10,... | collective-permute-start | bytes 786440 | tf_op jit(solution)/shard_map/ppermute | solution.py:24
  110.1 12.4 %collective-permute-start.19 = (bf16[128,1024]{1,0:T(8,128)(2,1)S(1)}, bf16[128,1024]{1,0:T(8,128)(2,1)S(1)}, u32[]{:S(2)}, u32[]{:S(2)}) collective-permute-start(bf16[128,1024]{1,0:T(8,128)(2,1)S(1)} %fusion.3), channel_id=1, source_target_pairs={{0,4},{1,5},{2,6},{3,7},{4,0},{5,1},{6,2},{7,3},{8,12},{9,13},{10,... | collective-permute-start | bytes 786440 | tf_op jit(solution)/shard_map/ppermute | solution.py:24
  110.7 8.2 %collective-permute-start.24 = (bf16[512,128]{1,0:T(8,128)(2,1)S(1)}, bf16[512,128]{1,0:T(8,128)(2,1)S(1)}, u32[]{:S(2)}, u32[]{:S(2)}) collective-permute-start(bf16[512,128]{1,0:T(8,128)(2,1)S(1)} %fusion.10), channel_id=1, source_target_pairs={{0,16},{8,24},{16,0},{24,8},{1,17},{9,25},{17,1},{25,9},{2,18},{10... | collective-permute-start | bytes 393224 | tf_op jit(solution)/shard_map/ppermute | solution.py:24
  119.0 6.0 %collective-permute-start.27 = (bf16[512,128]{1,0:T(8,128)(2,1)S(1)}, bf16[512,128]{1,0:T(8,128)(2,1)S(1)}, u32[]{:S(2)}, u32[]{:S(2)}) collective-permute-start(bf16[512,128]{1,0:T(8,128)(2,1)S(1)} %fusion.9.refs_0_), channel_id=1, source_target_pairs={{0,6},{1,7},{2,4},{3,5},{4,2},{5,3},{6,0},{7,1},{8,14},{9,15},{10,... | collective-permute-start | bytes 393224 | tf_op jit(solution)/shard_map/ppermute | solution.py:24
  120.8 5.5 %collective-permute-start.26 = (bf16[512,128]{1,0:T(8,128)(2,1)S(1)}, bf16[512,128]{1,0:T(8,128)(2,1)S(1)}, u32[]{:S(2)}, u32[]{:S(2)}) collective-permute-start(bf16[512,128]{1,0:T(8,128)(2,1)S(1)} %fusion.9.refs_0_), channel_id=1, source_target_pairs={{0,4},{1,5},{2,6},{3,7},{4,0},{5,1},{6,2},{7,3},{8,12},{9,13},{10,... | collective-permute-start | bytes 393224 | tf_op jit(solution)/shard_map/ppermute | solution.py:24
  121.9 5.0 %collective-permute-start.25 = (bf16[512,128]{1,0:T(8,128)(2,1)S(1)}, bf16[512,128]{1,0:T(8,128)(2,1)S(1)}, u32[]{:S(2)}, u32[]{:S(2)}) collective-permute-start(bf16[512,128]{1,0:T(8,128)(2,1)S(1)} %fusion.9.refs_0_), channel_id=1, source_target_pairs={{0,2},{1,3},{2,0},{3,1},{4,6},{5,7},{6,4},{7,5},{8,10},{9,11},{10,... | collective-permute-start | bytes 393224 | tf_op jit(solution)/shard_map/ppermute | solution.py:24
  122.6 5.1 %collective-permute-start.28 = (bf16[512,128]{1,0:T(8,128)(2,1)S(1)}, bf16[512,128]{1,0:T(8,128)(2,1)S(1)}, u32[]{:S(2)}, u32[]{:S(2)}) collective-permute-start(bf16[512,128]{1,0:T(8,128)(2,1)S(1)} %fusion.9.refs_0_), channel_id=1, source_target_pairs={{0,1},{1,0},{2,3},{3,2},{4,5},{5,4},{6,7},{7,6},{8,9},{9,8},{10,11... | collective-permute-start | bytes 393224 | tf_op jit(solution)/shard_map/ppermute | solution.py:24
  124.9 2.8 %collective-permute-start.31 = (bf16[512,128]{1,0:T(8,128)(2,1)S(1)}, bf16[512,128]{1,0:T(8,128)(2,1)S(1)}, u32[]{:S(2)}, u32[]{:S(2)}) collective-permute-start(bf16[512,128]{1,0:T(8,128)(2,1)S(1)} %collective-permute-done.27.refs_3_), channel_id=1, source_target_pairs={{0,1},{1,0},{2,3},{3,2},{4,5},{5,4},{6,7},{7,6},{8,9},{9,8},{10,11... | collective-permute-start | bytes 393224 | tf_op jit(solution)/shard_map/ppermute | solution.py:24
  126.3 1.5 %collective-permute-start.30 = (bf16[512,128]{1,0:T(8,128)(2,1)S(1)}, bf16[512,128]{1,0:T(8,128)(2,1)S(1)}, u32[]{:S(2)}, u32[]{:S(2)}) collective-permute-start(bf16[512,128]{1,0:T(8,128)(2,1)S(1)} %collective-permute-done.26.refs_2_), channel_id=1, source_target_pairs={{0,1},{1,0},{2,3},{3,2},{4,5},{5,4},{6,7},{7,6},{8,9},{9,8},{10,11... | collective-permute-start | bytes 393224 | tf_op jit(solution)/shard_map/ppermute | solution.py:24
  126.9 1.3 %collective-permute-start.29 = (bf16[512,128]{1,0:T(8,128)(2,1)S(1)}, bf16[512,128]{1,0:T(8,128)(2,1)S(1)}, u32[]{:S(2)}, u32[]{:S(2)}) collective-permute-start(bf16[512,128]{1,0:T(8,128)(2,1)S(1)} %collective-permute-done.25.refs_1_), channel_id=1, source_target_pairs={{0,1},{1,0},{2,3},{3,2},{4,5},{5,4},{6,7},{7,6},{8,9},{9,8},{10,11... | collective-permute-start | bytes 393224 | tf_op jit(solution)/shard_map/ppermute | solution.py:24
  (30 other events, 162.0 us)

commit v2 on v0

--- a/solution.py
+++ b/solution.py
@@ -1,6 +1,10 @@
+import functools
+
 import jax
 import jax.numpy as jnp
 from jax import lax
+from jax.experimental import pallas as pl
+from jax.experimental.pallas import tpu as pltpu
 from jax.sharding import PartitionSpec as P
 
 HEADS = 16
@@ -8,8 +12,341 @@
 HEAD_DIM = 128
 REACH = 4
 
-
 NEG_FILL = -1e30
+F32 = jnp.float32
+BF16 = jnp.bfloat16
+
+
+def swap(value, axis, bit):
+    count = lax.axis_size(axis)
+    return lax.ppermute(value, axis, [(i, i ^ bit) for i in range(count)])
+
+
+def dot(a, b, ca, cb):
+    return lax.dot_general(a, b, (((ca,), (cb,)), ((), ())), preferred_element_type=F32)
+
+
+def on_chip(shape, dtype=BF16):
+    return pltpu.VMEM(shape, dtype)
+
+
+def run(body, outs, scalars, arrays, scratch=(), room=16):
+    arrays = [pltpu.with_memory_space_constraint(v, pltpu.VMEM) for v in arrays]
+    return pl.pallas_call(
+        body,
+        out_shape=outs,
+        in_specs=[pl.BlockSpec(memory_space=pltpu.SMEM)] * len(scalars)
+        + [pl.BlockSpec(memory_space=pltpu.VMEM)] * len(arrays),
+        out_specs=jax.tree.map(
+            lambda _: pl.BlockSpec(memory_space=pltpu.VMEM), outs, is_leaf=lambda v: hasattr(v, "dtype")
+        ),
+        scratch_shapes=scratch,
+        compiler_params=pltpu.CompilerParams(vmem_limit_bytes=room << 20),
+    )(*scalars, *arrays)
+
+
+def head_of(chip):
+    return jnp.bitwise_xor(chip % 2, chip // 2)
+
+
+def column_of(chip, core):
+    return (chip // 2) * (KV_HEADS * HEAD_DIM) + (2 * core + head_of(chip)) * HEAD_DIM
+
+
+def quarter(z, r, size):
+    return pl.ds(pl.multiple_of(jnp.bitwise_xor(z, r) * size, size), size)
+
+
+def project_rows(z, xs, ws):
+    size = ws[0].shape[0]
+    total = None
+    for r, w in enumerate(ws):
+        x = jnp.concatenate([x[:, quarter(z, r, size)] for x in xs], axis=0)
+        term = dot(x, w, 1, 0)
+        total = term if total is None else total + term
+    return total.astype(BF16)
+
+
+def project_kernel(ids, *refs):
+    *xs, w0, w2, w13, out = refs
+    ws = (w0[...], w13[0], w2[...], w13[1])
+    out[...] = project_rows(ids[2], xs, ws)
+
+
+def window_kernel(ids, *refs):
+    *xs, w0, w2, w13, first, o0, o1, o2, o3, kv = refs
+    ws = (w0[...], w13[0], w2[...], w13[1])
+    m = ids[0]
+    rows = first.shape[0] // 3
+    for r in range(3):
+        kv[r] = first[r * rows : (r + 1) * rows, :]
+    kv[3] = project_rows(ids[2], xs, ws)
+    for r, out in ((3, o3), (1, o1), (2, o2), (0, o0)):
+        target = jnp.bitwise_xor(m, r)
+        for w in range(3):
+            chip = target + (w - 2)
+            rel = jnp.bitwise_xor(jnp.maximum(chip, 0), m)
+            out[w * rows : (w + 1) * rows, :] = jnp.where(
+                chip >= 0, kv[rel], jnp.zeros((rows, HEAD_DIM), BF16)
+            )
+
+
+def attend_kernel(side, docs, ids, lens, first, second, q_own, q_oth, g_own, g_oth,
+                  own, oth, d_first, d_second, bias):
+    m, c = ids[0], ids[1]
+    rows = q_own.shape[0]
+    keys = first.shape[0]
+    inv = HEAD_DIM ** (-0.5)
+    heads = HEADS // KV_HEADS
+    head = head_of(m) if side == 0 else 1 - head_of(m)
+    base = (2 * c + head) * (heads * HEAD_DIM)
+
+    def place(chip0, shape, dim):
+        t = lax.broadcasted_iota(jnp.int32, shape, dim)
+        chip = t // (2 * rows) + chip0
+        within = t % (2 * rows)
+        mine = within < rows
+        shard = 2 * chip + jnp.where(mine, c, 1 - c)
+        return shard * rows + jnp.where(mine, within, within - rows)
+
+    kpos = place(m - 2, (keys, 1), 0)
+    qpos = place(m, (1, 2 * rows), 1)
+    kdoc = jnp.where(kpos >= 0, 0, -1)
+    qdoc = jnp.zeros_like(qpos)
+    end = jnp.int32(0)
+    for k in range(docs):
+        end = end + lens[0, k]
+        kdoc = kdoc + (kpos >= end).astype(jnp.int32)
+        qdoc = qdoc + (qpos >= end).astype(jnp.int32)
+    bias[...] = jnp.where((kdoc == qdoc) & (kpos <= qpos), 0.0, NEG_FILL)
+
+    is_key = m < 2
+    key = jnp.where(is_key, first[...], second[...])
+    val = jnp.where(is_key, second[...], first[...])
+    key_t = key.T
+    val_t = val.T
+    dk = jnp.zeros((keys, HEAD_DIM), F32)
+    dv = jnp.zeros((keys, HEAD_DIM), F32)
+    for h in range(heads):
+        cols = pl.ds(pl.multiple_of(base + h * HEAD_DIM, HEAD_DIM), HEAD_DIM)
+        q = jnp.concatenate([q_own[:, cols], q_oth[:, cols]], axis=0)
+        g = jnp.concatenate([g_own[:, cols], g_oth[:, cols]], axis=0)
+        s = dot(key, q, 1, 1) * inv + bias[...]
+        p = jnp.exp(s - jnp.max(s, axis=0, keepdims=True))
+        p = p * (1.0 / jnp.sum(p, axis=0, keepdims=True))
+        low = p.astype(BF16)
+        out_t = dot(val_t, low, 1, 0).astype(BF16).astype(F32)
+        delta = jnp.sum(out_t * g.astype(F32).T, axis=0, keepdims=True)
+        dp = dot(val, g, 1, 1)
+        ds = (p * (dp - delta)).astype(BF16)
+        dq_t = dot(key_t, ds, 1, 0) * inv
+        dk = dk + dot(ds, q, 1, 0)
+        dv = dv + dot(low, g, 1, 0)
+        out = out_t.T.astype(BF16)
+        dq = dq_t.T.astype(BF16)
+        at = slice(h * HEAD_DIM, (h + 1) * HEAD_DIM)
+        own[0, :, at] = out[:rows]
+        oth[0, :, at] = out[rows:]
+        own[1, :, at] = dq[:rows]
+        oth[1, :, at] = dq[rows:]
+    dk = (dk * inv).astype(BF16)
+    dv = dv.astype(BF16)
+    d_first[...] = jnp.where(is_key, dk, dv)
+    d_second[...] = jnp.where(is_key, dv, dk)
+
+
+def attend(side, ids, lens, first, second, rest):
+    rows = rest[0].shape[0]
+    keys = first.shape[0]
+    part = on_chip((2, rows, HEADS // KV_HEADS * HEAD_DIM))
+    grad = on_chip((keys, HEAD_DIM))
+    return run(
+        functools.partial(attend_kernel, side, lens.shape[1]),
+        (part, part, grad, grad),
+        (ids, lens),
+        (first, second, *rest),
+        scratch=[pltpu.VMEM((keys, 2 * rows), F32)],
+        room=24,
+    )
+
+
+def place_kernel(ids, own_a, own_b, got_a, got_b, out, dq):
+    m, c = ids[0], ids[1]
+    width = own_a.shape[2]
+    for ref, core, head in (
+        (own_a, c, head_of(m)),
+        (own_b, c, 1 - head_of(m)),
+        (got_a, 1 - c, head_of(m)),
+        (got_b, 1 - c, 1 - head_of(m)),
+    ):
+        cols = pl.ds(pl.multiple_of((2 * core + head) * width, width), width)
+        out[:, cols] = ref[0]
+        dq[:, cols] = ref[1]
+
+
+def weight_block(z, r, g_t, xs, size):
+    x = jnp.concatenate([x[:, quarter(z, r, size)] for x in xs], axis=0)
+    return dot(g_t, x, 1, 0).T
+
+
+def sum_kernel(ids, *refs):
+    d0, d1, d2, d3, *xs, own, oth, g_t, send, acc = refs
+    m, z = ids[0], ids[2]
+    rows = own.shape[1]
+    acc[...] = jnp.zeros_like(acc)
+    for r, d in enumerate((d0, d1, d2, d3)):
+        start = pl.multiple_of(jnp.bitwise_xor(m, r) * (2 * rows), 2 * rows)
+        span = pl.ds(start, 6 * rows)
+        acc[span, :] = acc[span, :] + d[...].astype(F32)
+    for r in range(4):
+        start = pl.multiple_of((jnp.bitwise_xor(m, r) + 2) * (2 * rows), 2 * rows)
+        g = acc[pl.ds(start, 2 * rows), :].astype(BF16)
+        own[r] = g[:rows]
+        oth[r] = g[rows:]
+        g_t[:, r * 2 * rows : (r + 1) * 2 * rows] = g.T
+    for i, r in enumerate((1, 3)):
+        send[i] = weight_block(z, r, g_t[...], xs, send.shape[1]).astype(BF16)
+
+
+def keep_kernel(ids, g_t, *refs):
+    *xs, keep = refs
+    for i, r in enumerate((0, 2)):
+        keep[i] = weight_block(ids[2], r, g_t[...], xs, keep.shape[1])
+
+
+def fold_kernel(keep, got, now, later):
+    now[...] = keep[0] + got[0].astype(F32)
+    later[...] = (keep[1] + got[1].astype(F32)).astype(BF16)
+
+
+def last_kernel(now, got, out):
+    out[...] = (now[...] + got[...].astype(F32)).astype(BF16)
+
+
+def assemble_kernel(ids, *refs):
+    m, c = ids[0], ids[1]
+    out = refs[-1]
+    for side in range(2):
+        core = c if side == 0 else 1 - c
+        for r in range(4):
+            col = pl.multiple_of(column_of(jnp.bitwise_xor(m, r), core), HEAD_DIM)
+            out[:, pl.ds(col, HEAD_DIM)] = refs[4 * side + r][...].astype(F32)
+
+
+def token_kernel(own, oth, w0, w2, w13, u0, u2, u13, send_a, send_b, keep_a, keep_b):
+    rows = own.shape[1]
+    g = jnp.concatenate(
+        [jnp.concatenate([own[r] for r in range(4)], axis=0),
+         jnp.concatenate([oth[r] for r in range(4)], axis=0)], axis=1)
+    ws = (w0[...], w13[0], w2[...], w13[1])
+    us = (u0[...], u13[0], u2[...], u13[1])
+    size = w0.shape[0]
+    for i in range(4):
+        w = jnp.concatenate([ws[i], us[i]], axis=1)
+        t = dot(g, w, 1, 1)
+        at = slice((i % 2) * size, (i % 2 + 1) * size)
+        send, keep, away = (send_a, keep_a, (1, 3)) if i < 2 else (send_b, keep_b, (2, 3))
+        home = [r for r in range(4) if r not in away]
+        for k in range(2):
+            send[k, :, at] = t[away[k] * rows : (away[k] + 1) * rows].astype(BF16)
+            keep[k, :, at] = t[home[k] * rows : (home[k] + 1) * rows]
+
+
+def fold_both_kernel(keep_a, got_a, keep_b, got_b, a, a_send, b, b_send):
+    fold_kernel(keep_a, got_a, a, a_send)
+    fold_kernel(keep_b, got_b, b, b_send)
+
+
+def token_last_kernel(ids, a, got_a, b, got_b, out):
+    size = out.shape[1] // 4
+    for i in range(4):
+        now, got = (a, got_a) if i < 2 else (b, got_b)
+        at = slice((i % 2) * size, (i % 2 + 1) * size)
+        out[:, quarter(ids[2], i, size)] = (now[:, at] + got[:, at].astype(F32)).astype(BF16)
+
+
+def plane_local(tokens, kv_weight, queries, out_grad, doc_lengths):
+    rows, width = tokens.shape
+    size = kv_weight.shape[0]
+    m, c = lax.axis_index("bal") // 2, lax.axis_index("bal") % 2
+    ids = jnp.stack([m, c, lax.axis_index("fsdp")]).astype(jnp.int32)
+    pair = lambda v: swap(v, "bal", 1)
+    near = lambda v: swap(v, "bal", 2)
+    far = lambda v: swap(v, "bal", 4)
+    cross = lambda v: swap(v, "bal", 6)
+
+    x1, x2 = near(tokens), far(tokens)
+    w0 = lax.dynamic_slice(kv_weight, (0, column_of(m, c)), (size, HEAD_DIM))
+    w2 = swap(w0, "fsdp", 2)
+    w13 = swap(jnp.stack([w0, w2]), "fsdp", 1)
+    ws = (w0, w2, w13)
+    x3 = (far(x1[: rows // 2]), near(x2[rows // 2 :]))
+    y0, y1, y2 = pair(tokens), pair(x1), pair(x2)
+    y3 = (pair(x3[0]), pair(x3[1]))
+    early = (tokens, y0, x1, y1, x2, y2)
+    late = (*x3, *y3)
+    xs = early + late
+
+    rest = (queries, pair(queries), out_grad, pair(out_grad))
+
+    first = run(project_kernel, on_chip((6 * rows, HEAD_DIM)), (ids,), early + ws)
+    win = run(
+        window_kernel,
+        (on_chip((6 * rows, HEAD_DIM)),) * 4,
+        (ids,),
+        late + ws + (first,),
+        scratch=[pltpu.VMEM((4, 2 * rows, HEAD_DIM), BF16)],
+    )
+    win3, win1, win2 = cross(win[3]), near(win[1]), far(win[2])
+
+    own_a, oth_a, d0, d3 = attend(0, ids, doc_lengths, win[0], win3, rest)
+    d3 = cross(d3)
+    own_b, oth_b, d1, d2 = attend(1, ids, doc_lengths, win1, win2, rest)
+    d1, d2 = near(d1), far(d2)
+
+    block = on_chip((4, rows, HEAD_DIM))
+    g_own, g_oth, g_t, send = run(
+        sum_kernel,
+        (block, block, on_chip((HEAD_DIM, 8 * rows)), on_chip((2, size, HEAD_DIM))),
+        (ids,),
+        (d0, d1, d2, d3) + xs,
+        scratch=[pltpu.VMEM((12 * rows, HEAD_DIM), F32)],
+    )
+    got = swap(send, "fsdp", 1)
+    g_oth = pair(g_oth)
+    keep = run(keep_kernel, on_chip((2, size, HEAD_DIM), F32), (ids,), (g_t,) + xs)
+    us = tuple(pair(v) for v in ws)
+    half = (rows, width // 2)
+    send_a, send_b, keep_a, keep_b = run(
+        token_kernel,
+        (on_chip((2, *half)), on_chip((2, *half)), on_chip((2, *half), F32), on_chip((2, *half), F32)),
+        (),
+        (g_own, g_oth) + ws + us,
+    )
+    got_a, got_b = near(send_a), far(send_b)
+    fold = (on_chip((size, HEAD_DIM), F32), on_chip((size, HEAD_DIM)))
+    now, later = run(fold_kernel, fold, (), (keep, got))
+    got = swap(later, "fsdp", 2)
+    fold = (on_chip(half, F32), on_chip(half))
+    a, a_send, b, b_send = run(fold_both_kernel, fold + fold, (), (keep_a, got_a, keep_b, got_b))
+    got_a, got_b = far(a_send), near(b_send)
+    mine = run(last_kernel, on_chip((size, HEAD_DIM)), (), (now, got))
+    mine = [mine, near(mine), far(mine), cross(mine)]
+    theirs = [pair(v) for v in mine]
+    grad_weight = run(
+        assemble_kernel,
+        jax.ShapeDtypeStruct((size, kv_weight.shape[1]), F32),
+        (ids,),
+        mine + theirs,
+    )
+    grad_tokens = run(
+        token_last_kernel, jax.ShapeDtypeStruct(tokens.shape, BF16), (ids,), (a, got_a, b, got_b)
+    )
+    like = jax.ShapeDtypeStruct(queries.shape, BF16)
+    attn_out, grad_queries = run(
+        place_kernel, (like, like), (ids,), (own_a, own_b, pair(oth_a), pair(oth_b))
+    )
+    return attn_out, grad_queries, grad_tokens, grad_weight
 
 
 def from_behind(value, axis, steps):
@@ -52,7 +389,7 @@
     return jnp.einsum("hqk,qhd->kd", prob_tile, grad_group, preferred_element_type=jnp.float32)
 
 
-def attend(q_rows, kv_blocks, grad_rows, allowed_parts):
+def attend_rows(q_rows, kv_blocks, grad_rows, allowed_parts):
     row_count = q_rows.shape[0]
     key_rows = kv_blocks[0].shape[0]
     group_size = HEADS // KV_HEADS
@@ -133,7 +470,7 @@
     for distance in range(1, REACH + 1):
         earlier.append(from_behind(kv_rows, "bal", distance))
     kv_blocks = earlier[::-1]
-    attn_out, grad_queries, window_terms = attend(queries, kv_blocks, out_grad, allowed_parts)
+    attn_out, grad_queries, window_terms = attend_rows(queries, kv_blocks, out_grad, allowed_parts)
     grad_terms = window_terms[::-1]
     grad_sum = grad_terms[0]
     for distance in range(1, REACH + 1):
@@ -164,8 +501,9 @@
         P(("fsdp", "bal"), None),
         P("fsdp", None),
     )
+    one_plane = mesh.shape["bal"] == 8 and mesh.shape["fsdp"] == 4
     return jax.shard_map(
-        local,
+        plane_local if one_plane else local,
         mesh=mesh,
         in_specs=placed,
         out_specs=(

time: 316 us -> 106 us (0.34)
  waiting for transfers between devices: 222 us -> 40.1 us
  matrix products: 50 us -> 0 us
  Pallas kernels: 0 us -> 27.3 us
  starting transfers between devices: 15.3 us -> 32.9 us
  between operations: 15 us -> 0.85 us
  other arithmetic: 6.02 us -> 0.1 us
    all_gather x1 -> x0, waiting for transfers between devices: 84 us -> none  [local(): full_weight = lax.all_gather(kv_weight, 'fsdp', axis=0, tiled=True)]
    reduce_scatter x1 -> x0, waiting for transfers between devices: 58.5 us -> none  [local(): lax.psum_scatter(lax.dot_general(tokens, grad_kv, (((0,), (0,)), ((), ())...]
    psum x1 -> x0, waiting for transfers between devices: 55.1 us -> none  [local(): grad_weight = lax.psum(shard_sum, 'bal').astype(jnp.float32)]
    dot_general x123 -> x0, matrix products: 50 us -> none  [the longest x20 16.5 us: query_tile(): jnp.einsum('hqk,kd->qhd', dscore_tile, key_block, preferred_element_type=...]
    pallas_call x0 -> x13, Pallas kernels: none -> 27.3 us  [run(): pl.pallas_call(body, out_shape=outs, in_specs=[pl.BlockSpec(memory_space=...]
    ppermute x8 -> x38, starting transfers between devices: 15.2 us -> 32.9 us  [swap(): return lax.ppermute(value, axis, [(i, i ^ bit) for i in range(count)])]
    ppermute x8 -> x38, waiting for transfers between devices: 23.4 us -> 40.1 us  [swap(): return lax.ppermute(value, axis, [(i, i ^ bit) for i in range(count)])]
  transfers between devices with their start and end apart: 11 -> 38, of which waited for: 7 -> 15; matrix products, arithmetic and copies ran while one was open for 10% -> 0% of each run, Pallas kernels for 0% -> 24%
where the time goes in v2:
time: 106 us
  waiting for transfers between devices  40.1 us (38%)
  starting transfers between devices  32.9 us (31%)
  Pallas kernels  27.3 us (26%)
  local copies, waits for them, and re-layouts  4.53 us (4%)
    ppermute x38, waiting for transfers between devices, swap(): return lax.ppermute(value, axis, [(i, i ^ bit) for i in range(count)])  40.1 us
    ppermute x38, starting transfers between devices, swap(): return lax.ppermute(value, axis, [(i, i ^ bit) for i in range(count)])  32.9 us
    pallas_call x13, Pallas kernels, run(): pl.pallas_call(body, out_shape=outs, in_specs=[pl.BlockSpec(memory_space=...  27.3 us
    unnamed x24, local copies, waits for them, and re-layouts  4.42 us
  transfers between devices with their start and end apart: 38, of which 15 were waited for; matrix products, arithmetic and copies ran while one was open for 0% of the time, Pallas kernels for 24%

profile of v2, /device:TPU:0, one launch (start us, length us, event | category | flops | bytes accessed | tf_op | source)
XLA Modules:
  0.0 105.8 jit_solution(5933765494688360457)
XLA Ops:
  0.7 3.1 %collective-permute-start.2 = (bf16[128,2048]{1,0:T(8,128)(2,1)}, bf16[128,2048]{1,0:T(8,128)(2,1)S(1)}, u32[]{:S(2)}, u32[]{:S(2)}) collective-permute-start(bf16[128,2048]{1,0:T(8,128)(2,1)} %refs_0_.3), channel_id=1, source_target_pairs={{0,4},{1,5},{2,6},{3,7},{4,0},{5,1},{6,2},{7,3},{8,12},{9,13},{10,... | collective-permute-start | bytes 1572872 | tf_op jit(solution)/shard_map/ppermute | solution.py:22
  3.7 1.5 %collective-permute-start = (bf16[128,2048]{1,0:T(8,128)(2,1)}, bf16[128,2048]{1,0:T(8,128)(2,1)S(1)}, u32[]{:S(2)}, u32[]{:S(2)}) collective-permute-start(bf16[128,2048]{1,0:T(8,128)(2,1)} %refs_0_.3), channel_id=1, source_target_pairs={{0,2},{1,3},{2,0},{3,1},{4,6},{5,7},{6,4},{7,5},{8,10},{9,11},{10,... | collective-permute-start | bytes 1572872 | tf_op jit(solution)/shard_map/ppermute | solution.py:22
  5.3 2.7 %collective-permute-start.6 = (bf16[512,128]{1,0:T(8,128)(2,1)S(1)}, bf16[512,128]{1,0:T(8,128)(2,1)S(1)}, u32[]{:S(2)}, u32[]{:S(2)}) collective-permute-start(bf16[512,128]{1,0:T(8,128)(2,1)S(1)} %constant_dynamic-slice_fusion.refs_6_.refs_4_.w0), channel_id=1, source_target_pairs={{0,16},{8,24},{16,0},{24,8},{1,17},{9,25},{17,1},{25,9},{2,18},{10... | collective-permute-start | bytes 393224 | tf_op jit(solution)/shard_map/ppermute | solution.py:22
  7.9 5.8 %collective-permute-done.6.refs_7_.refs_5_.w2 = bf16[512,128]{1,0:T(8,128)(2,1)S(1)} collective-permute-done((bf16[512,128]{1,0:T(8,128)(2,1)S(1)}, bf16[512,128]{1,0:T(8,128)(2,1)S(1)}, u32[]{:S(2)}, u32[]{:S(2)}) %collective-permute-start.6) | collective-permute-done | bytes 131104 | tf_op jit(solution)/shard_map/ppermute | solution.py:22
  15.9 1.5 %collective-permute-done.refs_2_.refs_6_ = bf16[128,2048]{1,0:T(8,128)(2,1)S(1)} collective-permute-done((bf16[128,2048]{1,0:T(8,128)(2,1)}, bf16[128,2048]{1,0:T(8,128)(2,1)S(1)}, u32[]{:S(2)}, u32[]{:S(2)}) %collective-permute-start) | collective-permute-done | bytes 524320 | tf_op jit(solution)/shard_map/ppermute | solution.py:22
  17.8 1.7 %collective-permute-start.3 = (bf16[64,2048]{1,0:T(8,128)(2,1)S(1)}, bf16[64,2048]{1,0:T(8,128)(2,1)}, u32[]{:S(2)}, u32[]{:S(2)}) collective-permute-start(bf16[64,2048]{1,0:T(8,128)(2,1)S(1)} %slice.9), channel_id=1, source_target_pairs={{0,2},{1,3},{2,0},{3,1},{4,6},{5,7},{6,4},{7,5},{8,10},{9,11},{10,... | collective-permute-start | bytes 786440 | tf_op jit(solution)/shard_map/ppermute | solution.py:22
  19.5 1.5 %collective-permute-done.7.refs_8_.refs_6_.w13 = bf16[2,512,128]{2,1,0:T(8,128)(2,1)S(1)} collective-permute-done((bf16[2,512,128]{2,1,0:T(8,128)(2,1)S(1)}, bf16[2,512,128]{2,1,0:T(8,128)(2,1)S(1)}, u32[]{:S(2)}, u32[]{:S(2)}) %collective-permute-start.7) | collective-permute-done | bytes 262176 | tf_op jit(solution)/shard_map/ppermute | solution.py:22
  22.2 2.4 %collective-permute-done.1.refs_0_.refs_10_.refs_6_ = bf16[64,2048]{1,0:T(8,128)(2,1)S(1)} collective-permute-done((bf16[64,2048]{1,0:T(8,128)(2,1)S(1)}, bf16[64,2048]{1,0:T(8,128)(2,1)S(1)}, u32[]{:S(2)}, u32[]{:S(2)}) %collective-permute-start.1) | collective-permute-done | bytes 262176 | tf_op jit(solution)/shard_map/ppermute | solution.py:22
  24.7 1.6 %collective-permute-done.3.refs_1_.refs_11_.refs_7_ = bf16[64,2048]{1,0:T(8,128)(2,1)} collective-permute-done((bf16[64,2048]{1,0:T(8,128)(2,1)S(1)}, bf16[64,2048]{1,0:T(8,128)(2,1)}, u32[]{:S(2)}, u32[]{:S(2)}) %collective-permute-start.3) | collective-permute-done | bytes 262176 | tf_op jit(solution)/shard_map/ppermute | solution.py:22
  30.6 2.0 %shard_map.84.refs_7_ = bf16[768,128]{1,0:T(8,128)(2,1)S(1)} custom-call(s32[3]{0:T(128)S(1)} %pad_add_fusion.ids, bf16[128,2048]{1,0:T(8,128)(2,1)S(1)} %copy-done.1, bf16[128,2048]{1,0:T(8,128)(2,1)S(1)} %collective-permute-done.8.refs_1_.refs_5_, bf16[128,2048]{1,0:T(8,128)(2,1)S(1)} %collective-permute-done.refs_2_.refs_6_, ...), custom_call_target="tpu_custom_call" | custom-call | tf_op jit(solution)/shard_map/pallas_call | solution.py:35
  32.7 1.7 %shard_map.85 = (bf16[768,128]{1,0:T(8,128)(2,1)S(1)}, bf16[768,128]{1,0:T(8,128)(2,1)S(1)}, bf16[768,128]{1,0:T(8,128)(2,1)S(1)}, bf16[768,128]{1,0:T(8,128)(2,1)S(1)}) custom-call(s32[3]{0:T(128)S(1)} %pad_add_fusion.ids, bf16[64,2048]{1,0:T(8,128)(2,1)S(1)} %collective-permute-done.1.refs_0_.refs_10_.refs_6_, ...), custom_call_target="tpu_custom_call" | custom-call | tf_op jit(solution)/shard_map/pallas_call | solution.py:35
  34.4 1.6 %collective-permute-start.14 = (bf16[768,128]{1,0:T(8,128)(2,1)S(1)}, bf16[768,128]{1,0:T(8,128)(2,1)S(1)}, u32[]{:S(2)}, u32[]{:S(2)}) collective-permute-start(bf16[768,128]{1,0:T(8,128)(2,1)S(1)} %get-tuple-element.35), channel_id=1, source_target_pairs={{0,2},{1,3},{2,0},{3,1},{4,6},{5,7},{6,4},{7,5},{8,10},{9,11},{10,... | collective-permute-start | bytes 589832 | tf_op jit(solution)/shard_map/ppermute | solution.py:22
  36.5 1.5 %collective-permute-start.11 = (bf16[768,128]{1,0:T(8,128)(2,1)S(1)}, bf16[768,128]{1,0:T(8,128)(2,1)S(1)}, u32[]{:S(2)}, u32[]{:S(2)}) collective-permute-start(bf16[768,128]{1,0:T(8,128)(2,1)S(1)} %get-tuple-element.33), channel_id=1, source_target_pairs={{0,6},{1,7},{2,4},{3,5},{4,2},{5,3},{6,0},{7,1},{8,14},{9,15},{10,... | collective-permute-start | bytes 589832 | tf_op jit(solution)/shard_map/ppermute | solution.py:22
  38.0 4.3 %collective-permute-done.14.first = bf16[768,128]{1,0:T(8,128)(2,1)S(1)} collective-permute-done((bf16[768,128]{1,0:T(8,128)(2,1)S(1)}, bf16[768,128]{1,0:T(8,128)(2,1)S(1)}, u32[]{:S(2)}, u32[]{:S(2)}) %collective-permute-start.14) | collective-permute-done | bytes 196640 | tf_op jit(solution)/shard_map/ppermute | solution.py:22
  42.2 4.5 %collective-permute-done.15.second = bf16[768,128]{1,0:T(8,128)(2,1)S(1)} collective-permute-done((bf16[768,128]{1,0:T(8,128)(2,1)S(1)}, bf16[768,128]{1,0:T(8,128)(2,1)S(1)}, u32[]{:S(2)}, u32[]{:S(2)}) %collective-permute-start.15) | collective-permute-done | bytes 196640 | tf_op jit(solution)/shard_map/ppermute | solution.py:22
  46.7 6.7 %shard_map.87 = (bf16[2,128,512]{2,1,0:T(8,128)(2,1)S(1)}, bf16[2,128,512]{2,1,0:T(8,128)(2,1)S(1)}, bf16[768,128]{1,0:T(8,128)(2,1)S(1)}, bf16[768,128]{1,0:T(8,128)(2,1)S(1)}) custom-call(s32[3]{0:T(128)S(1)} %pad_add_fusion.ids, s32[1,4]{1,0:T(1,128)S(1)} %copy-done.11, bf16[768,128]{1,0:T(8,128)(2,1)S(1)} %collective-permute-done.14.first, ...), custom_call_target="tpu_custom_call" | custom-call | tf_op jit(solution)/shard_map/pallas_call | solution.py:35
  54.2 6.7 %shard_map.86 = (bf16[2,128,512]{2,1,0:T(8,128)(2,1)S(1)}, bf16[2,128,512]{2,1,0:T(8,128)(2,1)S(1)}, bf16[768,128]{1,0:T(8,128)(2,1)S(1)}, bf16[768,128]{1,0:T(8,128)(2,1)S(1)}) custom-call(s32[3]{0:T(128)S(1)} %pad_add_fusion.ids, s32[1,4]{1,0:T(1,128)S(1)} %copy-done.11, bf16[768,128]{1,0:T(8,128)(2,1)S(1)} %get-tuple-element.32.first, ...), custom_call_target="tpu_custom_call" | custom-call | tf_op jit(solution)/shard_map/pallas_call | solution.py:35
  60.9 2.9 %collective-permute-start.20 = (bf16[768,128]{1,0:T(8,128)(2,1)S(1)}, bf16[768,128]{1,0:T(8,128)(2,1)S(1)}, u32[]{:S(2)}, u32[]{:S(2)}) collective-permute-start(bf16[768,128]{1,0:T(8,128)(2,1)S(1)} %get-tuple-element.45), channel_id=1, source_target_pairs={{0,6},{1,7},{2,4},{3,5},{4,2},{5,3},{6,0},{7,1},{8,14},{9,15},{10,... | collective-permute-start | bytes 589832 | tf_op jit(solution)/shard_map/ppermute | solution.py:22
  64.4 3.2 %collective-permute-done.20.refs_3_ = bf16[768,128]{1,0:T(8,128)(2,1)S(1)} collective-permute-done((bf16[768,128]{1,0:T(8,128)(2,1)S(1)}, bf16[768,128]{1,0:T(8,128)(2,1)S(1)}, u32[]{:S(2)}, u32[]{:S(2)}) %collective-permute-start.20) | collective-permute-done | bytes 196640 | tf_op jit(solution)/shard_map/ppermute | solution.py:22
  67.5 2.0 %shard_map.89 = (bf16[4,128,128]{2,1,0:T(8,128)(2,1)S(1)}, bf16[4,128,128]{2,1,0:T(8,128)(2,1)S(1)}, bf16[128,1024]{1,0:T(8,128)(2,1)S(1)}, bf16[2,512,128]{2,1,0:T(8,128)(2,1)S(1)}) custom-call(s32[3]{0:T(128)S(1)} %pad_add_fusion.ids, bf16[768,128]{1,0:T(8,128)(2,1)S(1)} %get-tuple-element.42.refs_0_, ...), custom_call_target="tpu_custom_call" | custom-call | tf_op jit(solution)/shard_map/pallas_call | solution.py:35
  71.8 2.0 %collective-permute-start.25 = (bf16[2,128,1024]{2,1,0:T(8,128)(2,1)S(1)}, bf16[2,128,1024]{2,1,0:T(8,128)(2,1)S(1)}, u32[]{:S(2)}, u32[]{:S(2)}) collective-permute-start(bf16[2,128,1024]{2,1,0:T(8,128)(2,1)S(1)} %get-tuple-element.49), channel_id=1, source_target_pairs={{0,2},{1,3},{2,0},{3,1},{4,6},{5,7},{6,4},{7,5},{8,10},{9,11},{10,... | collective-permute-start | bytes 1572872 | tf_op jit(solution)/shard_map/ppermute | solution.py:22
  73.8 1.4 %collective-permute-start.26 = (bf16[2,128,1024]{2,1,0:T(8,128)(2,1)S(1)}, bf16[2,128,1024]{2,1,0:T(8,128)(2,1)S(1)}, u32[]{:S(2)}, u32[]{:S(2)}) collective-permute-start(bf16[2,128,1024]{2,1,0:T(8,128)(2,1)S(1)} %get-tuple-element.51), channel_id=1, source_target_pairs={{0,4},{1,5},{2,6},{3,7},{4,0},{5,1},{6,2},{7,3},{8,12},{9,13},{10,... | collective-permute-start | bytes 1572872 | tf_op jit(solution)/shard_map/ppermute | solution.py:22
  75.2 1.6 %collective-permute-start.29 = (bf16[2,512,128]{2,1,0:T(8,128)(2,1)S(1)}, bf16[2,512,128]{2,1,0:T(8,128)(2,1)S(1)}, u32[]{:S(2)}, u32[]{:S(2)}) collective-permute-start(bf16[2,512,128]{2,1,0:T(8,128)(2,1)S(1)} %get-tuple-element.57), channel_id=1, source_target_pairs={{0,8},{8,0},{16,24},{24,16},{1,9},{9,1},{17,25},{25,17},{2,10},{10... | collective-permute-start | bytes 786440 | tf_op jit(solution)/shard_map/ppermute | solution.py:22
  77.3 1.8 %shard_map.93.keep = f32[2,512,128]{2,1,0:T(8,128)S(1)} custom-call(s32[3]{0:T(128)S(1)} %pad_add_fusion.ids, bf16[128,1024]{1,0:T(8,128)(2,1)S(1)} %get-tuple-element.56.g_t, bf16[128,2048]{1,0:T(8,128)(2,1)S(1)} %copy-done.1, bf16[128,2048]{1,0:T(8,128)(2,1)S(1)} %collective-permute-done.8.refs_1_.refs_5_, ...), custom_call_target="tpu_custom_call" | custom-call | tf_op jit(solution)/shard_map/pallas_call | solution.py:35
  79.1 3.9 %collective-permute-done.29.got = bf16[2,512,128]{2,1,0:T(8,128)(2,1)S(1)} collective-permute-done((bf16[2,512,128]{2,1,0:T(8,128)(2,1)S(1)}, bf16[2,512,128]{2,1,0:T(8,128)(2,1)S(1)}, u32[]{:S(2)}, u32[]{:S(2)}) %collective-permute-start.29) | collective-permute-done | bytes 262176 | tf_op jit(solution)/shard_map/ppermute | solution.py:22
  83.1 2.7 %collective-permute-start.30 = (bf16[512,128]{1,0:T(8,128)(2,1)S(1)}, bf16[512,128]{1,0:T(8,128)(2,1)S(1)}, u32[]{:S(2)}, u32[]{:S(2)}) collective-permute-start(bf16[512,128]{1,0:T(8,128)(2,1)S(1)} %get-tuple-element.59), channel_id=1, source_target_pairs={{0,16},{8,24},{16,0},{24,8},{1,17},{9,25},{17,1},{25,9},{2,18},{10... | collective-permute-start | bytes 393224 | tf_op jit(solution)/shard_map/ppermute | solution.py:22
  85.7 5.3 %collective-permute-done.30.got = bf16[512,128]{1,0:T(8,128)(2,1)S(1)} collective-permute-done((bf16[512,128]{1,0:T(8,128)(2,1)S(1)}, bf16[512,128]{1,0:T(8,128)(2,1)S(1)}, u32[]{:S(2)}, u32[]{:S(2)}) %collective-permute-start.30) | collective-permute-done | bytes 131104 | tf_op jit(solution)/shard_map/ppermute | solution.py:22
  92.3 2.3 %collective-permute-start.33 = (bf16[512,128]{1,0:T(8,128)(2,1)S(1)}, bf16[512,128]{1,0:T(8,128)(2,1)S(1)}, u32[]{:S(2)}, u32[]{:S(2)}) collective-permute-start(bf16[512,128]{1,0:T(8,128)(2,1)S(1)} %shard_map.95.refs_0_), channel_id=1, source_target_pairs={{0,6},{1,7},{2,4},{3,5},{4,2},{5,3},{6,0},{7,1},{8,14},{9,15},{10,... | collective-permute-start | bytes 393224 | tf_op jit(solution)/shard_map/ppermute | solution.py:22
  97.0 1.9 %collective-permute-done.32.refs_2_ = bf16[512,128]{1,0:T(8,128)(2,1)S(1)} collective-permute-done((bf16[512,128]{1,0:T(8,128)(2,1)S(1)}, bf16[512,128]{1,0:T(8,128)(2,1)S(1)}, u32[]{:S(2)}, u32[]{:S(2)}) %collective-permute-start.32) | collective-permute-done | bytes 131104 | tf_op jit(solution)/shard_map/ppermute | solution.py:22
  99.5 1.6 %shard_map.88 = (bf16[128,2048]{1,0:T(8,128)(2,1)}, bf16[128,2048]{1,0:T(8,128)(2,1)}) custom-call(s32[3]{0:T(128)S(1)} %pad_add_fusion.ids, bf16[2,128,512]{2,1,0:T(8,128)(2,1)S(1)} %get-tuple-element.34.own_a, bf16[2,128,512]{2,1,0:T(8,128)(2,1)S(1)} %get-tuple-element.37.own_b, bf16[2,128,512]{2,1,0:T(8,128)(2,1)S(1)} %collective-permute-done.16.got_a, ...), custom_call_target="tpu_custom_call" | custom-call | tf_op jit(solution)/shard_map/pallas_call | solution.py:35
  101.1 2.1 %shard_map.96 = f32[512,1024]{1,0:T(8,128)} custom-call(s32[3]{0:T(128)S(1)} %pad_add_fusion.ids, bf16[512,128]{1,0:T(8,128)(2,1)S(1)} %shard_map.95.refs_0_, bf16[512,128]{1,0:T(8,128)(2,1)S(1)} %collective-permute-done.31.refs_1_, bf16[512,128]{1,0:T(8,128)(2,1)S(1)} %collective-permute-done.32.refs_2_, ...), custom_call_target="tpu_custom_call" | custom-call | tf_op jit(solution)/shard_map/pallas_call | solution.py:35
  104.4 1.4 %shard_map.92 = bf16[128,2048]{1,0:T(8,128)(2,1)} custom-call(s32[3]{0:T(128)S(1)} %pad_add_fusion.ids, f32[128,1024]{1,0:T(8,128)S(1)} %get-tuple-element.52.a, bf16[128,1024]{1,0:T(8,128)(2,1)S(1)} %collective-permute-done.27.got_a, f32[128,1024]{1,0:T(8,128)S(1)} %get-tuple-element.54.b, bf16[128,1024]{1,0:T(8,128)(2,1)S(1)} %collective-permute-done.28.got_b), custom_call_target="tpu_custom_call" | custom-call | tf_op jit(solution)/shard_map/pallas_call | solution.py:35
  (87 shorter events, 18.3 us)
Async XLA Ops:
  0.7 15.2 %collective-permute-start.2 = (bf16[128,2048]{1,0:T(8,128)(2,1)}, bf16[128,2048]{1,0:T(8,128)(2,1)S(1)}, u32[]{:S(2)}, u32[]{:S(2)}) collective-permute-start(bf16[128,2048]{1,0:T(8,128)(2,1)} %refs_0_.3), channel_id=1, source_target_pairs={{0,4},{1,5},{2,6},{3,7},{4,0},{5,1},{6,2},{7,3},{8,12},{9,13},{10,... | collective-permute-start | bytes 1572872 | tf_op jit(solution)/shard_map/ppermute | solution.py:22
  3.7 13.6 %collective-permute-start = (bf16[128,2048]{1,0:T(8,128)(2,1)}, bf16[128,2048]{1,0:T(8,128)(2,1)S(1)}, u32[]{:S(2)}, u32[]{:S(2)}) collective-permute-start(bf16[128,2048]{1,0:T(8,128)(2,1)} %refs_0_.3), channel_id=1, source_target_pairs={{0,2},{1,3},{2,0},{3,1},{4,6},{5,7},{6,4},{7,5},{8,10},{9,11},{10,... | collective-permute-start | bytes 1572872 | tf_op jit(solution)/shard_map/ppermute | solution.py:22
  5.3 8.4 %collective-permute-start.6 = (bf16[512,128]{1,0:T(8,128)(2,1)S(1)}, bf16[512,128]{1,0:T(8,128)(2,1)S(1)}, u32[]{:S(2)}, u32[]{:S(2)}) collective-permute-start(bf16[512,128]{1,0:T(8,128)(2,1)S(1)} %constant_dynamic-slice_fusion.refs_6_.refs_4_.w0), channel_id=1, source_target_pairs={{0,16},{8,24},{16,0},{24,8},{1,17},{9,25},{17,1},{25,9},{2,18},{10... | collective-permute-start | bytes 393224 | tf_op jit(solution)/shard_map/ppermute | solution.py:22
  7.9 13.8 %collective-permute-start.8 = (bf16[128,2048]{1,0:T(8,128)(2,1)}, bf16[128,2048]{1,0:T(8,128)(2,1)S(1)}, u32[]{:S(2)}, u32[]{:S(2)}) collective-permute-start(bf16[128,2048]{1,0:T(8,128)(2,1)} %refs_0_.3), channel_id=1, source_target_pairs={{0,1},{1,0},{2,3},{3,2},{4,5},{5,4},{6,7},{7,6},{8,9},{9,8},{10,11... | collective-permute-start | bytes 1572872 | tf_op jit(solution)/shard_map/ppermute | solution.py:22
  13.7 7.3 %collective-permute-start.7 = (bf16[2,512,128]{2,1,0:T(8,128)(2,1)S(1)}, bf16[2,512,128]{2,1,0:T(8,128)(2,1)S(1)}, u32[]{:S(2)}, u32[]{:S(2)}) collective-permute-start(bf16[2,512,128]{2,1,0:T(8,128)(2,1)S(1)} %pad_maximum_fusion), channel_id=1, source_target_pairs={{0,8},{8,0},{16,24},{24,16},{1,9},{9,1},{17,25},{25,17},{2,10},{10... | collective-permute-start | bytes 786440 | tf_op jit(solution)/shard_map/ppermute | solution.py:22
  15.9 10.5 %collective-permute-start.10 = (bf16[128,2048]{1,0:T(8,128)(2,1)S(1)}, bf16[128,2048]{1,0:T(8,128)(2,1)S(1)}, u32[]{:S(2)}, u32[]{:S(2)}) collective-permute-start(bf16[128,2048]{1,0:T(8,128)(2,1)S(1)} %collective-permute-done.2.refs_4_.refs_8_), channel_id=1, source_target_pairs={{0,1},{1,0},{2,3},{3,2},{4,5},{5,4},{6,7},{7,6},{8,9},{9,8},{10,11... | collective-permute-start | bytes 1572872 | tf_op jit(solution)/shard_map/ppermute | solution.py:22
  17.3 7.3 %collective-permute-start.1 = (bf16[64,2048]{1,0:T(8,128)(2,1)S(1)}, bf16[64,2048]{1,0:T(8,128)(2,1)S(1)}, u32[]{:S(2)}, u32[]{:S(2)}) collective-permute-start(bf16[64,2048]{1,0:T(8,128)(2,1)S(1)} %slice.8), channel_id=1, source_target_pairs={{0,4},{1,5},{2,6},{3,7},{4,0},{5,1},{6,2},{7,3},{8,12},{9,13},{10,... | collective-permute-start | bytes 786440 | tf_op jit(solution)/shard_map/ppermute | solution.py:22
  17.8 8.5 %collective-permute-start.3 = (bf16[64,2048]{1,0:T(8,128)(2,1)S(1)}, bf16[64,2048]{1,0:T(8,128)(2,1)}, u32[]{:S(2)}, u32[]{:S(2)}) collective-permute-start(bf16[64,2048]{1,0:T(8,128)(2,1)S(1)} %slice.9), channel_id=1, source_target_pairs={{0,2},{1,3},{2,0},{3,1},{4,6},{5,7},{6,4},{7,5},{8,10},{9,11},{10,... | collective-permute-start | bytes 786440 | tf_op jit(solution)/shard_map/ppermute | solution.py:22
  21.7 6.0 %collective-permute-start.9 = (bf16[128,2048]{1,0:T(8,128)(2,1)S(1)}, bf16[128,2048]{1,0:T(8,128)(2,1)}, u32[]{:S(2)}, u32[]{:S(2)}) collective-permute-start(bf16[128,2048]{1,0:T(8,128)(2,1)S(1)} %collective-permute-done.refs_2_.refs_6_), channel_id=1, source_target_pairs={{0,1},{1,0},{2,3},{3,2},{4,5},{5,4},{6,7},{7,6},{8,9},{9,8},{10,11... | collective-permute-start | bytes 1572872 | tf_op jit(solution)/shard_map/ppermute | solution.py:22
  21.7 16.2 %collective-permute-start.12 = (bf16[128,2048]{1,0:T(8,128)(2,1)}, bf16[128,2048]{1,0:T(8,128)(2,1)}, u32[]{:S(2)}, u32[]{:S(2)}) collective-permute-start(bf16[128,2048]{1,0:T(8,128)(2,1)} %q_own.3), channel_id=1, source_target_pairs={{0,1},{1,0},{2,3},{3,2},{4,5},{5,4},{6,7},{7,6},{8,9},{9,8},{10,11... | collective-permute-start | bytes 1572872 | tf_op jit(solution)/shard_map/ppermute | solution.py:22
  24.7 13.3 %collective-permute-start.13 = (bf16[128,2048]{1,0:T(8,128)(2,1)}, bf16[128,2048]{1,0:T(8,128)(2,1)}, u32[]{:S(2)}, u32[]{:S(2)}) collective-permute-start(bf16[128,2048]{1,0:T(8,128)(2,1)} %g_own.3), channel_id=1, source_target_pairs={{0,1},{1,0},{2,3},{3,2},{4,5},{5,4},{6,7},{7,6},{8,9},{9,8},{10,11... | collective-permute-start | bytes 1572872 | tf_op jit(solution)/shard_map/ppermute | solution.py:22
  26.3 6.3 %collective-permute-start.4 = (bf16[64,2048]{1,0:T(8,128)(2,1)S(1)}, bf16[64,2048]{1,0:T(8,128)(2,1)}, u32[]{:S(2)}, u32[]{:S(2)}) collective-permute-start(bf16[64,2048]{1,0:T(8,128)(2,1)S(1)} %collective-permute-done.1.refs_0_.refs_10_.refs_6_), channel_id=1, source_target_pairs={{0,1},{1,0},{2,3},{3,2},{4,5},{5,4},{6,7},{7,6},{8,9},{9,8},{10,11... | collective-permute-start | bytes 786440 | tf_op jit(solution)/shard_map/ppermute | solution.py:22
  27.1 5.5 %collective-permute-start.5 = (bf16[64,2048]{1,0:T(8,128)(2,1)}, bf16[64,2048]{1,0:T(8,128)(2,1)}, u32[]{:S(2)}, u32[]{:S(2)}) collective-permute-start(bf16[64,2048]{1,0:T(8,128)(2,1)} %collective-permute-done.3.refs_1_.refs_11_.refs_7_), channel_id=1, source_target_pairs={{0,1},{1,0},{2,3},{3,2},{4,5},{5,4},{6,7},{7,6},{8,9},{9,8},{10,11... | collective-permute-start | bytes 786440 | tf_op jit(solution)/shard_map/ppermute | solution.py:22
  34.4 7.8 %collective-permute-start.14 = (bf16[768,128]{1,0:T(8,128)(2,1)S(1)}, bf16[768,128]{1,0:T(8,128)(2,1)S(1)}, u32[]{:S(2)}, u32[]{:S(2)}) collective-permute-start(bf16[768,128]{1,0:T(8,128)(2,1)S(1)} %get-tuple-element.35), channel_id=1, source_target_pairs={{0,2},{1,3},{2,0},{3,1},{4,6},{5,7},{6,4},{7,5},{8,10},{9,11},{10,... | collective-permute-start | bytes 589832 | tf_op jit(solution)/shard_map/ppermute | solution.py:22
  36.0 10.7 %collective-permute-start.15 = (bf16[768,128]{1,0:T(8,128)(2,1)S(1)}, bf16[768,128]{1,0:T(8,128)(2,1)S(1)}, u32[]{:S(2)}, u32[]{:S(2)}) collective-permute-start(bf16[768,128]{1,0:T(8,128)(2,1)S(1)} %get-tuple-element.36), channel_id=1, source_target_pairs={{0,4},{1,5},{2,6},{3,7},{4,0},{5,1},{6,2},{7,3},{8,12},{9,13},{10,... | collective-permute-start | bytes 589832 | tf_op jit(solution)/shard_map/ppermute | solution.py:22
  36.5 17.7 %collective-permute-start.11 = (bf16[768,128]{1,0:T(8,128)(2,1)S(1)}, bf16[768,128]{1,0:T(8,128)(2,1)S(1)}, u32[]{:S(2)}, u32[]{:S(2)}) collective-permute-start(bf16[768,128]{1,0:T(8,128)(2,1)S(1)} %get-tuple-element.33), channel_id=1, source_target_pairs={{0,6},{1,7},{2,4},{3,5},{4,2},{5,3},{6,0},{7,1},{8,14},{9,15},{10,... | collective-permute-start | bytes 589832 | tf_op jit(solution)/shard_map/ppermute | solution.py:22
  53.4 10.9 %collective-permute-start.18 = (bf16[768,128]{1,0:T(8,128)(2,1)S(1)}, bf16[768,128]{1,0:T(8,128)(2,1)S(1)}, u32[]{:S(2)}, u32[]{:S(2)}) collective-permute-start(bf16[768,128]{1,0:T(8,128)(2,1)S(1)} %get-tuple-element.43), channel_id=1, source_target_pairs={{0,2},{1,3},{2,0},{3,1},{4,6},{5,7},{6,4},{7,5},{8,10},{9,11},{10,... | collective-permute-start | bytes 589832 | tf_op jit(solution)/shard_map/ppermute | solution.py:22
  54.0 10.3 %collective-permute-start.19 = (bf16[768,128]{1,0:T(8,128)(2,1)S(1)}, bf16[768,128]{1,0:T(8,128)(2,1)S(1)}, u32[]{:S(2)}, u32[]{:S(2)}) collective-permute-start(bf16[768,128]{1,0:T(8,128)(2,1)S(1)} %get-tuple-element.44), channel_id=1, source_target_pairs={{0,4},{1,5},{2,6},{3,7},{4,0},{5,1},{6,2},{7,3},{8,12},{9,13},{10,... | collective-permute-start | bytes 589832 | tf_op jit(solution)/shard_map/ppermute | solution.py:22
  60.9 6.6 %collective-permute-start.20 = (bf16[768,128]{1,0:T(8,128)(2,1)S(1)}, bf16[768,128]{1,0:T(8,128)(2,1)S(1)}, u32[]{:S(2)}, u32[]{:S(2)}) collective-permute-start(bf16[768,128]{1,0:T(8,128)(2,1)S(1)} %get-tuple-element.45), channel_id=1, source_target_pairs={{0,6},{1,7},{2,4},{3,5},{4,2},{5,3},{6,0},{7,1},{8,14},{9,15},{10,... | collective-permute-start | bytes 589832 | tf_op jit(solution)/shard_map/ppermute | solution.py:22
  63.8 5.9 %collective-permute-start.24 = (bf16[2,512,128]{2,1,0:T(8,128)(2,1)S(1)}, bf16[2,512,128]{2,1,0:T(8,128)(2,1)S(1)}, u32[]{:S(2)}, u32[]{:S(2)}) collective-permute-start(bf16[2,512,128]{2,1,0:T(8,128)(2,1)S(1)} %copy-done.7), channel_id=1, source_target_pairs={{0,1},{1,0},{2,3},{3,2},{4,5},{5,4},{6,7},{7,6},{8,9},{9,8},{10,11... | collective-permute-start | bytes 786440 | tf_op jit(solution)/shard_map/ppermute | solution.py:22
  63.8 5.9 %collective-permute-start.22 = (bf16[512,128]{1,0:T(8,128)(2,1)S(1)}, bf16[512,128]{1,0:T(8,128)(2,1)S(1)}, u32[]{:S(2)}, u32[]{:S(2)}) collective-permute-start(bf16[512,128]{1,0:T(8,128)(2,1)S(1)} %constant_dynamic-slice_fusion.refs_6_.refs_4_.w0), channel_id=1, source_target_pairs={{0,1},{1,0},{2,3},{3,2},{4,5},{5,4},{6,7},{7,6},{8,9},{9,8},{10,11... | collective-permute-start | bytes 393224 | tf_op jit(solution)/shard_map/ppermute | solution.py:22
  64.3 5.4 %collective-permute-start.23 = (bf16[512,128]{1,0:T(8,128)(2,1)S(1)}, bf16[512,128]{1,0:T(8,128)(2,1)S(1)}, u32[]{:S(2)}, u32[]{:S(2)}) collective-permute-start(bf16[512,128]{1,0:T(8,128)(2,1)S(1)} %copy-done.10), channel_id=1, source_target_pairs={{0,1},{1,0},{2,3},{3,2},{4,5},{5,4},{6,7},{7,6},{8,9},{9,8},{10,11... | collective-permute-start | bytes 393224 | tf_op jit(solution)/shard_map/ppermute | solution.py:22
  71.8 19.9 %collective-permute-start.25 = (bf16[2,128,1024]{2,1,0:T(8,128)(2,1)S(1)}, bf16[2,128,1024]{2,1,0:T(8,128)(2,1)S(1)}, u32[]{:S(2)}, u32[]{:S(2)}) collective-permute-start(bf16[2,128,1024]{2,1,0:T(8,128)(2,1)S(1)} %get-tuple-element.49), channel_id=1, source_target_pairs={{0,2},{1,3},{2,0},{3,1},{4,6},{5,7},{6,4},{7,5},{8,10},{9,11},{10,... | collective-permute-start | bytes 1572872 | tf_op jit(solution)/shard_map/ppermute | solution.py:22
  73.8 18.5 %collective-permute-start.26 = (bf16[2,128,1024]{2,1,0:T(8,128)(2,1)S(1)}, bf16[2,128,1024]{2,1,0:T(8,128)(2,1)S(1)}, u32[]{:S(2)}, u32[]{:S(2)}) collective-permute-start(bf16[2,128,1024]{2,1,0:T(8,128)(2,1)S(1)} %get-tuple-element.51), channel_id=1, source_target_pairs={{0,4},{1,5},{2,6},{3,7},{4,0},{5,1},{6,2},{7,3},{8,12},{9,13},{10,... | collective-permute-start | bytes 1572872 | tf_op jit(solution)/shard_map/ppermute | solution.py:22
  75.2 7.8 %collective-permute-start.29 = (bf16[2,512,128]{2,1,0:T(8,128)(2,1)S(1)}, bf16[2,512,128]{2,1,0:T(8,128)(2,1)S(1)}, u32[]{:S(2)}, u32[]{:S(2)}) collective-permute-start(bf16[2,512,128]{2,1,0:T(8,128)(2,1)S(1)} %get-tuple-element.57), channel_id=1, source_target_pairs={{0,8},{8,0},{16,24},{24,16},{1,9},{9,1},{17,25},{25,17},{2,10},{10... | collective-permute-start | bytes 786440 | tf_op jit(solution)/shard_map/ppermute | solution.py:22
  76.8 18.0 %collective-permute-start.17 = (bf16[2,128,512]{2,1,0:T(8,128)(2,1)S(1)}, bf16[2,128,512]{2,1,0:T(8,128)(2,1)S(1)}, u32[]{:S(2)}, u32[]{:S(2)}) collective-permute-start(bf16[2,128,512]{2,1,0:T(8,128)(2,1)S(1)} %get-tuple-element.39), channel_id=1, source_target_pairs={{0,1},{1,0},{2,3},{3,2},{4,5},{5,4},{6,7},{7,6},{8,9},{9,8},{10,11... | collective-permute-start | bytes 786440 | tf_op jit(solution)/shard_map/ppermute | solution.py:22
  76.8 18.1 %collective-permute-start.16 = (bf16[2,128,512]{2,1,0:T(8,128)(2,1)S(1)}, bf16[2,128,512]{2,1,0:T(8,128)(2,1)S(1)}, u32[]{:S(2)}, u32[]{:S(2)}) collective-permute-start(bf16[2,128,512]{2,1,0:T(8,128)(2,1)S(1)} %get-tuple-element.38), channel_id=1, source_target_pairs={{0,1},{1,0},{2,3},{3,2},{4,5},{5,4},{6,7},{7,6},{8,9},{9,8},{10,11... | collective-permute-start | bytes 786440 | tf_op jit(solution)/shard_map/ppermute | solution.py:22
  83.1 7.9 %collective-permute-start.30 = (bf16[512,128]{1,0:T(8,128)(2,1)S(1)}, bf16[512,128]{1,0:T(8,128)(2,1)S(1)}, u32[]{:S(2)}, u32[]{:S(2)}) collective-permute-start(bf16[512,128]{1,0:T(8,128)(2,1)S(1)} %get-tuple-element.59), channel_id=1, source_target_pairs={{0,16},{8,24},{16,0},{24,8},{1,17},{9,25},{17,1},{25,9},{2,18},{10... | collective-permute-start | bytes 393224 | tf_op jit(solution)/shard_map/ppermute | solution.py:22
  91.6 7.3 %collective-permute-start.32 = (bf16[512,128]{1,0:T(8,128)(2,1)S(1)}, bf16[512,128]{1,0:T(8,128)(2,1)S(1)}, u32[]{:S(2)}, u32[]{:S(2)}) collective-permute-start(bf16[512,128]{1,0:T(8,128)(2,1)S(1)} %shard_map.95.refs_0_), channel_id=1, source_target_pairs={{0,4},{1,5},{2,6},{3,7},{4,0},{5,1},{6,2},{7,3},{8,12},{9,13},{10,... | collective-permute-start | bytes 393224 | tf_op jit(solution)/shard_map/ppermute | solution.py:22
  92.3 6.6 %collective-permute-start.33 = (bf16[512,128]{1,0:T(8,128)(2,1)S(1)}, bf16[512,128]{1,0:T(8,128)(2,1)S(1)}, u32[]{:S(2)}, u32[]{:S(2)}) collective-permute-start(bf16[512,128]{1,0:T(8,128)(2,1)S(1)} %shard_map.95.refs_0_), channel_id=1, source_target_pairs={{0,6},{1,7},{2,4},{3,5},{4,2},{5,3},{6,0},{7,1},{8,14},{9,15},{10,... | collective-permute-start | bytes 393224 | tf_op jit(solution)/shard_map/ppermute | solution.py:22
  94.8 9.5 %collective-permute-start.27 = (bf16[128,1024]{1,0:T(8,128)(2,1)S(1)}, bf16[128,1024]{1,0:T(8,128)(2,1)S(1)}, u32[]{:S(2)}, u32[]{:S(2)}) collective-permute-start(bf16[128,1024]{1,0:T(8,128)(2,1)S(1)} %get-tuple-element.53), channel_id=1, source_target_pairs={{0,4},{1,5},{2,6},{3,7},{4,0},{5,1},{6,2},{7,3},{8,12},{9,13},{10,... | collective-permute-start | bytes 786440 | tf_op jit(solution)/shard_map/ppermute | solution.py:22
  96.0 8.3 %collective-permute-start.28 = (bf16[128,1024]{1,0:T(8,128)(2,1)S(1)}, bf16[128,1024]{1,0:T(8,128)(2,1)S(1)}, u32[]{:S(2)}, u32[]{:S(2)}) collective-permute-start(bf16[128,1024]{1,0:T(8,128)(2,1)S(1)} %get-tuple-element.55), channel_id=1, source_target_pairs={{0,2},{1,3},{2,0},{3,1},{4,6},{5,7},{6,4},{7,5},{8,10},{9,11},{10,... | collective-permute-start | bytes 786440 | tf_op jit(solution)/shard_map/ppermute | solution.py:22
  (18 other events, 159.1 us)

commit v3 on v2

--- a/solution.py
+++ b/solution.py
@@ -30,7 +30,7 @@
     return pltpu.VMEM(shape, dtype)
 
 
-def run(body, outs, scalars, arrays, scratch=(), room=16):
+def run(body, outs, scalars, arrays, scratch=(), room=16, flops=0, exps=0):
     arrays = [pltpu.with_memory_space_constraint(v, pltpu.VMEM) for v in arrays]
     return pl.pallas_call(
         body,
@@ -42,6 +42,8 @@
         ),
         scratch_shapes=scratch,
         compiler_params=pltpu.CompilerParams(vmem_limit_bytes=room << 20),
+        cost_estimate=pl.CostEstimate(flops=flops, transcendentals=exps, bytes_accessed=4 << 20),
+        name=getattr(body, "func", body).__name__,
     )(*scalars, *arrays)
 
 
@@ -67,15 +69,42 @@
     return total.astype(BF16)
 
 
+def prep_kernel(ids, block, weight, x, w, x0):
+    w[...] = weight[...]
+    x0[...] = x[...]
+
+
+def prepare(ids, block, weight, x):
+    size = weight.shape[0]
+    whole = pl.BlockSpec(x.shape, lambda i, ids, block: (0, 0))
+    return pl.pallas_call(
+        prep_kernel,
+        out_shape=(on_chip((size, HEAD_DIM)), on_chip(x.shape)),
+        grid_spec=pltpu.PrefetchScalarGridSpec(
+            num_scalar_prefetch=2,
+            grid=(1,),
+            in_specs=[pl.BlockSpec((size, HEAD_DIM), lambda i, ids, block: (0, block[0])), whole],
+            out_specs=[pl.BlockSpec(memory_space=pltpu.VMEM)] * 2,
+        ),
+        compiler_params=pltpu.CompilerParams(vmem_limit_bytes=16 << 20),
+        name="prep_kernel",
+    )(ids, block, *[pltpu.with_memory_space_constraint(v, pltpu.HBM) for v in (weight, x)])
+
+
+def cut_kernel(x1, x2, top, low):
+    half = top.shape[0]
+    top[...] = x1[:half, :]
+    low[...] = x2[half:, :]
+
+
 def project_kernel(ids, *refs):
-    *xs, w0, w2, w13, out = refs
-    ws = (w0[...], w13[0], w2[...], w13[1])
-    out[...] = project_rows(ids[2], xs, ws)
+    *xs, w0, w1, w2, w3, out = refs
+    out[...] = project_rows(ids[2], xs, (w0[...], w1[...], w2[...], w3[...]))
 
 
 def window_kernel(ids, *refs):
-    *xs, w0, w2, w13, first, o0, o1, o2, o3, kv = refs
-    ws = (w0[...], w13[0], w2[...], w13[1])
+    *xs, w0, w1, w2, w3, first, o0, o1, o2, o3, kv = refs
+    ws = (w0[...], w1[...], w2[...], w3[...])
     m = ids[0]
     rows = first.shape[0] // 3
     for r in range(3):
@@ -167,6 +196,8 @@
         (first, second, *rest),
         scratch=[pltpu.VMEM((keys, 2 * rows), F32)],
         room=24,
+        flops=12 * keys * 2 * rows * HEADS // KV_HEADS * HEAD_DIM,
+        exps=keys * 2 * rows * HEADS // KV_HEADS,
     )
 
 
@@ -190,7 +221,7 @@
 
 
 def sum_kernel(ids, *refs):
-    d0, d1, d2, d3, *xs, own, oth, g_t, send, acc = refs
+    d0, d1, d2, d3, *xs, own, oth, g_t, send1, send2, send3, acc = refs
     m, z = ids[0], ids[2]
     rows = own.shape[1]
     acc[...] = jnp.zeros_like(acc)
@@ -204,14 +235,13 @@
         own[r] = g[:rows]
         oth[r] = g[rows:]
         g_t[:, r * 2 * rows : (r + 1) * 2 * rows] = g.T
-    for i, r in enumerate((1, 3)):
-        send[i] = weight_block(z, r, g_t[...], xs, send.shape[1]).astype(BF16)
+    for r, send in ((3, send3), (2, send2), (1, send1)):
+        send[...] = weight_block(z, r, g_t[...], xs, send.shape[0]).astype(BF16)
 
 
 def keep_kernel(ids, g_t, *refs):
     *xs, keep = refs
-    for i, r in enumerate((0, 2)):
-        keep[i] = weight_block(ids[2], r, g_t[...], xs, keep.shape[1])
+    keep[...] = weight_block(ids[2], 0, g_t[...], xs, keep.shape[0])
 
 
 def fold_kernel(keep, got, now, later):
@@ -219,8 +249,9 @@
     later[...] = (keep[1] + got[1].astype(F32)).astype(BF16)
 
 
-def last_kernel(now, got, out):
-    out[...] = (now[...] + got[...].astype(F32)).astype(BF16)
+def last_kernel(keep, got1, got2, got3, out):
+    got = (got1[...].astype(F32) + got2[...].astype(F32)) + got3[...].astype(F32)
+    out[...] = (keep[...] + got).astype(BF16)
 
 
 def assemble_kernel(ids, *refs):
@@ -233,13 +264,13 @@
             out[:, pl.ds(col, HEAD_DIM)] = refs[4 * side + r][...].astype(F32)
 
 
-def token_kernel(own, oth, w0, w2, w13, u0, u2, u13, send_a, send_b, keep_a, keep_b):
+def token_kernel(own, oth, w0, w1, w2, w3, u0, u1, u2, u3, send_a, send_b, keep_a, keep_b):
     rows = own.shape[1]
     g = jnp.concatenate(
         [jnp.concatenate([own[r] for r in range(4)], axis=0),
          jnp.concatenate([oth[r] for r in range(4)], axis=0)], axis=1)
-    ws = (w0[...], w13[0], w2[...], w13[1])
-    us = (u0[...], u13[0], u2[...], u13[1])
+    ws = (w0[...], w1[...], w2[...], w3[...])
+    us = (u0[...], u1[...], u2[...], u3[...])
     size = w0.shape[0]
     for i in range(4):
         w = jnp.concatenate([ws[i], us[i]], axis=1)
@@ -276,20 +307,25 @@
     cross = lambda v: swap(v, "bal", 6)
 
     x1, x2 = near(tokens), far(tokens)
-    w0 = lax.dynamic_slice(kv_weight, (0, column_of(m, c)), (size, HEAD_DIM))
-    w2 = swap(w0, "fsdp", 2)
-    w13 = swap(jnp.stack([w0, w2]), "fsdp", 1)
-    ws = (w0, w2, w13)
-    x3 = (far(x1[: rows // 2]), near(x2[rows // 2 :]))
-    y0, y1, y2 = pair(tokens), pair(x1), pair(x2)
-    y3 = (pair(x3[0]), pair(x3[1]))
-    early = (tokens, y0, x1, y1, x2, y2)
-    late = (*x3, *y3)
+    block = (column_of(m, c) // HEAD_DIM).astype(jnp.int32).reshape(1)
+    w0, x0 = prepare(ids, block, kv_weight, tokens)
+    w2, w1 = swap(w0, "fsdp", 2), swap(w0, "fsdp", 1)
+    x1, x2, w1, w2 = lax.optimization_barrier((x1, x2, w1, w2))
+    w3 = swap(w2, "fsdp", 1)
+    ws = (w0, w1, w2, w3)
+    half = on_chip((rows // 2, width))
+    top, low = run(cut_kernel, (half, half), (), (x1, x2))
+    x3 = [far(top), near(low)]
+    flip = lambda vs: [pair(v) for v in vs]
+    early = (x0, pair(x0), x1, pair(x1), x2, pair(x2))
+    first = run(project_kernel, on_chip((6 * rows, HEAD_DIM)), (ids,), early + ws)
+    *x3, first = lax.optimization_barrier((*x3, first))
+    late = (*x3, *flip(x3))
     xs = early + late
 
     rest = (queries, pair(queries), out_grad, pair(out_grad))
-
-    first = run(project_kernel, on_chip((6 * rows, HEAD_DIM)), (ids,), early + ws)
+    us = tuple(flip(ws))
+
     win = run(
         window_kernel,
         (on_chip((6 * rows, HEAD_DIM)),) * 4,
@@ -297,25 +333,32 @@
         late + ws + (first,),
         scratch=[pltpu.VMEM((4, 2 * rows, HEAD_DIM), BF16)],
     )
-    win3, win1, win2 = cross(win[3]), near(win[1]), far(win[2])
+    win3, win1, win2 = lax.optimization_barrier((cross(win[3]), win[1], win[2]))
+    win1, win2 = near(win1), far(win2)
 
     own_a, oth_a, d0, d3 = attend(0, ids, doc_lengths, win[0], win3, rest)
     d3 = cross(d3)
+    got_a = pair(oth_a)
+    win1, win2, d0 = lax.optimization_barrier((win1, win2, d0))
     own_b, oth_b, d1, d2 = attend(1, ids, doc_lengths, win1, win2, rest)
+    d1, d2, d3, got_a, us = lax.optimization_barrier((d1, d2, d3, got_a, us))
     d1, d2 = near(d1), far(d2)
+    got_b = pair(oth_b)
+    like = jax.ShapeDtypeStruct(queries.shape, BF16)
+    attn_out, grad_queries = run(place_kernel, (like, like), (ids,), (own_a, own_b, got_a, got_b))
 
     block = on_chip((4, rows, HEAD_DIM))
-    g_own, g_oth, g_t, send = run(
+    third = on_chip((size, HEAD_DIM))
+    g_own, g_oth, g_t, *sends = run(
         sum_kernel,
-        (block, block, on_chip((HEAD_DIM, 8 * rows)), on_chip((2, size, HEAD_DIM))),
+        (block, block, on_chip((HEAD_DIM, 8 * rows)), third, third, third),
         (ids,),
         (d0, d1, d2, d3) + xs,
         scratch=[pltpu.VMEM((12 * rows, HEAD_DIM), F32)],
     )
-    got = swap(send, "fsdp", 1)
+    gots = [swap(v, "fsdp", bit) for v, bit in zip(sends, (1, 2, 3))]
     g_oth = pair(g_oth)
-    keep = run(keep_kernel, on_chip((2, size, HEAD_DIM), F32), (ids,), (g_t,) + xs)
-    us = tuple(pair(v) for v in ws)
+    g_t, g_oth = lax.optimization_barrier((g_t, g_oth))
     half = (rows, width // 2)
     send_a, send_b, keep_a, keep_b = run(
         token_kernel,
@@ -324,13 +367,12 @@
         (g_own, g_oth) + ws + us,
     )
     got_a, got_b = near(send_a), far(send_b)
-    fold = (on_chip((size, HEAD_DIM), F32), on_chip((size, HEAD_DIM)))
-    now, later = run(fold_kernel, fold, (), (keep, got))
-    got = swap(later, "fsdp", 2)
+    keep = run(keep_kernel, on_chip((size, HEAD_DIM), F32), (ids,), (g_t,) + xs)
+    *gots, attn_out, grad_queries = lax.optimization_barrier((*gots, attn_out, grad_queries))
+    mine = run(last_kernel, on_chip((size, HEAD_DIM)), (), (keep, *gots))
     fold = (on_chip(half, F32), on_chip(half))
     a, a_send, b, b_send = run(fold_both_kernel, fold + fold, (), (keep_a, got_a, keep_b, got_b))
     got_a, got_b = far(a_send), near(b_send)
-    mine = run(last_kernel, on_chip((size, HEAD_DIM)), (), (now, got))
     mine = [mine, near(mine), far(mine), cross(mine)]
     theirs = [pair(v) for v in mine]
     grad_weight = run(
@@ -341,10 +383,6 @@
     )
     grad_tokens = run(
         token_last_kernel, jax.ShapeDtypeStruct(tokens.shape, BF16), (ids,), (a, got_a, b, got_b)
-    )
-    like = jax.ShapeDtypeStruct(queries.shape, BF16)
-    attn_out, grad_queries = run(
-        place_kernel, (like, like), (ids,), (own_a, own_b, pair(oth_a), pair(oth_b))
     )
     return attn_out, grad_queries, grad_tokens, grad_weight
 

time: 106 us -> 98.3 us (0.927)
  local copies, waits for them, and re-layouts: 4.53 us -> 0.01 us
  Pallas kernels: 27.3 us -> 24.6 us
  waiting for transfers between devices: 40.1 us -> 37.9 us
  starting transfers between devices: 32.9 us -> 34.8 us
    unnamed x24 -> x6, local copies, waits for them, and re-layouts: 4.42 us -> 0.01 us
    pallas_call x13, Pallas kernels: 27.3 us -> 22.9 us  [run(): pl.pallas_call(body, out_shape=outs, in_specs=[pl.BlockSpec(memory_space=...]
    ppermute x38 -> x41, waiting for transfers between devices: 40.1 us -> 37.9 us  [swap(): return lax.ppermute(value, axis, [(i, i ^ bit) for i in range(count)])]
    ppermute x38 -> x41, starting transfers between devices: 32.9 us -> 34.8 us  [swap(): return lax.ppermute(value, axis, [(i, i ^ bit) for i in range(count)])]
    pallas_call x0 -> x1, Pallas kernels: none -> 1.7 us  [prepare(): pl.pallas_call(prep_kernel, out_shape=(on_chip((size, HEAD_DIM)), on_chip...]
  transfers between devices with their start and end apart: 38 -> 41, of which waited for: 15 -> 17; matrix products, arithmetic and copies ran while one was open for 0% -> 0% of each run, Pallas kernels for 24% -> 22%
where the time goes in v3:
time: 98.3 us; the launch traced here: 98.2 us
  waiting for transfers between devices  37.9 us (39%)
  starting transfers between devices  34.8 us (35%)
  Pallas kernels  24.6 us (25%)
    ppermute x41, waiting for transfers between devices, swap(): return lax.ppermute(value, axis, [(i, i ^ bit) for i in range(count)])  37.9 us
    ppermute x41, starting transfers between devices, swap(): return lax.ppermute(value, axis, [(i, i ^ bit) for i in range(count)])  34.8 us
    pallas_call x13, Pallas kernels, run(): pl.pallas_call(body, out_shape=outs, in_specs=[pl.BlockSpec(memory_space=...  22.9 us
  transfers between devices with their start and end apart: 41, of which 17 were waited for; matrix products, arithmetic and copies ran while one was open for 0% of the time, Pallas kernels for 22%

profile of v3, /device:TPU:0, one launch (start us, length us, event | category | flops | bytes accessed | tf_op | source)
XLA Modules:
  0.0 98.2 jit_solution(18084411120842844396)
XLA Ops:
  0.7 3.0 %collective-permute-start = (bf16[128,2048]{1,0:T(8,128)(2,1)}, bf16[128,2048]{1,0:T(8,128)(2,1)S(1)}, u32[]{:S(2)}, u32[]{:S(2)}) collective-permute-start(bf16[128,2048]{1,0:T(8,128)(2,1)} %x.1), channel_id=1, source_target_pairs={{0,2},{1,3},{2,0},{3,1},{4,6},{5,7},{6,4},{7,5},{8,10},{9,11},{10,... | collective-permute-start | bytes 1572872 | tf_op jit(solution)/shard_map/ppermute | solution.py:22
  3.7 1.5 %collective-permute-start.1 = (bf16[128,2048]{1,0:T(8,128)(2,1)}, bf16[128,2048]{1,0:T(8,128)(2,1)S(1)}, u32[]{:S(2)}, u32[]{:S(2)}) collective-permute-start(bf16[128,2048]{1,0:T(8,128)(2,1)} %x.1), channel_id=1, source_target_pairs={{0,4},{1,5},{2,6},{3,7},{4,0},{5,1},{6,2},{7,3},{8,12},{9,13},{10,... | collective-permute-start | bytes 1572872 | tf_op jit(solution)/shard_map/ppermute | solution.py:22
  5.3 1.7 %prep_kernel.1 = (bf16[512,128]{1,0:T(8,128)(2,1)S(1)}, bf16[128,2048]{1,0:T(8,128)(2,1)S(1)}) custom-call(s32[3]{0:T(128)S(1)} %pad_add_fusion.ids, s32[1]{0:T(128)} %bitcast.3.block, bf16[512,1024]{1,0:T(8,128)(2,1)} %weight.1, bf16[128,2048]{1,0:T(8,128)(2,1)} %x.1), custom_call_target="tpu_custom_call" | custom-call | tf_op jit(solution)/shard_map/prep_kernel/pallas_call | solution.py:80
  7.0 1.6 %collective-permute-start.2 = (bf16[512,128]{1,0:T(8,128)(2,1)S(1)}, bf16[512,128]{1,0:T(8,128)(2,1)S(1)}, u32[]{:S(2)}, u32[]{:S(2)}) collective-permute-start(bf16[512,128]{1,0:T(8,128)(2,1)S(1)} %get-tuple-element.64.refs_6_.refs_4_.w0), channel_id=1, source_target_pairs={{0,8},{8,0},{16,24},{24,16},{1,9},{9,1},{17,25},{25,17},{2,10},{10... | collective-permute-start | bytes 393224 | tf_op jit(solution)/shard_map/ppermute | solution.py:22
  8.6 2.6 %collective-permute-start.3 = (bf16[512,128]{1,0:T(8,128)(2,1)S(1)}, bf16[512,128]{1,0:T(8,128)(2,1)S(1)}, u32[]{:S(2)}, u32[]{:S(2)}) collective-permute-start(bf16[512,128]{1,0:T(8,128)(2,1)S(1)} %get-tuple-element.64.refs_6_.refs_4_.w0), channel_id=1, source_target_pairs={{0,16},{8,24},{16,0},{24,8},{1,17},{9,25},{17,1},{25,9},{2,18},{10... | collective-permute-start | bytes 393224 | tf_op jit(solution)/shard_map/ppermute | solution.py:22
  11.2 2.5 %collective-permute-done.2.refs_7_.refs_5_.w1 = bf16[512,128]{1,0:T(8,128)(2,1)S(1)} collective-permute-done((bf16[512,128]{1,0:T(8,128)(2,1)S(1)}, bf16[512,128]{1,0:T(8,128)(2,1)S(1)}, u32[]{:S(2)}, u32[]{:S(2)}) %collective-permute-start.2) | collective-permute-done | bytes 131104 | tf_op jit(solution)/shard_map/ppermute | solution.py:22
  13.7 3.0 %collective-permute-done.3.refs_8_.refs_6_.w2 = bf16[512,128]{1,0:T(8,128)(2,1)S(1)} collective-permute-done((bf16[512,128]{1,0:T(8,128)(2,1)S(1)}, bf16[512,128]{1,0:T(8,128)(2,1)S(1)}, u32[]{:S(2)}, u32[]{:S(2)}) %collective-permute-start.3) | collective-permute-done | bytes 131104 | tf_op jit(solution)/shard_map/ppermute | solution.py:22
  17.8 1.6 %collective-permute-start.4 = (bf16[64,2048]{1,0:T(8,128)(2,1)S(1)}, bf16[64,2048]{1,0:T(8,128)(2,1)S(1)}, u32[]{:S(2)}, u32[]{:S(2)}) collective-permute-start(bf16[64,2048]{1,0:T(8,128)(2,1)S(1)} %get-tuple-element.67), channel_id=1, source_target_pairs={{0,4},{1,5},{2,6},{3,7},{4,0},{5,1},{6,2},{7,3},{8,12},{9,13},{10,... | collective-permute-start | bytes 786440 | tf_op jit(solution)/shard_map/ppermute | solution.py:22
  20.0 1.6 %collective-permute-start.9 = (bf16[512,128]{1,0:T(8,128)(2,1)S(1)}, bf16[512,128]{1,0:T(8,128)(2,1)S(1)}, u32[]{:S(2)}, u32[]{:S(2)}) collective-permute-start(bf16[512,128]{1,0:T(8,128)(2,1)S(1)} %collective-permute-done.3.refs_8_.refs_6_.w2), channel_id=1, source_target_pairs={{0,8},{8,0},{16,24},{24,16},{1,9},{9,1},{17,25},{25,17},{2,10},{10... | collective-permute-start | bytes 393224 | tf_op jit(solution)/shard_map/ppermute | solution.py:22
  21.5 3.4 %collective-permute-done.9.refs_9_.refs_7_.w3 = bf16[512,128]{1,0:T(8,128)(2,1)S(1)} collective-permute-done((bf16[512,128]{1,0:T(8,128)(2,1)S(1)}, bf16[512,128]{1,0:T(8,128)(2,1)S(1)}, u32[]{:S(2)}, u32[]{:S(2)}) %collective-permute-start.9) | collective-permute-done | bytes 131104 | tf_op jit(solution)/shard_map/ppermute | solution.py:22
  25.4 1.5 %project_kernel.1.refs_8_ = bf16[768,128]{1,0:T(8,128)(2,1)S(1)} custom-call(s32[3]{0:T(128)S(1)} %pad_add_fusion.ids, bf16[128,2048]{1,0:T(8,128)(2,1)S(1)} %get-tuple-element.69.refs_0_.refs_4_, bf16[128,2048]{1,0:T(8,128)(2,1)S(1)} %collective-permute-done.6.refs_1_.refs_5_, bf16[128,2048]{1,0:T(8,128)(2,1)S(1)} %collective-permute-done.x1.refs_2_.refs_6_, ...), custom_call_target="tpu_custom_call" | custom-call | bytes 4194304 | tf_op jit(solution)/shard_map/project_kernel/pallas_call | solution.py:35
  29.3 1.1 %window_kernel.1 = (bf16[768,128]{1,0:T(8,128)(2,1)S(1)}, bf16[768,128]{1,0:T(8,128)(2,1)S(1)}, bf16[768,128]{1,0:T(8,128)(2,1)S(1)}, bf16[768,128]{1,0:T(8,128)(2,1)S(1)}) custom-call(s32[3]{0:T(128)S(1)} %pad_add_fusion.ids, bf16[64,2048]{1,0:T(8,128)(2,1)S(1)} %collective-permute-done.4.refs_0_.refs_10_.refs_6_, ...), custom_call_target="tpu_custom_call" | custom-call | bytes 4194304 | tf_op jit(solution)/shard_map/window_kernel/pallas_call | solution.py:35
  30.4 1.2 %collective-permute-start.12 = (bf16[768,128]{1,0:T(8,128)(2,1)S(1)}, bf16[768,128]{1,0:T(8,128)(2,1)S(1)}, u32[]{:S(2)}, u32[]{:S(2)}) collective-permute-start(bf16[768,128]{1,0:T(8,128)(2,1)S(1)} %get-tuple-element.75), channel_id=1, source_target_pairs={{0,6},{1,7},{2,4},{3,5},{4,2},{5,3},{6,0},{7,1},{8,14},{9,15},{10,... | collective-permute-start | bytes 589832 | tf_op jit(solution)/shard_map/ppermute | solution.py:22
  31.6 6.7 %collective-permute-done.12.second = bf16[768,128]{1,0:T(8,128)(2,1)S(1)} collective-permute-done((bf16[768,128]{1,0:T(8,128)(2,1)S(1)}, bf16[768,128]{1,0:T(8,128)(2,1)S(1)}, u32[]{:S(2)}, u32[]{:S(2)}) %collective-permute-start.12) | collective-permute-done | bytes 196640 | tf_op jit(solution)/shard_map/ppermute | solution.py:22
  38.3 1.2 %collective-permute-start.13 = (bf16[768,128]{1,0:T(8,128)(2,1)S(1)}, bf16[768,128]{1,0:T(8,128)(2,1)S(1)}, u32[]{:S(2)}, u32[]{:S(2)}) collective-permute-start(bf16[768,128]{1,0:T(8,128)(2,1)S(1)} %get-tuple-element.78), channel_id=1, source_target_pairs={{0,2},{1,3},{2,0},{3,1},{4,6},{5,7},{6,4},{7,5},{8,10},{9,11},{10,... | collective-permute-start | bytes 589832 | tf_op jit(solution)/shard_map/ppermute | solution.py:22
  40.0 5.7 %attend_kernel.2 = (bf16[2,128,512]{2,1,0:T(8,128)(2,1)S(1)}, bf16[2,128,512]{2,1,0:T(8,128)(2,1)S(1)}, bf16[768,128]{1,0:T(8,128)(2,1)S(1)}, bf16[768,128]{1,0:T(8,128)(2,1)S(1)}) custom-call(s32[3]{0:T(128)S(1)} %pad_add_fusion.ids, s32[1,4]{1,0:T(1,128)S(1)} %copy-done.2, bf16[768,128]{1,0:T(8,128)(2,1)S(1)} %get-tuple-element.80.first, ...), custom_call_target="tpu_custom_call" | custom-call | flops 1207959552 | bytes 4194304 | tf_op jit(solution)/shard_map/attend_kernel/pallas_call | solution.py:35
  45.9 1.9 %collective-permute-start.17 = (bf16[768,128]{1,0:T(8,128)(2,1)S(1)}, bf16[768,128]{1,0:T(8,128)(2,1)S(1)}, u32[]{:S(2)}, u32[]{:S(2)}) collective-permute-start(bf16[768,128]{1,0:T(8,128)(2,1)S(1)} %get-tuple-element.88), channel_id=1, source_target_pairs={{0,6},{1,7},{2,4},{3,5},{4,2},{5,3},{6,0},{7,1},{8,14},{9,15},{10,... | collective-permute-start | bytes 589832 | tf_op jit(solution)/shard_map/ppermute | solution.py:22
  48.4 5.9 %attend_kernel.3 = (bf16[2,128,512]{2,1,0:T(8,128)(2,1)S(1)}, bf16[2,128,512]{2,1,0:T(8,128)(2,1)S(1)}, bf16[768,128]{1,0:T(8,128)(2,1)S(1)}, bf16[768,128]{1,0:T(8,128)(2,1)S(1)}) custom-call(s32[3]{0:T(128)S(1)} %pad_add_fusion.ids, s32[1,4]{1,0:T(1,128)S(1)} %copy-done.2, bf16[768,128]{1,0:T(8,128)(2,1)S(1)} %collective-permute-done.13.first, ...), custom_call_target="tpu_custom_call" | custom-call | flops 1207959552 | bytes 4194304 | tf_op jit(solution)/shard_map/attend_kernel/pallas_call | solution.py:35
  54.4 1.3 %collective-permute-start.23 = (bf16[768,128]{1,0:T(8,128)(2,1)S(1)}, bf16[768,128]{1,0:T(8,128)(2,1)S(1)}, u32[]{:S(2)}, u32[]{:S(2)}) collective-permute-start(bf16[768,128]{1,0:T(8,128)(2,1)S(1)} %get-tuple-element.90), channel_id=1, source_target_pairs={{0,2},{1,3},{2,0},{3,1},{4,6},{5,7},{6,4},{7,5},{8,10},{9,11},{10,... | collective-permute-start | bytes 589832 | tf_op jit(solution)/shard_map/ppermute | solution.py:22
  56.4 5.2 %collective-permute-done.23.refs_1_ = bf16[768,128]{1,0:T(8,128)(2,1)S(1)} collective-permute-done((bf16[768,128]{1,0:T(8,128)(2,1)S(1)}, bf16[768,128]{1,0:T(8,128)(2,1)S(1)}, u32[]{:S(2)}, u32[]{:S(2)}) %collective-permute-start.23) | collective-permute-done | bytes 196640 | tf_op jit(solution)/shard_map/ppermute | solution.py:22
  62.5 1.4 %sum_kernel.1 = (bf16[4,128,128]{2,1,0:T(8,128)(2,1)S(1)}, bf16[4,128,128]{2,1,0:T(8,128)(2,1)S(1)}, bf16[128,1024]{1,0:T(8,128)(2,1)S(1)}, bf16[512,128]{1,0:T(...) custom-call(s32[3]{0:T(128)S(1)} %pad_add_fusion.ids, ...), custom_call_target="tpu_custom_call" | custom-call | bytes 4194304 | tf_op jit(solution)/shard_map/sum_kernel/pallas_call | solution.py:35
  67.5 1.6 %collective-permute-start.25 = (bf16[512,128]{1,0:T(8,128)(2,1)S(1)}, bf16[512,128]{1,0:T(8,128)(2,1)S(1)}, u32[]{:S(2)}, u32[]{:S(2)}) collective-permute-start(bf16[512,128]{1,0:T(8,128)(2,1)S(1)} %get-tuple-element.93), channel_id=1, source_target_pairs={{0,8},{8,0},{16,24},{24,16},{1,9},{9,1},{17,25},{25,17},{2,10},{10... | collective-permute-start | bytes 393224 | tf_op jit(solution)/shard_map/ppermute | solution.py:22
  69.1 2.6 %collective-permute-start.26 = (bf16[512,128]{1,0:T(8,128)(2,1)S(1)}, bf16[512,128]{1,0:T(8,128)(2,1)S(1)}, u32[]{:S(2)}, u32[]{:S(2)}) collective-permute-start(bf16[512,128]{1,0:T(8,128)(2,1)S(1)} %get-tuple-element.94), channel_id=1, source_target_pairs={{0,16},{8,24},{16,0},{24,8},{1,17},{9,25},{17,1},{25,9},{2,18},{10... | collective-permute-start | bytes 393224 | tf_op jit(solution)/shard_map/ppermute | solution.py:22
  71.9 1.6 %place_kernel.1 = (bf16[128,2048]{1,0:T(8,128)(2,1)}, bf16[128,2048]{1,0:T(8,128)(2,1)}) custom-call(s32[3]{0:T(128)S(1)} %pad_add_fusion.ids, bf16[2,128,512]{2,1,0:T(8,128)(2,1)S(1)} %get-tuple-element.96.own_a, bf16[2,128,512]{2,1,0:T(8,128)(2,1)S(1)} %get-tuple-element.97.own_b, bf16[2,128,512]{2,1,0:T(8,128)(2,1)S(1)} %collective-permute-done.18.got_a, ...), custom_call_target="tpu_custom_call" | custom-call | bytes 4194304 | tf_op jit(solution)/shard_map/place_kernel/pallas_call | solution.py:35
  74.0 7.7 %collective-permute-done.26.got2 = bf16[512,128]{1,0:T(8,128)(2,1)S(1)} collective-permute-done((bf16[512,128]{1,0:T(8,128)(2,1)S(1)}, bf16[512,128]{1,0:T(8,128)(2,1)S(1)}, u32[]{:S(2)}, u32[]{:S(2)}) %collective-permute-start.26) | collective-permute-done | bytes 131104 | tf_op jit(solution)/shard_map/ppermute | solution.py:22
  82.8 1.3 %collective-permute-start.34 = (bf16[512,128]{1,0:T(8,128)(2,1)S(1)}, bf16[512,128]{1,0:T(8,128)(2,1)S(1)}, u32[]{:S(2)}, u32[]{:S(2)}) collective-permute-start(bf16[512,128]{1,0:T(8,128)(2,1)S(1)} %last_kernel.1.refs_0_), channel_id=1, source_target_pairs={{0,2},{1,3},{2,0},{3,1},{4,6},{5,7},{6,4},{7,5},{8,10},{9,11},{10,... | collective-permute-start | bytes 393224 | tf_op jit(solution)/shard_map/ppermute | solution.py:22
  84.1 1.5 %collective-permute-start.35 = (bf16[512,128]{1,0:T(8,128)(2,1)S(1)}, bf16[512,128]{1,0:T(8,128)(2,1)S(1)}, u32[]{:S(2)}, u32[]{:S(2)}) collective-permute-start(bf16[512,128]{1,0:T(8,128)(2,1)S(1)} %last_kernel.1.refs_0_), channel_id=1, source_target_pairs={{0,4},{1,5},{2,6},{3,7},{4,0},{5,1},{6,2},{7,3},{8,12},{9,13},{10,... | collective-permute-start | bytes 393224 | tf_op jit(solution)/shard_map/ppermute | solution.py:22
  86.5 1.6 %collective-permute-start.32 = (bf16[128,1024]{1,0:T(8,128)(2,1)S(1)}, bf16[128,1024]{1,0:T(8,128)(2,1)S(1)}, u32[]{:S(2)}, u32[]{:S(2)}) collective-permute-start(bf16[128,1024]{1,0:T(8,128)(2,1)S(1)} %get-tuple-element.117), channel_id=1, source_target_pairs={{0,4},{1,5},{2,6},{3,7},{4,0},{5,1},{6,2},{7,3},{8,12},{9,13},{10,... | collective-permute-start | bytes 786440 | tf_op jit(solution)/shard_map/ppermute | solution.py:22
  88.1 1.2 %collective-permute-start.33 = (bf16[128,1024]{1,0:T(8,128)(2,1)S(1)}, bf16[128,1024]{1,0:T(8,128)(2,1)S(1)}, u32[]{:S(2)}, u32[]{:S(2)}) collective-permute-start(bf16[128,1024]{1,0:T(8,128)(2,1)S(1)} %get-tuple-element.119), channel_id=1, source_target_pairs={{0,2},{1,3},{2,0},{3,1},{4,6},{5,7},{6,4},{7,5},{8,10},{9,11},{10,... | collective-permute-start | bytes 786440 | tf_op jit(solution)/shard_map/ppermute | solution.py:22
  89.3 2.7 %collective-permute-done.36.refs_3_ = bf16[512,128]{1,0:T(8,128)(2,1)S(1)} collective-permute-done((bf16[512,128]{1,0:T(8,128)(2,1)S(1)}, bf16[512,128]{1,0:T(8,128)(2,1)S(1)}, u32[]{:S(2)}, u32[]{:S(2)}) %collective-permute-start.36) | collective-permute-done | bytes 131104 | tf_op jit(solution)/shard_map/ppermute | solution.py:22
  93.6 2.1 %assemble_kernel.1 = f32[512,1024]{1,0:T(8,128)} custom-call(s32[3]{0:T(128)S(1)} %pad_add_fusion.ids, bf16[512,128]{1,0:T(8,128)(2,1)S(1)} %last_kernel.1.refs_0_, bf16[512,128]{1,0:T(8,128)(2,1)S(1)} %collective-permute-done.34.refs_1_, bf16[512,128]{1,0:T(8,128)(2,1)S(1)} %collective-permute-done.35.refs_2_, ...), custom_call_target="tpu_custom_call" | custom-call | bytes 4194304 | tf_op jit(solution)/shard_map/assemble_kernel/pallas_call | solution.py:35
  96.7 1.4 %token_last_kernel.1 = bf16[128,2048]{1,0:T(8,128)(2,1)} custom-call(s32[3]{0:T(128)S(1)} %pad_add_fusion.ids, f32[128,1024]{1,0:T(8,128)S(1)} %get-tuple-element.116.a, bf16[128,1024]{1,0:T(8,128)(2,1)S(1)} %collective-permute-done.32.got_a, f32[128,1024]{1,0:T(8,128)S(1)} %get-tuple-element.118.b, bf16[128,1024]{1,0:T(8,128)(2,1)S(1)} %collective-permute-done.33.got_b), custom_call_target="tpu_custom_call" | custom-call | bytes 4194304 | tf_op jit(solution)/shard_map/token_last_kernel/pallas_call | solution.py:35
  (71 shorter events, 16.3 us)
Async XLA Ops:
  0.7 16.1 %collective-permute-start = (bf16[128,2048]{1,0:T(8,128)(2,1)}, bf16[128,2048]{1,0:T(8,128)(2,1)S(1)}, u32[]{:S(2)}, u32[]{:S(2)}) collective-permute-start(bf16[128,2048]{1,0:T(8,128)(2,1)} %x.1), channel_id=1, source_target_pairs={{0,2},{1,3},{2,0},{3,1},{4,6},{5,7},{6,4},{7,5},{8,10},{9,11},{10,... | collective-permute-start | bytes 1572872 | tf_op jit(solution)/shard_map/ppermute | solution.py:22
  3.7 13.6 %collective-permute-start.1 = (bf16[128,2048]{1,0:T(8,128)(2,1)}, bf16[128,2048]{1,0:T(8,128)(2,1)S(1)}, u32[]{:S(2)}, u32[]{:S(2)}) collective-permute-start(bf16[128,2048]{1,0:T(8,128)(2,1)} %x.1), channel_id=1, source_target_pairs={{0,4},{1,5},{2,6},{3,7},{4,0},{5,1},{6,2},{7,3},{8,12},{9,13},{10,... | collective-permute-start | bytes 1572872 | tf_op jit(solution)/shard_map/ppermute | solution.py:22
  7.0 6.8 %collective-permute-start.2 = (bf16[512,128]{1,0:T(8,128)(2,1)S(1)}, bf16[512,128]{1,0:T(8,128)(2,1)S(1)}, u32[]{:S(2)}, u32[]{:S(2)}) collective-permute-start(bf16[512,128]{1,0:T(8,128)(2,1)S(1)} %get-tuple-element.64.refs_6_.refs_4_.w0), channel_id=1, source_target_pairs={{0,8},{8,0},{16,24},{24,16},{1,9},{9,1},{17,25},{25,17},{2,10},{10... | collective-permute-start | bytes 393224 | tf_op jit(solution)/shard_map/ppermute | solution.py:22
  8.6 8.2 %collective-permute-start.3 = (bf16[512,128]{1,0:T(8,128)(2,1)S(1)}, bf16[512,128]{1,0:T(8,128)(2,1)S(1)}, u32[]{:S(2)}, u32[]{:S(2)}) collective-permute-start(bf16[512,128]{1,0:T(8,128)(2,1)S(1)} %get-tuple-element.64.refs_6_.refs_4_.w0), channel_id=1, source_target_pairs={{0,16},{8,24},{16,0},{24,8},{1,17},{9,25},{17,1},{25,9},{2,18},{10... | collective-permute-start | bytes 393224 | tf_op jit(solution)/shard_map/ppermute | solution.py:22
  11.2 8.7 %collective-permute-start.6 = (bf16[128,2048]{1,0:T(8,128)(2,1)S(1)}, bf16[128,2048]{1,0:T(8,128)(2,1)S(1)}, u32[]{:S(2)}, u32[]{:S(2)}) collective-permute-start(bf16[128,2048]{1,0:T(8,128)(2,1)S(1)} %get-tuple-element.69.refs_0_.refs_4_), channel_id=1, source_target_pairs={{0,1},{1,0},{2,3},{3,2},{4,5},{5,4},{6,7},{7,6},{8,9},{9,8},{10,11... | collective-permute-start | bytes 1572872 | tf_op jit(solution)/shard_map/ppermute | solution.py:22
  17.3 7.7 %collective-permute-start.7 = (bf16[128,2048]{1,0:T(8,128)(2,1)S(1)}, bf16[128,2048]{1,0:T(8,128)(2,1)S(1)}, u32[]{:S(2)}, u32[]{:S(2)}) collective-permute-start(bf16[128,2048]{1,0:T(8,128)(2,1)S(1)} %collective-permute-done.x1.refs_2_.refs_6_), channel_id=1, source_target_pairs={{0,1},{1,0},{2,3},{3,2},{4,5},{5,4},{6,7},{7,6},{8,9},{9,8},{10,11... | collective-permute-start | bytes 1572872 | tf_op jit(solution)/shard_map/ppermute | solution.py:22
  17.3 8.2 %collective-permute-start.8 = (bf16[128,2048]{1,0:T(8,128)(2,1)S(1)}, bf16[128,2048]{1,0:T(8,128)(2,1)S(1)}, u32[]{:S(2)}, u32[]{:S(2)}) collective-permute-start(bf16[128,2048]{1,0:T(8,128)(2,1)S(1)} %collective-permute-done.1.x2.refs_4_.refs_8_), channel_id=1, source_target_pairs={{0,1},{1,0},{2,3},{3,2},{4,5},{5,4},{6,7},{7,6},{8,9},{9,8},{10,11... | collective-permute-start | bytes 1572872 | tf_op jit(solution)/shard_map/ppermute | solution.py:22
  17.8 9.1 %collective-permute-start.4 = (bf16[64,2048]{1,0:T(8,128)(2,1)S(1)}, bf16[64,2048]{1,0:T(8,128)(2,1)S(1)}, u32[]{:S(2)}, u32[]{:S(2)}) collective-permute-start(bf16[64,2048]{1,0:T(8,128)(2,1)S(1)} %get-tuple-element.67), channel_id=1, source_target_pairs={{0,4},{1,5},{2,6},{3,7},{4,0},{5,1},{6,2},{7,3},{8,12},{9,13},{10,... | collective-permute-start | bytes 786440 | tf_op jit(solution)/shard_map/ppermute | solution.py:22
  19.4 7.9 %collective-permute-start.5 = (bf16[64,2048]{1,0:T(8,128)(2,1)S(1)}, bf16[64,2048]{1,0:T(8,128)(2,1)S(1)}, u32[]{:S(2)}, u32[]{:S(2)}) collective-permute-start(bf16[64,2048]{1,0:T(8,128)(2,1)S(1)} %get-tuple-element.68), channel_id=1, source_target_pairs={{0,2},{1,3},{2,0},{3,1},{4,6},{5,7},{6,4},{7,5},{8,10},{9,11},{10,... | collective-permute-start | bytes 786440 | tf_op jit(solution)/shard_map/ppermute | solution.py:22
  24.9 15.1 %collective-permute-start.15 = (bf16[128,2048]{1,0:T(8,128)(2,1)S(1)}, bf16[128,2048]{1,0:T(8,128)(2,1)S(1)}, u32[]{:S(2)}, u32[]{:S(2)}) collective-permute-start(bf16[128,2048]{1,0:T(8,128)(2,1)S(1)} %copy-done), channel_id=1, source_target_pairs={{0,1},{1,0},{2,3},{3,2},{4,5},{5,4},{6,7},{7,6},{8,9},{9,8},{10,11... | collective-permute-start | bytes 1572872 | tf_op jit(solution)/shard_map/ppermute | solution.py:22
  24.9 15.1 %collective-permute-start.16 = (bf16[128,2048]{1,0:T(8,128)(2,1)S(1)}, bf16[128,2048]{1,0:T(8,128)(2,1)S(1)}, u32[]{:S(2)}, u32[]{:S(2)}) collective-permute-start(bf16[128,2048]{1,0:T(8,128)(2,1)S(1)} %copy-done.1), channel_id=1, source_target_pairs={{0,1},{1,0},{2,3},{3,2},{4,5},{5,4},{6,7},{7,6},{8,9},{9,8},{10,11... | collective-permute-start | bytes 1572872 | tf_op jit(solution)/shard_map/ppermute | solution.py:22
  30.4 7.9 %collective-permute-start.12 = (bf16[768,128]{1,0:T(8,128)(2,1)S(1)}, bf16[768,128]{1,0:T(8,128)(2,1)S(1)}, u32[]{:S(2)}, u32[]{:S(2)}) collective-permute-start(bf16[768,128]{1,0:T(8,128)(2,1)S(1)} %get-tuple-element.75), channel_id=1, source_target_pairs={{0,6},{1,7},{2,4},{3,5},{4,2},{5,3},{6,0},{7,1},{8,14},{9,15},{10,... | collective-permute-start | bytes 589832 | tf_op jit(solution)/shard_map/ppermute | solution.py:22
  31.6 16.1 %collective-permute-start.19 = (bf16[512,128]{1,0:T(8,128)(2,1)S(1)}, bf16[512,128]{1,0:T(8,128)(2,1)S(1)}, u32[]{:S(2)}, u32[]{:S(2)}) collective-permute-start(bf16[512,128]{1,0:T(8,128)(2,1)S(1)} %get-tuple-element.64.refs_6_.refs_4_.w0), channel_id=1, source_target_pairs={{0,1},{1,0},{2,3},{3,2},{4,5},{5,4},{6,7},{7,6},{8,9},{9,8},{10,11... | collective-permute-start | bytes 393224 | tf_op jit(solution)/shard_map/ppermute | solution.py:22
  38.3 9.6 %collective-permute-start.13 = (bf16[768,128]{1,0:T(8,128)(2,1)S(1)}, bf16[768,128]{1,0:T(8,128)(2,1)S(1)}, u32[]{:S(2)}, u32[]{:S(2)}) collective-permute-start(bf16[768,128]{1,0:T(8,128)(2,1)S(1)} %get-tuple-element.78), channel_id=1, source_target_pairs={{0,2},{1,3},{2,0},{3,1},{4,6},{5,7},{6,4},{7,5},{8,10},{9,11},{10,... | collective-permute-start | bytes 589832 | tf_op jit(solution)/shard_map/ppermute | solution.py:22
  39.5 8.7 %collective-permute-start.14 = (bf16[768,128]{1,0:T(8,128)(2,1)S(1)}, bf16[768,128]{1,0:T(8,128)(2,1)S(1)}, u32[]{:S(2)}, u32[]{:S(2)}) collective-permute-start(bf16[768,128]{1,0:T(8,128)(2,1)S(1)} %get-tuple-element.79), channel_id=1, source_target_pairs={{0,4},{1,5},{2,6},{3,7},{4,0},{5,1},{6,2},{7,3},{8,12},{9,13},{10,... | collective-permute-start | bytes 589832 | tf_op jit(solution)/shard_map/ppermute | solution.py:22
  45.8 8.6 %collective-permute-start.18 = (bf16[2,128,512]{2,1,0:T(8,128)(2,1)S(1)}, bf16[2,128,512]{2,1,0:T(8,128)(2,1)S(1)}, u32[]{:S(2)}, u32[]{:S(2)}) collective-permute-start(bf16[2,128,512]{2,1,0:T(8,128)(2,1)S(1)} %get-tuple-element.89), channel_id=1, source_target_pairs={{0,1},{1,0},{2,3},{3,2},{4,5},{5,4},{6,7},{7,6},{8,9},{9,8},{10,11... | collective-permute-start | bytes 786440 | tf_op jit(solution)/shard_map/ppermute | solution.py:22
  45.9 8.5 %collective-permute-start.17 = (bf16[768,128]{1,0:T(8,128)(2,1)S(1)}, bf16[768,128]{1,0:T(8,128)(2,1)S(1)}, u32[]{:S(2)}, u32[]{:S(2)}) collective-permute-start(bf16[768,128]{1,0:T(8,128)(2,1)S(1)} %get-tuple-element.88), channel_id=1, source_target_pairs={{0,6},{1,7},{2,4},{3,5},{4,2},{5,3},{6,0},{7,1},{8,14},{9,15},{10,... | collective-permute-start | bytes 589832 | tf_op jit(solution)/shard_map/ppermute | solution.py:22
  47.7 6.6 %collective-permute-start.20 = (bf16[512,128]{1,0:T(8,128)(2,1)S(1)}, bf16[512,128]{1,0:T(8,128)(2,1)S(1)}, u32[]{:S(2)}, u32[]{:S(2)}) collective-permute-start(bf16[512,128]{1,0:T(8,128)(2,1)S(1)} %collective-permute-done.2.refs_7_.refs_5_.w1), channel_id=1, source_target_pairs={{0,1},{1,0},{2,3},{3,2},{4,5},{5,4},{6,7},{7,6},{8,9},{9,8},{10,11... | collective-permute-start | bytes 393224 | tf_op jit(solution)/shard_map/ppermute | solution.py:22
  47.9 6.5 %collective-permute-start.21 = (bf16[512,128]{1,0:T(8,128)(2,1)S(1)}, bf16[512,128]{1,0:T(8,128)(2,1)S(1)}, u32[]{:S(2)}, u32[]{:S(2)}) collective-permute-start(bf16[512,128]{1,0:T(8,128)(2,1)S(1)} %collective-permute-done.3.refs_8_.refs_6_.w2), channel_id=1, source_target_pairs={{0,1},{1,0},{2,3},{3,2},{4,5},{5,4},{6,7},{7,6},{8,9},{9,8},{10,11... | collective-permute-start | bytes 393224 | tf_op jit(solution)/shard_map/ppermute | solution.py:22
  48.2 6.1 %collective-permute-start.22 = (bf16[512,128]{1,0:T(8,128)(2,1)S(1)}, bf16[512,128]{1,0:T(8,128)(2,1)S(1)}, u32[]{:S(2)}, u32[]{:S(2)}) collective-permute-start(bf16[512,128]{1,0:T(8,128)(2,1)S(1)} %collective-permute-done.9.refs_9_.refs_7_.w3), channel_id=1, source_target_pairs={{0,1},{1,0},{2,3},{3,2},{4,5},{5,4},{6,7},{7,6},{8,9},{9,8},{10,11... | collective-permute-start | bytes 393224 | tf_op jit(solution)/shard_map/ppermute | solution.py:22
  54.4 7.2 %collective-permute-start.23 = (bf16[768,128]{1,0:T(8,128)(2,1)S(1)}, bf16[768,128]{1,0:T(8,128)(2,1)S(1)}, u32[]{:S(2)}, u32[]{:S(2)}) collective-permute-start(bf16[768,128]{1,0:T(8,128)(2,1)S(1)} %get-tuple-element.90), channel_id=1, source_target_pairs={{0,2},{1,3},{2,0},{3,1},{4,6},{5,7},{6,4},{7,5},{8,10},{9,11},{10,... | collective-permute-start | bytes 589832 | tf_op jit(solution)/shard_map/ppermute | solution.py:22
  55.6 6.9 %collective-permute-start.24 = (bf16[768,128]{1,0:T(8,128)(2,1)S(1)}, bf16[768,128]{1,0:T(8,128)(2,1)S(1)}, u32[]{:S(2)}, u32[]{:S(2)}) collective-permute-start(bf16[768,128]{1,0:T(8,128)(2,1)S(1)} %get-tuple-element.91), channel_id=1, source_target_pairs={{0,4},{1,5},{2,6},{3,7},{4,0},{5,1},{6,2},{7,3},{8,12},{9,13},{10,... | collective-permute-start | bytes 589832 | tf_op jit(solution)/shard_map/ppermute | solution.py:22
  64.0 7.7 %collective-permute-start.28 = (bf16[2,128,512]{2,1,0:T(8,128)(2,1)S(1)}, bf16[2,128,512]{2,1,0:T(8,128)(2,1)S(1)}, u32[]{:S(2)}, u32[]{:S(2)}) collective-permute-start(bf16[2,128,512]{2,1,0:T(8,128)(2,1)S(1)} %get-tuple-element.99), channel_id=1, source_target_pairs={{0,1},{1,0},{2,3},{3,2},{4,5},{5,4},{6,7},{7,6},{8,9},{9,8},{10,11... | collective-permute-start | bytes 786440 | tf_op jit(solution)/shard_map/ppermute | solution.py:22
  66.1 20.3 %collective-permute-start.30 = (bf16[2,128,1024]{2,1,0:T(8,128)(2,1)S(1)}, bf16[2,128,1024]{2,1,0:T(8,128)(2,1)S(1)}, u32[]{:S(2)}, u32[]{:S(2)}) collective-permute-start(bf16[2,128,1024]{2,1,0:T(8,128)(2,1)S(1)} %get-tuple-element.113), channel_id=1, source_target_pairs={{0,2},{1,3},{2,0},{3,1},{4,6},{5,7},{6,4},{7,5},{8,10},{9,11},{10,... | collective-permute-start | bytes 1572872 | tf_op jit(solution)/shard_map/ppermute | solution.py:22
  67.0 19.4 %collective-permute-start.31 = (bf16[2,128,1024]{2,1,0:T(8,128)(2,1)S(1)}, bf16[2,128,1024]{2,1,0:T(8,128)(2,1)S(1)}, u32[]{:S(2)}, u32[]{:S(2)}) collective-permute-start(bf16[2,128,1024]{2,1,0:T(8,128)(2,1)S(1)} %get-tuple-element.115), channel_id=1, source_target_pairs={{0,4},{1,5},{2,6},{3,7},{4,0},{5,1},{6,2},{7,3},{8,12},{9,13},{10,... | collective-permute-start | bytes 1572872 | tf_op jit(solution)/shard_map/ppermute | solution.py:22
  67.5 6.5 %collective-permute-start.25 = (bf16[512,128]{1,0:T(8,128)(2,1)S(1)}, bf16[512,128]{1,0:T(8,128)(2,1)S(1)}, u32[]{:S(2)}, u32[]{:S(2)}) collective-permute-start(bf16[512,128]{1,0:T(8,128)(2,1)S(1)} %get-tuple-element.93), channel_id=1, source_target_pairs={{0,8},{8,0},{16,24},{24,16},{1,9},{9,1},{17,25},{25,17},{2,10},{10... | collective-permute-start | bytes 393224 | tf_op jit(solution)/shard_map/ppermute | solution.py:22
  69.1 12.7 %collective-permute-start.26 = (bf16[512,128]{1,0:T(8,128)(2,1)S(1)}, bf16[512,128]{1,0:T(8,128)(2,1)S(1)}, u32[]{:S(2)}, u32[]{:S(2)}) collective-permute-start(bf16[512,128]{1,0:T(8,128)(2,1)S(1)} %get-tuple-element.94), channel_id=1, source_target_pairs={{0,16},{8,24},{16,0},{24,8},{1,17},{9,25},{17,1},{25,9},{2,18},{10... | collective-permute-start | bytes 393224 | tf_op jit(solution)/shard_map/ppermute | solution.py:22
  71.7 10.1 %collective-permute-start.27 = (bf16[512,128]{1,0:T(8,128)(2,1)S(1)}, bf16[512,128]{1,0:T(8,128)(2,1)S(1)}, u32[]{:S(2)}, u32[]{:S(2)}) collective-permute-start(bf16[512,128]{1,0:T(8,128)(2,1)S(1)} %get-tuple-element.95), channel_id=1, source_target_pairs={{0,24},{8,16},{16,8},{24,0},{1,25},{9,17},{17,9},{25,1},{2,26},{10... | collective-permute-start | bytes 393224 | tf_op jit(solution)/shard_map/ppermute | solution.py:22
  85.6 6.4 %collective-permute-start.36 = (bf16[512,128]{1,0:T(8,128)(2,1)S(1)}, bf16[512,128]{1,0:T(8,128)(2,1)S(1)}, u32[]{:S(2)}, u32[]{:S(2)}) collective-permute-start(bf16[512,128]{1,0:T(8,128)(2,1)S(1)} %last_kernel.1.refs_0_), channel_id=1, source_target_pairs={{0,6},{1,7},{2,4},{3,5},{4,2},{5,3},{6,0},{7,1},{8,14},{9,15},{10,... | collective-permute-start | bytes 393224 | tf_op jit(solution)/shard_map/ppermute | solution.py:22
  86.4 5.7 %collective-permute-start.37 = (bf16[512,128]{1,0:T(8,128)(2,1)S(1)}, bf16[512,128]{1,0:T(8,128)(2,1)S(1)}, u32[]{:S(2)}, u32[]{:S(2)}) collective-permute-start(bf16[512,128]{1,0:T(8,128)(2,1)S(1)} %last_kernel.1.refs_0_), channel_id=1, source_target_pairs={{0,1},{1,0},{2,3},{3,2},{4,5},{5,4},{6,7},{7,6},{8,9},{9,8},{10,11... | collective-permute-start | bytes 393224 | tf_op jit(solution)/shard_map/ppermute | solution.py:22
  86.5 10.2 %collective-permute-start.32 = (bf16[128,1024]{1,0:T(8,128)(2,1)S(1)}, bf16[128,1024]{1,0:T(8,128)(2,1)S(1)}, u32[]{:S(2)}, u32[]{:S(2)}) collective-permute-start(bf16[128,1024]{1,0:T(8,128)(2,1)S(1)} %get-tuple-element.117), channel_id=1, source_target_pairs={{0,4},{1,5},{2,6},{3,7},{4,0},{5,1},{6,2},{7,3},{8,12},{9,13},{10,... | collective-permute-start | bytes 786440 | tf_op jit(solution)/shard_map/ppermute | solution.py:22
  88.1 8.6 %collective-permute-start.33 = (bf16[128,1024]{1,0:T(8,128)(2,1)S(1)}, bf16[128,1024]{1,0:T(8,128)(2,1)S(1)}, u32[]{:S(2)}, u32[]{:S(2)}) collective-permute-start(bf16[128,1024]{1,0:T(8,128)(2,1)S(1)} %get-tuple-element.119), channel_id=1, source_target_pairs={{0,2},{1,3},{2,0},{3,1},{4,6},{5,7},{6,4},{7,5},{8,10},{9,11},{10,... | collective-permute-start | bytes 786440 | tf_op jit(solution)/shard_map/ppermute | solution.py:22
  (12 other events, 95.7 us)

commit v4 on v3

--- a/solution.py
+++ b/solution.py
@@ -30,7 +30,7 @@
     return pltpu.VMEM(shape, dtype)
 
 
-def run(body, outs, scalars, arrays, scratch=(), room=16, flops=0, exps=0):
+def run(body, outs, scalars, arrays, scratch=(), room=16):
     arrays = [pltpu.with_memory_space_constraint(v, pltpu.VMEM) for v in arrays]
     return pl.pallas_call(
         body,
@@ -42,17 +42,12 @@
         ),
         scratch_shapes=scratch,
         compiler_params=pltpu.CompilerParams(vmem_limit_bytes=room << 20),
-        cost_estimate=pl.CostEstimate(flops=flops, transcendentals=exps, bytes_accessed=4 << 20),
         name=getattr(body, "func", body).__name__,
     )(*scalars, *arrays)
 
 
-def head_of(chip):
-    return jnp.bitwise_xor(chip % 2, chip // 2)
-
-
 def column_of(chip, core):
-    return (chip // 2) * (KV_HEADS * HEAD_DIM) + (2 * core + head_of(chip)) * HEAD_DIM
+    return core * (KV_HEADS * HEAD_DIM) + chip * HEAD_DIM
 
 
 def quarter(z, r, size):
@@ -102,117 +97,154 @@
     out[...] = project_rows(ids[2], xs, (w0[...], w1[...], w2[...], w3[...]))
 
 
-def window_kernel(ids, *refs):
-    *xs, w0, w1, w2, w3, first, o0, o1, o2, o3, kv = refs
-    ws = (w0[...], w1[...], w2[...], w3[...])
-    m = ids[0]
-    rows = first.shape[0] // 3
-    for r in range(3):
-        kv[r] = first[r * rows : (r + 1) * rows, :]
-    kv[3] = project_rows(ids[2], xs, ws)
-    for r, out in ((3, o3), (1, o1), (2, o2), (0, o0)):
-        target = jnp.bitwise_xor(m, r)
-        for w in range(3):
-            chip = target + (w - 2)
-            rel = jnp.bitwise_xor(jnp.maximum(chip, 0), m)
-            out[w * rows : (w + 1) * rows, :] = jnp.where(
-                chip >= 0, kv[rel], jnp.zeros((rows, HEAD_DIM), BF16)
-            )
-
-
-def attend_kernel(side, docs, ids, lens, first, second, q_own, q_oth, g_own, g_oth,
-                  own, oth, d_first, d_second, bias):
+def order_kernel(ids, *refs):
+    *xs, w0, w1, w2, w3, first, out = refs
+    m, c, z = ids[0], ids[1], ids[2]
+    chip_rows = first.shape[0] // 3
+    rows = chip_rows // 2
+    last = project_rows(z, xs, (w0[...], w1[...], w2[...], w3[...]))
+    for r in range(4):
+        part = first[r * chip_rows : (r + 1) * chip_rows, :] if r < 3 else last
+        chip = jnp.bitwise_xor(m, r)
+        out[shard_rows(2 * chip + c, rows), :] = part[:rows]
+        out[shard_rows(2 * chip + 1 - c, rows), :] = part[rows:]
+
+
+def shard_rows(shard, rows, count=1):
+    return pl.ds(pl.multiple_of(shard * rows, rows), rows * count)
+
+
+def cut_heads_kernel(ids, *refs):
+    for r in range(4):
+        refs[8 + r][0] = refs[2 * r][...]
+        refs[8 + r][1] = refs[2 * r + 1][...]
+
+
+def cut_heads(ids, queries, out_grad):
+    rows = queries.shape[0]
+    width = queries.shape[1] // KV_HEADS
+    both = [pltpu.with_memory_space_constraint(v, pltpu.HBM) for v in (queries, out_grad)]
+    return pl.pallas_call(
+        cut_heads_kernel,
+        out_shape=(on_chip((2, rows, width)),) * 4,
+        grid_spec=pltpu.PrefetchScalarGridSpec(
+            num_scalar_prefetch=1,
+            grid=(1,),
+            in_specs=[
+                pl.BlockSpec((rows, width), lambda i, ids, r=r: (0, jnp.bitwise_xor(ids[0], r)))
+                for r in (0, 0, 1, 1, 2, 2, 3, 3)
+            ],
+            out_specs=[pl.BlockSpec(memory_space=pltpu.VMEM)] * 4,
+        ),
+        compiler_params=pltpu.CompilerParams(vmem_limit_bytes=16 << 20),
+        name="cut_heads_kernel",
+    )(ids, *(both * 4))
+
+
+def attend_kernel(rels, docs, first_call, last_call, ids, lens, mine, got, *refs):
+    count = len(rels)
+    qgs, refs = refs[:count], refs[count:]
+    if not first_call:
+        dk_in, dv_in = refs[:2]
+        refs = refs[2:]
+    outs, refs = refs[:count], refs[count:]
+    if last_call:
+        own, send, *refs = refs
+    dk, dv, key, val, key_t, val_t = refs
     m, c = ids[0], ids[1]
-    rows = q_own.shape[0]
-    keys = first.shape[0]
+    rows = qgs[0].shape[1]
+    keys = mine.shape[0]
+    heads = HEADS // KV_HEADS
     inv = HEAD_DIM ** (-0.5)
-    heads = HEADS // KV_HEADS
-    head = head_of(m) if side == 0 else 1 - head_of(m)
-    base = (2 * c + head) * (heads * HEAD_DIM)
-
-    def place(chip0, shape, dim):
-        t = lax.broadcasted_iota(jnp.int32, shape, dim)
-        chip = t // (2 * rows) + chip0
-        within = t % (2 * rows)
-        mine = within < rows
-        shard = 2 * chip + jnp.where(mine, c, 1 - c)
-        return shard * rows + jnp.where(mine, within, within - rows)
-
-    kpos = place(m - 2, (keys, 1), 0)
-    qpos = place(m, (1, 2 * rows), 1)
-    kdoc = jnp.where(kpos >= 0, 0, -1)
-    qdoc = jnp.zeros_like(qpos)
-    end = jnp.int32(0)
-    for k in range(docs):
-        end = end + lens[0, k]
-        kdoc = kdoc + (kpos >= end).astype(jnp.int32)
-        qdoc = qdoc + (qpos >= end).astype(jnp.int32)
-    bias[...] = jnp.where((kdoc == qdoc) & (kpos <= qpos), 0.0, NEG_FILL)
-
-    is_key = m < 2
-    key = jnp.where(is_key, first[...], second[...])
-    val = jnp.where(is_key, second[...], first[...])
-    key_t = key.T
-    val_t = val.T
-    dk = jnp.zeros((keys, HEAD_DIM), F32)
-    dv = jnp.zeros((keys, HEAD_DIM), F32)
-    for h in range(heads):
-        cols = pl.ds(pl.multiple_of(base + h * HEAD_DIM, HEAD_DIM), HEAD_DIM)
-        q = jnp.concatenate([q_own[:, cols], q_oth[:, cols]], axis=0)
-        g = jnp.concatenate([g_own[:, cols], g_oth[:, cols]], axis=0)
-        s = dot(key, q, 1, 1) * inv + bias[...]
-        p = jnp.exp(s - jnp.max(s, axis=0, keepdims=True))
-        p = p * (1.0 / jnp.sum(p, axis=0, keepdims=True))
-        low = p.astype(BF16)
-        out_t = dot(val_t, low, 1, 0).astype(BF16).astype(F32)
-        delta = jnp.sum(out_t * g.astype(F32).T, axis=0, keepdims=True)
-        dp = dot(val, g, 1, 1)
-        ds = (p * (dp - delta)).astype(BF16)
-        dq_t = dot(key_t, ds, 1, 0) * inv
-        dk = dk + dot(ds, q, 1, 0)
-        dv = dv + dot(low, g, 1, 0)
-        out = out_t.T.astype(BF16)
-        dq = dq_t.T.astype(BF16)
-        at = slice(h * HEAD_DIM, (h + 1) * HEAD_DIM)
-        own[0, :, at] = out[:rows]
-        oth[0, :, at] = out[rows:]
-        own[1, :, at] = dq[:rows]
-        oth[1, :, at] = dq[rows:]
-    dk = (dk * inv).astype(BF16)
-    dv = dv.astype(BF16)
-    d_first[...] = jnp.where(is_key, dk, dv)
-    d_second[...] = jnp.where(is_key, dv, dk)
-
-
-def attend(side, ids, lens, first, second, rest):
-    rows = rest[0].shape[0]
-    keys = first.shape[0]
-    part = on_chip((2, rows, HEADS // KV_HEADS * HEAD_DIM))
-    grad = on_chip((keys, HEAD_DIM))
-    return run(
-        functools.partial(attend_kernel, side, lens.shape[1]),
-        (part, part, grad, grad),
+    is_key = c == 0
+    key[...] = jnp.where(is_key, mine[...], got[...])
+    val[...] = jnp.where(is_key, got[...], mine[...])
+    key_t[...] = key[...].T
+    val_t[...] = val[...].T
+    if first_call:
+        dk[...] = jnp.zeros_like(dk)
+        dv[...] = jnp.zeros_like(dv)
+    else:
+        dk[...] = dk_in[...]
+        dv[...] = dv_in[...]
+
+    def body(i, shard, begin, shards):
+        span = shard_rows(begin, rows, shards)
+        size = shards * rows
+        kpos = lax.broadcasted_iota(jnp.int32, (size, 1), 0) + begin * rows
+        qpos = lax.broadcasted_iota(jnp.int32, (1, rows), 1) + shard * rows
+        kdoc = jnp.zeros_like(kpos)
+        qdoc = jnp.zeros_like(qpos)
+        end = jnp.int32(0)
+        for k in range(docs):
+            end = end + lens[0, k]
+            kdoc = kdoc + (kpos >= end).astype(jnp.int32)
+            qdoc = qdoc + (qpos >= end).astype(jnp.int32)
+        bias = jnp.where((kdoc == qdoc) & (kpos <= qpos), 0.0, NEG_FILL)
+        bias = jnp.concatenate([bias, bias], axis=1)
+        k, v, k_t, v_t = key[span, :], val[span, :], key_t[:, span], val_t[:, span]
+        grads_k, grads_v = [], []
+        for h in range(0, heads, 2):
+            cols = [slice((h + e) * HEAD_DIM, (h + e + 1) * HEAD_DIM) for e in range(2)]
+            q = jnp.concatenate([qgs[i][0, :, at] for at in cols], axis=0)
+            g = jnp.concatenate([qgs[i][1, :, at] for at in cols], axis=0)
+            s = dot(k, q, 1, 1) * inv + bias
+            p = jnp.exp(s - jnp.max(s, axis=0, keepdims=True))
+            p = p * (1.0 / jnp.sum(p, axis=0, keepdims=True))
+            low = p.astype(BF16)
+            out_t = dot(v_t, low, 1, 0).astype(BF16).astype(F32)
+            delta = jnp.sum(out_t * g.astype(F32).T, axis=0, keepdims=True)
+            ds = (p * (dot(v, g, 1, 1) - delta)).astype(BF16)
+            dq_t = dot(k_t, ds, 1, 0) * inv
+            grads_k.append(dot(ds, q, 1, 0))
+            grads_v.append(dot(low, g, 1, 0))
+            out = out_t.T.astype(BF16)
+            dq = dq_t.T.astype(BF16)
+            for e, at in enumerate(cols):
+                outs[i][0, :, at] = out[e * rows : (e + 1) * rows]
+                outs[i][1, :, at] = dq[e * rows : (e + 1) * rows]
+        dk[span, :] = dk[span, :] + (grads_k[0] + grads_k[1]) * inv
+        dv[span, :] = dv[span, :] + (grads_v[0] + grads_v[1])
+
+    for i, r in enumerate(rels):
+        chip = jnp.bitwise_xor(m, r)
+        shard = 2 * chip + c
+
+        @pl.when(chip == 0)
+        def _():
+            body(i, shard, 0, 2)
+
+        @pl.when(chip > 0)
+        def _():
+            body(i, shard, jnp.maximum(shard - REACH, 0), REACH + 1)
+
+    if last_call:
+        own[...] = jnp.where(is_key, dk[...], dv[...])
+        send[...] = jnp.where(is_key, dv[...], dk[...]).astype(BF16)
+
+
+def attend(rels, ids, lens, mine, got, qgs, sums=(), last=False):
+    keys = mine.shape[0]
+    total = (keys, HEAD_DIM)
+    wide, tall = pltpu.VMEM(total, BF16), pltpu.VMEM((HEAD_DIM, keys), BF16)
+    sides = (on_chip(total, F32), on_chip(total) if last else on_chip(total, F32))
+    *outs, first, second = run(
+        functools.partial(attend_kernel, rels, lens.shape[1], not sums, last),
+        tuple(on_chip(v.shape) for v in qgs) + sides,
         (ids, lens),
-        (first, second, *rest),
-        scratch=[pltpu.VMEM((keys, 2 * rows), F32)],
+        (mine, got, *qgs, *sums),
+        scratch=([pltpu.VMEM(total, F32)] * 2 if last else []) + [wide, wide, tall, tall],
         room=24,
-        flops=12 * keys * 2 * rows * HEADS // KV_HEADS * HEAD_DIM,
-        exps=keys * 2 * rows * HEADS // KV_HEADS,
-    )
-
-
-def place_kernel(ids, own_a, own_b, got_a, got_b, out, dq):
-    m, c = ids[0], ids[1]
-    width = own_a.shape[2]
-    for ref, core, head in (
-        (own_a, c, head_of(m)),
-        (own_b, c, 1 - head_of(m)),
-        (got_a, 1 - c, head_of(m)),
-        (got_b, 1 - c, 1 - head_of(m)),
-    ):
-        cols = pl.ds(pl.multiple_of((2 * core + head) * width, width), width)
-        out[:, cols] = ref[0]
-        dq[:, cols] = ref[1]
+    )
+    return outs, (first, second)
+
+
+def place_kernel(ids, p0, p1, p2, p3, out, dq):
+    width = p0.shape[2]
+    for r, part in enumerate((p0, p1, p2, p3)):
+        cols = quarter(ids[0], r, width)
+        out[:, cols] = part[0]
+        dq[:, cols] = part[1]
 
 
 def weight_block(z, r, g_t, xs, size):
@@ -220,28 +252,26 @@
     return dot(g_t, x, 1, 0).T
 
 
-def sum_kernel(ids, *refs):
-    d0, d1, d2, d3, *xs, own, oth, g_t, send1, send2, send3, acc = refs
-    m, z = ids[0], ids[2]
+def sum_kernel(ids, mine, got, own, oth):
+    m, c = ids[0], ids[1]
     rows = own.shape[1]
-    acc[...] = jnp.zeros_like(acc)
-    for r, d in enumerate((d0, d1, d2, d3)):
-        start = pl.multiple_of(jnp.bitwise_xor(m, r) * (2 * rows), 2 * rows)
-        span = pl.ds(start, 6 * rows)
-        acc[span, :] = acc[span, :] + d[...].astype(F32)
     for r in range(4):
-        start = pl.multiple_of((jnp.bitwise_xor(m, r) + 2) * (2 * rows), 2 * rows)
-        g = acc[pl.ds(start, 2 * rows), :].astype(BF16)
-        own[r] = g[:rows]
-        oth[r] = g[rows:]
-        g_t[:, r * 2 * rows : (r + 1) * 2 * rows] = g.T
+        chip = jnp.bitwise_xor(m, r)
+        for core, out in ((c, own), (1 - c, oth)):
+            span = shard_rows(2 * chip + core, rows)
+            out[r] = (mine[span, :] + got[span, :].astype(F32)).astype(BF16)
+
+
+def weight_kernel(ids, own, oth, *refs):
+    *xs, keep, send1, send2, send3, g_t = refs
+    z = ids[2]
+    rows = own.shape[1]
+    for r in range(4):
+        g_t[:, 2 * r * rows : (2 * r + 1) * rows] = own[r].T
+        g_t[:, (2 * r + 1) * rows : (2 * r + 2) * rows] = oth[r].T
     for r, send in ((3, send3), (2, send2), (1, send1)):
         send[...] = weight_block(z, r, g_t[...], xs, send.shape[0]).astype(BF16)
-
-
-def keep_kernel(ids, g_t, *refs):
-    *xs, keep = refs
-    keep[...] = weight_block(ids[2], 0, g_t[...], xs, keep.shape[0])
+    keep[...] = weight_block(z, 0, g_t[...], xs, keep.shape[0])
 
 
 def fold_kernel(keep, got, now, later):
@@ -320,60 +350,55 @@
     early = (x0, pair(x0), x1, pair(x1), x2, pair(x2))
     first = run(project_kernel, on_chip((6 * rows, HEAD_DIM)), (ids,), early + ws)
     *x3, first = lax.optimization_barrier((*x3, first))
+    us = tuple(flip(ws))
+    p0, *away = cut_heads(ids, queries, out_grad)
+    p1, p2, p3 = away
+    p1, p2 = near(p1), far(p2)
     late = (*x3, *flip(x3))
     xs = early + late
-
-    rest = (queries, pair(queries), out_grad, pair(out_grad))
-    us = tuple(flip(ws))
-
-    win = run(
-        window_kernel,
-        (on_chip((6 * rows, HEAD_DIM)),) * 4,
-        (ids,),
-        late + ws + (first,),
-        scratch=[pltpu.VMEM((4, 2 * rows, HEAD_DIM), BF16)],
-    )
-    win3, win1, win2 = lax.optimization_barrier((cross(win[3]), win[1], win[2]))
-    win1, win2 = near(win1), far(win2)
-
-    own_a, oth_a, d0, d3 = attend(0, ids, doc_lengths, win[0], win3, rest)
-    d3 = cross(d3)
-    got_a = pair(oth_a)
-    win1, win2, d0 = lax.optimization_barrier((win1, win2, d0))
-    own_b, oth_b, d1, d2 = attend(1, ids, doc_lengths, win1, win2, rest)
-    d1, d2, d3, got_a, us = lax.optimization_barrier((d1, d2, d3, got_a, us))
-    d1, d2 = near(d1), far(d2)
-    got_b = pair(oth_b)
-    like = jax.ShapeDtypeStruct(queries.shape, BF16)
-    attn_out, grad_queries = run(place_kernel, (like, like), (ids,), (own_a, own_b, got_a, got_b))
+    p1, p2, p3, first = lax.optimization_barrier((p1, p2, p3, first))
+    mine = run(order_kernel, on_chip((8 * rows, HEAD_DIM)), (ids,), late + ws + (first,))
+    p3 = cross(p3)
+    got = pair(mine)
+    (o0,), sums = attend((0,), ids, doc_lengths, mine, got, (p0,))
+    p1, p2, *sums = lax.optimization_barrier((p1, p2, *sums))
+    (o1, o2), sums = attend((1, 2), ids, doc_lengths, mine, got, (p1, p2), sums)
+    o1, o2 = near(o1), far(o2)
+    p3, *sums = lax.optimization_barrier((p3, *sums))
+    (o3,), (g_mine, g_send) = attend((3,), ids, doc_lengths, mine, got, (p3,), sums, True)
+    g_send, us = lax.optimization_barrier((g_send, us))
+    g_got = pair(g_send)
+    o3 = cross(o3)
 
     block = on_chip((4, rows, HEAD_DIM))
     third = on_chip((size, HEAD_DIM))
-    g_own, g_oth, g_t, *sends = run(
-        sum_kernel,
-        (block, block, on_chip((HEAD_DIM, 8 * rows)), third, third, third),
-        (ids,),
-        (d0, d1, d2, d3) + xs,
-        scratch=[pltpu.VMEM((12 * rows, HEAD_DIM), F32)],
-    )
-    gots = [swap(v, "fsdp", bit) for v, bit in zip(sends, (1, 2, 3))]
-    g_oth = pair(g_oth)
-    g_t, g_oth = lax.optimization_barrier((g_t, g_oth))
+    g_own, g_oth = run(sum_kernel, (block, block), (ids,), (g_mine, g_got))
+    g_got = pair(g_oth)
     half = (rows, width // 2)
     send_a, send_b, keep_a, keep_b = run(
         token_kernel,
         (on_chip((2, *half)), on_chip((2, *half)), on_chip((2, *half), F32), on_chip((2, *half), F32)),
         (),
-        (g_own, g_oth) + ws + us,
+        (g_own, g_got) + ws + us,
     )
     got_a, got_b = near(send_a), far(send_b)
-    keep = run(keep_kernel, on_chip((size, HEAD_DIM), F32), (ids,), (g_t,) + xs)
-    *gots, attn_out, grad_queries = lax.optimization_barrier((*gots, attn_out, grad_queries))
+    keep, *sends = run(
+        weight_kernel,
+        (on_chip((size, HEAD_DIM), F32), third, third, third),
+        (ids,),
+        (g_own, g_oth) + xs,
+        scratch=[pltpu.VMEM((HEAD_DIM, 8 * rows), BF16)],
+    )
+    gots = [swap(v, "fsdp", bit) for v, bit in zip(sends, (1, 2, 3))]
     mine = run(last_kernel, on_chip((size, HEAD_DIM)), (), (keep, *gots))
+    got_a, got_b, mine = lax.optimization_barrier((got_a, got_b, mine))
     fold = (on_chip(half, F32), on_chip(half))
     a, a_send, b, b_send = run(fold_both_kernel, fold + fold, (), (keep_a, got_a, keep_b, got_b))
     got_a, got_b = far(a_send), near(b_send)
+    like = jax.ShapeDtypeStruct(queries.shape, BF16)
+    attn_out, grad_queries = run(place_kernel, (like, like), (ids,), (o0, o1, o2, o3))
     mine = [mine, near(mine), far(mine), cross(mine)]
+    *mine, attn_out, grad_queries = lax.optimization_barrier((*mine, attn_out, grad_queries))
     theirs = [pair(v) for v in mine]
     grad_weight = run(
         assemble_kernel,

time: 98.3 us -> 93.8 us (0.954)
  waiting for transfers between devices: 37.9 us -> 33.3 us
    ppermute x41 -> x39, waiting for transfers between devices: 37.9 us -> 33.3 us  [swap(): return lax.ppermute(value, axis, [(i, i ^ bit) for i in range(count)])]
    pallas_call x0 -> x1, Pallas kernels: none -> 1.9 us  [cut_heads(): pl.pallas_call(cut_heads_kernel, out_shape=(on_chip((2, rows, width)),) *...]
    pallas_call x13 -> x14, Pallas kernels: 22.9 us -> 21.9 us  [run(): pl.pallas_call(body, out_shape=outs, in_specs=[pl.BlockSpec(memory_space=...]
    ppermute x41 -> x39, starting transfers between devices: 34.8 us -> 34 us  [swap(): return lax.ppermute(value, axis, [(i, i ^ bit) for i in range(count)])]
  transfers between devices with their start and end apart: 41 -> 39, of which waited for: 17 -> 15; matrix products, arithmetic and copies ran while one was open for 0% -> 0% of each run, Pallas kernels for 22% -> 22%
where the time goes in v4:
time: 93.8 us; the launch traced here: 93.6 us
  starting transfers between devices  34 us (36%)
  waiting for transfers between devices  33.3 us (36%)
  Pallas kernels  25.5 us (27%)
    ppermute x39, starting transfers between devices, swap(): return lax.ppermute(value, axis, [(i, i ^ bit) for i in range(count)])  34 us
    ppermute x39, waiting for transfers between devices, swap(): return lax.ppermute(value, axis, [(i, i ^ bit) for i in range(count)])  33.3 us
    pallas_call x14, Pallas kernels, run(): pl.pallas_call(body, out_shape=outs, in_specs=[pl.BlockSpec(memory_space=...  21.9 us
    pallas_call x1, Pallas kernels, cut_heads(): pl.pallas_call(cut_heads_kernel, out_shape=(on_chip((2, rows, width)),) *...  1.9 us
  transfers between devices with their start and end apart: 39, of which 15 were waited for; matrix products, arithmetic and copies ran while one was open for 0% of the time, Pallas kernels for 22%

profile of v4, /device:TPU:0, one launch (start us, length us, event | category | flops | bytes accessed | tf_op | source)
XLA Modules:
  0.0 93.6 jit_solution(2256977700868796655)
XLA Ops:
  0.6 3.0 %collective-permute-start = (bf16[128,2048]{1,0:T(8,128)(2,1)}, bf16[128,2048]{1,0:T(8,128)(2,1)S(1)}, u32[]{:S(2)}, u32[]{:S(2)}) collective-permute-start(bf16[128,2048]{1,0:T(8,128)(2,1)} %x.1), channel_id=1, source_target_pairs={{0,2},{1,3},{2,0},{3,1},{4,6},{5,7},{6,4},{7,5},{8,10},{9,11},{10,... | collective-permute-start | bytes 1572872 | tf_op jit(solution)/shard_map/ppermute | solution.py:22
  3.7 1.5 %collective-permute-start.1 = (bf16[128,2048]{1,0:T(8,128)(2,1)}, bf16[128,2048]{1,0:T(8,128)(2,1)S(1)}, u32[]{:S(2)}, u32[]{:S(2)}) collective-permute-start(bf16[128,2048]{1,0:T(8,128)(2,1)} %x.1), channel_id=1, source_target_pairs={{0,4},{1,5},{2,6},{3,7},{4,0},{5,1},{6,2},{7,3},{8,12},{9,13},{10,... | collective-permute-start | bytes 1572872 | tf_op jit(solution)/shard_map/ppermute | solution.py:22
  5.3 1.7 %prep_kernel.1 = (bf16[512,128]{1,0:T(8,128)(2,1)S(1)}, bf16[128,2048]{1,0:T(8,128)(2,1)S(1)}) custom-call(s32[3]{0:T(128)S(1)} %pad_add_fusion.ids, s32[1]{0:T(128)} %bitcast.3.block, bf16[512,1024]{1,0:T(8,128)(2,1)} %weight.1, bf16[128,2048]{1,0:T(8,128)(2,1)} %x.1), custom_call_target="tpu_custom_call" | custom-call | tf_op jit(solution)/shard_map/prep_kernel/pallas_call | solution.py:75
  7.0 1.6 %collective-permute-start.2 = (bf16[512,128]{1,0:T(8,128)(2,1)S(1)}, bf16[512,128]{1,0:T(8,128)(2,1)S(1)}, u32[]{:S(2)}, u32[]{:S(2)}) collective-permute-start(bf16[512,128]{1,0:T(8,128)(2,1)S(1)} %get-tuple-element.70.refs_6_.refs_4_.w0), channel_id=1, source_target_pairs={{0,8},{8,0},{16,24},{24,16},{1,9},{9,1},{17,25},{25,17},{2,10},{10... | collective-permute-start | bytes 393224 | tf_op jit(solution)/shard_map/ppermute | solution.py:22
  8.6 2.6 %collective-permute-start.3 = (bf16[512,128]{1,0:T(8,128)(2,1)S(1)}, bf16[512,128]{1,0:T(8,128)(2,1)S(1)}, u32[]{:S(2)}, u32[]{:S(2)}) collective-permute-start(bf16[512,128]{1,0:T(8,128)(2,1)S(1)} %get-tuple-element.70.refs_6_.refs_4_.w0), channel_id=1, source_target_pairs={{0,16},{8,24},{16,0},{24,8},{1,17},{9,25},{17,1},{25,9},{2,18},{10... | collective-permute-start | bytes 393224 | tf_op jit(solution)/shard_map/ppermute | solution.py:22
  11.2 2.5 %collective-permute-done.2.refs_7_.refs_5_.w1 = bf16[512,128]{1,0:T(8,128)(2,1)S(1)} collective-permute-done((bf16[512,128]{1,0:T(8,128)(2,1)S(1)}, bf16[512,128]{1,0:T(8,128)(2,1)S(1)}, u32[]{:S(2)}, u32[]{:S(2)}) %collective-permute-start.2) | collective-permute-done | bytes 131104 | tf_op jit(solution)/shard_map/ppermute | solution.py:22
  13.7 3.0 %collective-permute-done.3.refs_8_.refs_6_.w2 = bf16[512,128]{1,0:T(8,128)(2,1)S(1)} collective-permute-done((bf16[512,128]{1,0:T(8,128)(2,1)S(1)}, bf16[512,128]{1,0:T(8,128)(2,1)S(1)}, u32[]{:S(2)}, u32[]{:S(2)}) %collective-permute-start.3) | collective-permute-done | bytes 131104 | tf_op jit(solution)/shard_map/ppermute | solution.py:22
  17.8 1.6 %collective-permute-start.4 = (bf16[64,2048]{1,0:T(8,128)(2,1)S(1)}, bf16[64,2048]{1,0:T(8,128)(2,1)S(1)}, u32[]{:S(2)}, u32[]{:S(2)}) collective-permute-start(bf16[64,2048]{1,0:T(8,128)(2,1)S(1)} %get-tuple-element.73), channel_id=1, source_target_pairs={{0,4},{1,5},{2,6},{3,7},{4,0},{5,1},{6,2},{7,3},{8,12},{9,13},{10,... | collective-permute-start | bytes 786440 | tf_op jit(solution)/shard_map/ppermute | solution.py:22
  19.9 1.6 %collective-permute-start.9 = (bf16[512,128]{1,0:T(8,128)(2,1)S(1)}, bf16[512,128]{1,0:T(8,128)(2,1)S(1)}, u32[]{:S(2)}, u32[]{:S(2)}) collective-permute-start(bf16[512,128]{1,0:T(8,128)(2,1)S(1)} %collective-permute-done.3.refs_8_.refs_6_.w2), channel_id=1, source_target_pairs={{0,8},{8,0},{16,24},{24,16},{1,9},{9,1},{17,25},{25,17},{2,10},{10... | collective-permute-start | bytes 393224 | tf_op jit(solution)/shard_map/ppermute | solution.py:22
  21.5 1.9 %cut_heads_kernel.1 = (bf16[2,128,512]{2,1,0:T(8,128)(2,1)S(1)}, bf16[2,128,512]{2,1,0:T(8,128)(2,1)S(1)}, bf16[2,128,512]{2,1,0:T(8,128)(2,1)S(1)}, bf16[2,128,512]{2,1,0:T(8,128)(2,1)S(1)}) custom-call(s32[3]{0:T(128)S(1)} %pad_add_fusion.ids, bf16[128,2048]{1,0:T(8,128)(2,1)} %refs_6_.1, bf16[128,2048]{1,0:T(8,128)(2,1)} %refs_7_.1, ...), custom_call_target="tpu_custom_call" | custom-call | tf_op jit(solution)/shard_map/cut_heads_kernel/pallas_call | solution.py:127
  23.4 1.5 %collective-permute-done.9.refs_9_.refs_7_.w3 = bf16[512,128]{1,0:T(8,128)(2,1)S(1)} collective-permute-done((bf16[512,128]{1,0:T(8,128)(2,1)S(1)}, bf16[512,128]{1,0:T(8,128)(2,1)S(1)}, u32[]{:S(2)}, u32[]{:S(2)}) %collective-permute-start.9) | collective-permute-done | bytes 131104 | tf_op jit(solution)/shard_map/ppermute | solution.py:22
  24.9 1.5 %collective-permute-start.12 = (bf16[2,128,512]{2,1,0:T(8,128)(2,1)S(1)}, bf16[2,128,512]{2,1,0:T(8,128)(2,1)S(1)}, u32[]{:S(2)}, u32[]{:S(2)}) collective-permute-start(bf16[2,128,512]{2,1,0:T(8,128)(2,1)S(1)} %get-tuple-element.80), channel_id=1, source_target_pairs={{0,2},{1,3},{2,0},{3,1},{4,6},{5,7},{6,4},{7,5},{8,10},{9,11},{10,... | collective-permute-start | bytes 786440 | tf_op jit(solution)/shard_map/ppermute | solution.py:22
  26.9 1.5 %project_kernel.1.refs_8_ = bf16[768,128]{1,0:T(8,128)(2,1)S(1)} custom-call(s32[3]{0:T(128)S(1)} %pad_add_fusion.ids, bf16[128,2048]{1,0:T(8,128)(2,1)S(1)} %get-tuple-element.75.refs_0_, bf16[128,2048]{1,0:T(8,128)(2,1)S(1)} %collective-permute-done.6.refs_1_, bf16[128,2048]{1,0:T(8,128)(2,1)S(1)} %collective-permute-done.x1.refs_2_, ...), custom_call_target="tpu_custom_call" | custom-call | tf_op jit(solution)/shard_map/project_kernel/pallas_call | solution.py:35
  29.1 3.9 %collective-permute-done.12.refs_0_ = bf16[2,128,512]{2,1,0:T(8,128)(2,1)S(1)} collective-permute-done((bf16[2,128,512]{2,1,0:T(8,128)(2,1)S(1)}, bf16[2,128,512]{2,1,0:T(8,128)(2,1)S(1)}, u32[]{:S(2)}, u32[]{:S(2)}) %collective-permute-start.12) | collective-permute-done | bytes 262176 | tf_op jit(solution)/shard_map/ppermute | solution.py:22
  35.7 2.3 %attend_kernel.3 = (bf16[2,128,512]{2,1,0:T(8,128)(2,1)S(1)}, f32[1024,128]{1,0:T(8,128)S(1)}, f32[1024,128]{1,0:T(8,128)S(1)}) custom-call(s32[3]{0:T(128)S(1)} %pad_add_fusion.ids, s32[1,4]{1,0:T(1,128)S(1)} %copy-done, bf16[1024,128]{1,0:T(8,128)(2,1)S(1)} %order_kernel.1.mine, bf16[1024,128]{1,0:T(8,128)(2,1)S(1)} %collective-permute-done.14.got, ...), custom_call_target="tpu_custom_call" | custom-call | tf_op jit(solution)/shard_map/attend_kernel/pallas_call | solution.py:35
  38.0 5.6 %attend_kernel.4 = (bf16[2,128,512]{2,1,0:T(8,128)(2,1)S(1)}, bf16[2,128,512]{2,1,0:T(8,128)(2,1)S(1)}, f32[1024,128]{1,0:T(8,128)S(1)}, f32[1024,128]{1,0:T(8,128)S(1)}) custom-call(s32[3]{0:T(128)S(1)} %pad_add_fusion.ids, s32[1,4]{1,0:T(1,128)S(1)} %copy-done, bf16[1024,128]{1,0:T(8,128)(2,1)S(1)} %order_kernel.1.mine, ...), custom_call_target="tpu_custom_call" | custom-call | tf_op jit(solution)/shard_map/attend_kernel/pallas_call | solution.py:35
  43.6 3.3 %attend_kernel.5 = (bf16[2,128,512]{2,1,0:T(8,128)(2,1)S(1)}, f32[1024,128]{1,0:T(8,128)S(1)}, bf16[1024,128]{1,0:T(8,128)(2,1)S(1)}) custom-call(s32[3]{0:T(128)S(1)} %pad_add_fusion.ids, s32[1,4]{1,0:T(1,128)S(1)} %copy-done, bf16[1024,128]{1,0:T(8,128)(2,1)S(1)} %order_kernel.1.mine, bf16[1024,128]{1,0:T(8,128)(2,1)S(1)} %collective-permute-done.14.got, ...), custom_call_target="tpu_custom_call" | custom-call | tf_op jit(solution)/shard_map/attend_kernel/pallas_call | solution.py:35
  47.4 1.2 %collective-permute-done.20.got = bf16[1024,128]{1,0:T(8,128)(2,1)S(1)} collective-permute-done((bf16[1024,128]{1,0:T(8,128)(2,1)S(1)}, bf16[1024,128]{1,0:T(8,128)(2,1)S(1)}, u32[]{:S(2)}, u32[]{:S(2)}) %collective-permute-start.20) | collective-permute-done | bytes 262176 | tf_op jit(solution)/shard_map/ppermute | solution.py:22
  51.3 1.4 %collective-permute-start.22 = (bf16[2,128,1024]{2,1,0:T(8,128)(2,1)S(1)}, bf16[2,128,1024]{2,1,0:T(8,128)(2,1)S(1)}, u32[]{:S(2)}, u32[]{:S(2)}) collective-permute-start(bf16[2,128,1024]{2,1,0:T(8,128)(2,1)S(1)} %get-tuple-element.109), channel_id=1, source_target_pairs={{0,2},{1,3},{2,0},{3,1},{4,6},{5,7},{6,4},{7,5},{8,10},{9,11},{10,... | collective-permute-start | bytes 1572872 | tf_op jit(solution)/shard_map/ppermute | solution.py:22
  52.8 1.5 %collective-permute-start.23 = (bf16[2,128,1024]{2,1,0:T(8,128)(2,1)S(1)}, bf16[2,128,1024]{2,1,0:T(8,128)(2,1)S(1)}, u32[]{:S(2)}, u32[]{:S(2)}) collective-permute-start(bf16[2,128,1024]{2,1,0:T(8,128)(2,1)S(1)} %get-tuple-element.110), channel_id=1, source_target_pairs={{0,4},{1,5},{2,6},{3,7},{4,0},{5,1},{6,2},{7,3},{8,12},{9,13},{10,... | collective-permute-start | bytes 1572872 | tf_op jit(solution)/shard_map/ppermute | solution.py:22
  54.3 1.4 %weight_kernel.1 = (f32[512,128]{1,0:T(8,128)S(1)}, bf16[512,128]{1,0:T(8,128)(2,1)S(1)}, bf16[512,128]{1,0:T(8,128)(2,1)S(1)}, bf16[512,128]{1,0:T(8,128)(2,1)S(1)}) custom-call(s32[3]{0:T(128)S(1)} %pad_add_fusion.ids, bf16[4,128,128]{2,1,0:T(8,128)(2,1)S(1)} %get-tuple-element.103.own, bf16[4,128,128]{2,1,0:T(8,128)(2,1)S(1)} %get-tuple-element.104.oth, ...), custom_call_target="tpu_custom_call" | custom-call | tf_op jit(solution)/shard_map/weight_kernel/pallas_call | solution.py:35
  55.7 1.6 %collective-permute-start.24 = (bf16[512,128]{1,0:T(8,128)(2,1)S(1)}, bf16[512,128]{1,0:T(8,128)(2,1)S(1)}, u32[]{:S(2)}, u32[]{:S(2)}) collective-permute-start(bf16[512,128]{1,0:T(8,128)(2,1)S(1)} %get-tuple-element.112), channel_id=1, source_target_pairs={{0,8},{8,0},{16,24},{24,16},{1,9},{9,1},{17,25},{25,17},{2,10},{10... | collective-permute-start | bytes 393224 | tf_op jit(solution)/shard_map/ppermute | solution.py:22
  57.4 2.6 %collective-permute-start.25 = (bf16[512,128]{1,0:T(8,128)(2,1)S(1)}, bf16[512,128]{1,0:T(8,128)(2,1)S(1)}, u32[]{:S(2)}, u32[]{:S(2)}) collective-permute-start(bf16[512,128]{1,0:T(8,128)(2,1)S(1)} %get-tuple-element.113), channel_id=1, source_target_pairs={{0,16},{8,24},{16,0},{24,8},{1,17},{9,25},{17,1},{25,9},{2,18},{10... | collective-permute-start | bytes 393224 | tf_op jit(solution)/shard_map/ppermute | solution.py:22
  60.2 2.1 %collective-permute-done.24.got1 = bf16[512,128]{1,0:T(8,128)(2,1)S(1)} collective-permute-done((bf16[512,128]{1,0:T(8,128)(2,1)S(1)}, bf16[512,128]{1,0:T(8,128)(2,1)S(1)}, u32[]{:S(2)}, u32[]{:S(2)}) %collective-permute-start.24) | collective-permute-done | bytes 131104 | tf_op jit(solution)/shard_map/ppermute | solution.py:22
  63.2 6.9 %collective-permute-done.25.got2 = bf16[512,128]{1,0:T(8,128)(2,1)S(1)} collective-permute-done((bf16[512,128]{1,0:T(8,128)(2,1)S(1)}, bf16[512,128]{1,0:T(8,128)(2,1)S(1)}, u32[]{:S(2)}, u32[]{:S(2)}) %collective-permute-start.25) | collective-permute-done | bytes 131104 | tf_op jit(solution)/shard_map/ppermute | solution.py:22
  72.2 2.5 %collective-permute-start.33 = (bf16[128,1024]{1,0:T(8,128)(2,1)S(1)}, bf16[128,1024]{1,0:T(8,128)(2,1)S(1)}, u32[]{:S(2)}, u32[]{:S(2)}) collective-permute-start(bf16[128,1024]{1,0:T(8,128)(2,1)S(1)} %get-tuple-element.129), channel_id=1, source_target_pairs={{0,4},{1,5},{2,6},{3,7},{4,0},{5,1},{6,2},{7,3},{8,12},{9,13},{10,... | collective-permute-start | bytes 786440 | tf_op jit(solution)/shard_map/ppermute | solution.py:22
  75.0 3.3 %collective-permute-done.30.p1 = bf16[2,128,512]{2,1,0:T(8,128)(2,1)S(1)} collective-permute-done((bf16[2,128,512]{2,1,0:T(8,128)(2,1)S(1)}, bf16[2,128,512]{2,1,0:T(8,128)(2,1)S(1)}, u32[]{:S(2)}, u32[]{:S(2)}) %collective-permute-start.30) | collective-permute-done | bytes 262176 | tf_op jit(solution)/shard_map/ppermute | solution.py:22
  78.3 1.7 %collective-permute-start.29 = (bf16[512,128]{1,0:T(8,128)(2,1)S(1)}, bf16[512,128]{1,0:T(8,128)(2,1)S(1)}, u32[]{:S(2)}, u32[]{:S(2)}) collective-permute-start(bf16[512,128]{1,0:T(8,128)(2,1)S(1)} %last_kernel.1.refs_0_), channel_id=1, source_target_pairs={{0,6},{1,7},{2,4},{3,5},{4,2},{5,3},{6,0},{7,1},{8,14},{9,15},{10,... | collective-permute-start | bytes 393224 | tf_op jit(solution)/shard_map/ppermute | solution.py:22
  81.7 1.6 %place_kernel.1 = (bf16[128,2048]{1,0:T(8,128)(2,1)}, bf16[128,2048]{1,0:T(8,128)(2,1)}) custom-call(s32[3]{0:T(128)S(1)} %pad_add_fusion.ids, bf16[2,128,512]{2,1,0:T(8,128)(2,1)S(1)} %get-tuple-element.116.p0, bf16[2,128,512]{2,1,0:T(8,128)(2,1)S(1)} %collective-permute-done.30.p1, bf16[2,128,512]{2,1,0:T(8,128)(2,1)S(1)} %collective-permute-done.31.p2, ...), custom_call_target="tpu_custom_call" | custom-call | tf_op jit(solution)/shard_map/place_kernel/pallas_call | solution.py:35
  83.3 5.7 %collective-permute-done.28.refs_2_ = bf16[512,128]{1,0:T(8,128)(2,1)S(1)} collective-permute-done((bf16[512,128]{1,0:T(8,128)(2,1)S(1)}, bf16[512,128]{1,0:T(8,128)(2,1)S(1)}, u32[]{:S(2)}, u32[]{:S(2)}) %collective-permute-start.28) | collective-permute-done | bytes 131104 | tf_op jit(solution)/shard_map/ppermute | solution.py:22
  90.0 1.4 %token_last_kernel.1 = bf16[128,2048]{1,0:T(8,128)(2,1)} custom-call(s32[3]{0:T(128)S(1)} %pad_add_fusion.ids, f32[128,1024]{1,0:T(8,128)S(1)} %get-tuple-element.128.a, bf16[128,1024]{1,0:T(8,128)(2,1)S(1)} %collective-permute-done.33.got_a, f32[128,1024]{1,0:T(8,128)S(1)} %get-tuple-element.130.b, bf16[128,1024]{1,0:T(8,128)(2,1)S(1)} %collective-permute-done.34.got_b), custom_call_target="tpu_custom_call" | custom-call | tf_op jit(solution)/shard_map/token_last_kernel/pallas_call | solution.py:35
  91.5 2.1 %assemble_kernel.1 = f32[512,1024]{1,0:T(8,128)} custom-call(s32[3]{0:T(128)S(1)} %pad_add_fusion.ids, bf16[512,128]{1,0:T(8,128)(2,1)S(1)} %last_kernel.1.refs_0_, bf16[512,128]{1,0:T(8,128)(2,1)S(1)} %collective-permute-done.27.refs_1_, bf16[512,128]{1,0:T(8,128)(2,1)S(1)} %collective-permute-done.28.refs_2_, ...), custom_call_target="tpu_custom_call" | custom-call | tf_op jit(solution)/shard_map/assemble_kernel/pallas_call | solution.py:35
  (65 shorter events, 15.0 us)
Async XLA Ops:
  0.6 16.1 %collective-permute-start = (bf16[128,2048]{1,0:T(8,128)(2,1)}, bf16[128,2048]{1,0:T(8,128)(2,1)S(1)}, u32[]{:S(2)}, u32[]{:S(2)}) collective-permute-start(bf16[128,2048]{1,0:T(8,128)(2,1)} %x.1), channel_id=1, source_target_pairs={{0,2},{1,3},{2,0},{3,1},{4,6},{5,7},{6,4},{7,5},{8,10},{9,11},{10,... | collective-permute-start | bytes 1572872 | tf_op jit(solution)/shard_map/ppermute | solution.py:22
  3.7 13.6 %collective-permute-start.1 = (bf16[128,2048]{1,0:T(8,128)(2,1)}, bf16[128,2048]{1,0:T(8,128)(2,1)S(1)}, u32[]{:S(2)}, u32[]{:S(2)}) collective-permute-start(bf16[128,2048]{1,0:T(8,128)(2,1)} %x.1), channel_id=1, source_target_pairs={{0,4},{1,5},{2,6},{3,7},{4,0},{5,1},{6,2},{7,3},{8,12},{9,13},{10,... | collective-permute-start | bytes 1572872 | tf_op jit(solution)/shard_map/ppermute | solution.py:22
  7.0 6.8 %collective-permute-start.2 = (bf16[512,128]{1,0:T(8,128)(2,1)S(1)}, bf16[512,128]{1,0:T(8,128)(2,1)S(1)}, u32[]{:S(2)}, u32[]{:S(2)}) collective-permute-start(bf16[512,128]{1,0:T(8,128)(2,1)S(1)} %get-tuple-element.70.refs_6_.refs_4_.w0), channel_id=1, source_target_pairs={{0,8},{8,0},{16,24},{24,16},{1,9},{9,1},{17,25},{25,17},{2,10},{10... | collective-permute-start | bytes 393224 | tf_op jit(solution)/shard_map/ppermute | solution.py:22
  8.6 8.2 %collective-permute-start.3 = (bf16[512,128]{1,0:T(8,128)(2,1)S(1)}, bf16[512,128]{1,0:T(8,128)(2,1)S(1)}, u32[]{:S(2)}, u32[]{:S(2)}) collective-permute-start(bf16[512,128]{1,0:T(8,128)(2,1)S(1)} %get-tuple-element.70.refs_6_.refs_4_.w0), channel_id=1, source_target_pairs={{0,16},{8,24},{16,0},{24,8},{1,17},{9,25},{17,1},{25,9},{2,18},{10... | collective-permute-start | bytes 393224 | tf_op jit(solution)/shard_map/ppermute | solution.py:22
  11.2 8.7 %collective-permute-start.6 = (bf16[128,2048]{1,0:T(8,128)(2,1)S(1)}, bf16[128,2048]{1,0:T(8,128)(2,1)S(1)}, u32[]{:S(2)}, u32[]{:S(2)}) collective-permute-start(bf16[128,2048]{1,0:T(8,128)(2,1)S(1)} %get-tuple-element.75.refs_0_), channel_id=1, source_target_pairs={{0,1},{1,0},{2,3},{3,2},{4,5},{5,4},{6,7},{7,6},{8,9},{9,8},{10,11... | collective-permute-start | bytes 1572872 | tf_op jit(solution)/shard_map/ppermute | solution.py:22
  17.3 9.1 %collective-permute-start.7 = (bf16[128,2048]{1,0:T(8,128)(2,1)S(1)}, bf16[128,2048]{1,0:T(8,128)(2,1)S(1)}, u32[]{:S(2)}, u32[]{:S(2)}) collective-permute-start(bf16[128,2048]{1,0:T(8,128)(2,1)S(1)} %collective-permute-done.x1.refs_2_), channel_id=1, source_target_pairs={{0,1},{1,0},{2,3},{3,2},{4,5},{5,4},{6,7},{7,6},{8,9},{9,8},{10,11... | collective-permute-start | bytes 1572872 | tf_op jit(solution)/shard_map/ppermute | solution.py:22
  17.3 9.6 %collective-permute-start.8 = (bf16[128,2048]{1,0:T(8,128)(2,1)S(1)}, bf16[128,2048]{1,0:T(8,128)(2,1)S(1)}, u32[]{:S(2)}, u32[]{:S(2)}) collective-permute-start(bf16[128,2048]{1,0:T(8,128)(2,1)S(1)} %collective-permute-done.1.x2.refs_4_), channel_id=1, source_target_pairs={{0,1},{1,0},{2,3},{3,2},{4,5},{5,4},{6,7},{7,6},{8,9},{9,8},{10,11... | collective-permute-start | bytes 1572872 | tf_op jit(solution)/shard_map/ppermute | solution.py:22
  17.8 10.6 %collective-permute-start.4 = (bf16[64,2048]{1,0:T(8,128)(2,1)S(1)}, bf16[64,2048]{1,0:T(8,128)(2,1)S(1)}, u32[]{:S(2)}, u32[]{:S(2)}) collective-permute-start(bf16[64,2048]{1,0:T(8,128)(2,1)S(1)} %get-tuple-element.73), channel_id=1, source_target_pairs={{0,4},{1,5},{2,6},{3,7},{4,0},{5,1},{6,2},{7,3},{8,12},{9,13},{10,... | collective-permute-start | bytes 786440 | tf_op jit(solution)/shard_map/ppermute | solution.py:22
  19.4 9.2 %collective-permute-start.5 = (bf16[64,2048]{1,0:T(8,128)(2,1)S(1)}, bf16[64,2048]{1,0:T(8,128)(2,1)S(1)}, u32[]{:S(2)}, u32[]{:S(2)}) collective-permute-start(bf16[64,2048]{1,0:T(8,128)(2,1)S(1)} %get-tuple-element.74), channel_id=1, source_target_pairs={{0,2},{1,3},{2,0},{3,1},{4,6},{5,7},{6,4},{7,5},{8,10},{9,11},{10,... | collective-permute-start | bytes 786440 | tf_op jit(solution)/shard_map/ppermute | solution.py:22
  19.9 5.0 %collective-permute-start.9 = (bf16[512,128]{1,0:T(8,128)(2,1)S(1)}, bf16[512,128]{1,0:T(8,128)(2,1)S(1)}, u32[]{:S(2)}, u32[]{:S(2)}) collective-permute-start(bf16[512,128]{1,0:T(8,128)(2,1)S(1)} %collective-permute-done.3.refs_8_.refs_6_.w2), channel_id=1, source_target_pairs={{0,8},{8,0},{16,24},{24,16},{1,9},{9,1},{17,25},{25,17},{2,10},{10... | collective-permute-start | bytes 393224 | tf_op jit(solution)/shard_map/ppermute | solution.py:22
  24.9 8.0 %collective-permute-start.12 = (bf16[2,128,512]{2,1,0:T(8,128)(2,1)S(1)}, bf16[2,128,512]{2,1,0:T(8,128)(2,1)S(1)}, u32[]{:S(2)}, u32[]{:S(2)}) collective-permute-start(bf16[2,128,512]{2,1,0:T(8,128)(2,1)S(1)} %get-tuple-element.80), channel_id=1, source_target_pairs={{0,2},{1,3},{2,0},{3,1},{4,6},{5,7},{6,4},{7,5},{8,10},{9,11},{10,... | collective-permute-start | bytes 786440 | tf_op jit(solution)/shard_map/ppermute | solution.py:22
  26.4 6.6 %collective-permute-start.13 = (bf16[2,128,512]{2,1,0:T(8,128)(2,1)S(1)}, bf16[2,128,512]{2,1,0:T(8,128)(2,1)S(1)}, u32[]{:S(2)}, u32[]{:S(2)}) collective-permute-start(bf16[2,128,512]{2,1,0:T(8,128)(2,1)S(1)} %get-tuple-element.81), channel_id=1, source_target_pairs={{0,4},{1,5},{2,6},{3,7},{4,0},{5,1},{6,2},{7,3},{8,12},{9,13},{10,... | collective-permute-start | bytes 786440 | tf_op jit(solution)/shard_map/ppermute | solution.py:22
  28.6 4.4 %collective-permute-start.10 = (bf16[64,2048]{1,0:T(8,128)(2,1)S(1)}, bf16[64,2048]{1,0:T(8,128)(2,1)S(1)}, u32[]{:S(2)}, u32[]{:S(2)}) collective-permute-start(bf16[64,2048]{1,0:T(8,128)(2,1)S(1)} %collective-permute-done.4.refs_0_.refs_6_), channel_id=1, source_target_pairs={{0,1},{1,0},{2,3},{3,2},{4,5},{5,4},{6,7},{7,6},{8,9},{9,8},{10,11... | collective-permute-start | bytes 786440 | tf_op jit(solution)/shard_map/ppermute | solution.py:22
  28.6 4.4 %collective-permute-start.11 = (bf16[64,2048]{1,0:T(8,128)(2,1)S(1)}, bf16[64,2048]{1,0:T(8,128)(2,1)S(1)}, u32[]{:S(2)}, u32[]{:S(2)}) collective-permute-start(bf16[64,2048]{1,0:T(8,128)(2,1)S(1)} %collective-permute-done.5.refs_1_.refs_7_), channel_id=1, source_target_pairs={{0,1},{1,0},{2,3},{3,2},{4,5},{5,4},{6,7},{7,6},{8,9},{9,8},{10,11... | collective-permute-start | bytes 786440 | tf_op jit(solution)/shard_map/ppermute | solution.py:22
  34.0 9.6 %collective-permute-start.15 = (bf16[2,128,512]{2,1,0:T(8,128)(2,1)S(1)}, bf16[2,128,512]{2,1,0:T(8,128)(2,1)S(1)}, u32[]{:S(2)}, u32[]{:S(2)}) collective-permute-start(bf16[2,128,512]{2,1,0:T(8,128)(2,1)S(1)} %get-tuple-element.85), channel_id=1, source_target_pairs={{0,6},{1,7},{2,4},{3,5},{4,2},{5,3},{6,0},{7,1},{8,14},{9,15},{10,... | collective-permute-start | bytes 786440 | tf_op jit(solution)/shard_map/ppermute | solution.py:22
  34.4 12.5 %collective-permute-start.16 = (bf16[512,128]{1,0:T(8,128)(2,1)S(1)}, bf16[512,128]{1,0:T(8,128)(2,1)S(1)}, u32[]{:S(2)}, u32[]{:S(2)}) collective-permute-start(bf16[512,128]{1,0:T(8,128)(2,1)S(1)} %get-tuple-element.70.refs_6_.refs_4_.w0), channel_id=1, source_target_pairs={{0,1},{1,0},{2,3},{3,2},{4,5},{5,4},{6,7},{7,6},{8,9},{9,8},{10,11... | collective-permute-start | bytes 393224 | tf_op jit(solution)/shard_map/ppermute | solution.py:22
  34.6 12.4 %collective-permute-start.17 = (bf16[512,128]{1,0:T(8,128)(2,1)S(1)}, bf16[512,128]{1,0:T(8,128)(2,1)S(1)}, u32[]{:S(2)}, u32[]{:S(2)}) collective-permute-start(bf16[512,128]{1,0:T(8,128)(2,1)S(1)} %collective-permute-done.2.refs_7_.refs_5_.w1), channel_id=1, source_target_pairs={{0,1},{1,0},{2,3},{3,2},{4,5},{5,4},{6,7},{7,6},{8,9},{9,8},{10,11... | collective-permute-start | bytes 393224 | tf_op jit(solution)/shard_map/ppermute | solution.py:22
  34.9 12.0 %collective-permute-start.18 = (bf16[512,128]{1,0:T(8,128)(2,1)S(1)}, bf16[512,128]{1,0:T(8,128)(2,1)S(1)}, u32[]{:S(2)}, u32[]{:S(2)}) collective-permute-start(bf16[512,128]{1,0:T(8,128)(2,1)S(1)} %collective-permute-done.3.refs_8_.refs_6_.w2), channel_id=1, source_target_pairs={{0,1},{1,0},{2,3},{3,2},{4,5},{5,4},{6,7},{7,6},{8,9},{9,8},{10,11... | collective-permute-start | bytes 393224 | tf_op jit(solution)/shard_map/ppermute | solution.py:22
  35.5 11.4 %collective-permute-start.19 = (bf16[512,128]{1,0:T(8,128)(2,1)S(1)}, bf16[512,128]{1,0:T(8,128)(2,1)S(1)}, u32[]{:S(2)}, u32[]{:S(2)}) collective-permute-start(bf16[512,128]{1,0:T(8,128)(2,1)S(1)} %collective-permute-done.9.refs_9_.refs_7_.w3), channel_id=1, source_target_pairs={{0,1},{1,0},{2,3},{3,2},{4,5},{5,4},{6,7},{7,6},{8,9},{9,8},{10,11... | collective-permute-start | bytes 393224 | tf_op jit(solution)/shard_map/ppermute | solution.py:22
  51.3 20.1 %collective-permute-start.22 = (bf16[2,128,1024]{2,1,0:T(8,128)(2,1)S(1)}, bf16[2,128,1024]{2,1,0:T(8,128)(2,1)S(1)}, u32[]{:S(2)}, u32[]{:S(2)}) collective-permute-start(bf16[2,128,1024]{2,1,0:T(8,128)(2,1)S(1)} %get-tuple-element.109), channel_id=1, source_target_pairs={{0,2},{1,3},{2,0},{3,1},{4,6},{5,7},{6,4},{7,5},{8,10},{9,11},{10,... | collective-permute-start | bytes 1572872 | tf_op jit(solution)/shard_map/ppermute | solution.py:22
  52.8 19.2 %collective-permute-start.23 = (bf16[2,128,1024]{2,1,0:T(8,128)(2,1)S(1)}, bf16[2,128,1024]{2,1,0:T(8,128)(2,1)S(1)}, u32[]{:S(2)}, u32[]{:S(2)}) collective-permute-start(bf16[2,128,1024]{2,1,0:T(8,128)(2,1)S(1)} %get-tuple-element.110), channel_id=1, source_target_pairs={{0,4},{1,5},{2,6},{3,7},{4,0},{5,1},{6,2},{7,3},{8,12},{9,13},{10,... | collective-permute-start | bytes 1572872 | tf_op jit(solution)/shard_map/ppermute | solution.py:22
  55.7 6.6 %collective-permute-start.24 = (bf16[512,128]{1,0:T(8,128)(2,1)S(1)}, bf16[512,128]{1,0:T(8,128)(2,1)S(1)}, u32[]{:S(2)}, u32[]{:S(2)}) collective-permute-start(bf16[512,128]{1,0:T(8,128)(2,1)S(1)} %get-tuple-element.112), channel_id=1, source_target_pairs={{0,8},{8,0},{16,24},{24,16},{1,9},{9,1},{17,25},{25,17},{2,10},{10... | collective-permute-start | bytes 393224 | tf_op jit(solution)/shard_map/ppermute | solution.py:22
  57.4 12.7 %collective-permute-start.25 = (bf16[512,128]{1,0:T(8,128)(2,1)S(1)}, bf16[512,128]{1,0:T(8,128)(2,1)S(1)}, u32[]{:S(2)}, u32[]{:S(2)}) collective-permute-start(bf16[512,128]{1,0:T(8,128)(2,1)S(1)} %get-tuple-element.113), channel_id=1, source_target_pairs={{0,16},{8,24},{16,0},{24,8},{1,17},{9,25},{17,1},{25,9},{2,18},{10... | collective-permute-start | bytes 393224 | tf_op jit(solution)/shard_map/ppermute | solution.py:22
  60.0 10.6 %collective-permute-start.26 = (bf16[512,128]{1,0:T(8,128)(2,1)S(1)}, bf16[512,128]{1,0:T(8,128)(2,1)S(1)}, u32[]{:S(2)}, u32[]{:S(2)}) collective-permute-start(bf16[512,128]{1,0:T(8,128)(2,1)S(1)} %get-tuple-element.114), channel_id=1, source_target_pairs={{0,24},{8,16},{16,8},{24,0},{1,25},{9,17},{17,9},{25,1},{2,26},{10... | collective-permute-start | bytes 393224 | tf_op jit(solution)/shard_map/ppermute | solution.py:22
  62.3 12.4 %collective-permute-start.32 = (bf16[2,128,512]{2,1,0:T(8,128)(2,1)S(1)}, bf16[2,128,512]{2,1,0:T(8,128)(2,1)S(1)}, u32[]{:S(2)}, u32[]{:S(2)}) collective-permute-start(bf16[2,128,512]{2,1,0:T(8,128)(2,1)S(1)} %get-tuple-element.119), channel_id=1, source_target_pairs={{0,6},{1,7},{2,4},{3,5},{4,2},{5,3},{6,0},{7,1},{8,14},{9,15},{10,... | collective-permute-start | bytes 786440 | tf_op jit(solution)/shard_map/ppermute | solution.py:22
  70.1 8.2 %collective-permute-start.30 = (bf16[2,128,512]{2,1,0:T(8,128)(2,1)S(1)}, bf16[2,128,512]{2,1,0:T(8,128)(2,1)S(1)}, u32[]{:S(2)}, u32[]{:S(2)}) collective-permute-start(bf16[2,128,512]{2,1,0:T(8,128)(2,1)S(1)} %get-tuple-element.117), channel_id=1, source_target_pairs={{0,2},{1,3},{2,0},{3,1},{4,6},{5,7},{6,4},{7,5},{8,10},{9,11},{10,... | collective-permute-start | bytes 786440 | tf_op jit(solution)/shard_map/ppermute | solution.py:22
  70.6 10.0 %collective-permute-start.31 = (bf16[2,128,512]{2,1,0:T(8,128)(2,1)S(1)}, bf16[2,128,512]{2,1,0:T(8,128)(2,1)S(1)}, u32[]{:S(2)}, u32[]{:S(2)}) collective-permute-start(bf16[2,128,512]{2,1,0:T(8,128)(2,1)S(1)} %get-tuple-element.118), channel_id=1, source_target_pairs={{0,4},{1,5},{2,6},{3,7},{4,0},{5,1},{6,2},{7,3},{8,12},{9,13},{10,... | collective-permute-start | bytes 786440 | tf_op jit(solution)/shard_map/ppermute | solution.py:22
  72.2 17.3 %collective-permute-start.33 = (bf16[128,1024]{1,0:T(8,128)(2,1)S(1)}, bf16[128,1024]{1,0:T(8,128)(2,1)S(1)}, u32[]{:S(2)}, u32[]{:S(2)}) collective-permute-start(bf16[128,1024]{1,0:T(8,128)(2,1)S(1)} %get-tuple-element.129), channel_id=1, source_target_pairs={{0,4},{1,5},{2,6},{3,7},{4,0},{5,1},{6,2},{7,3},{8,12},{9,13},{10,... | collective-permute-start | bytes 786440 | tf_op jit(solution)/shard_map/ppermute | solution.py:22
  74.7 8.6 %collective-permute-start.27 = (bf16[512,128]{1,0:T(8,128)(2,1)S(1)}, bf16[512,128]{1,0:T(8,128)(2,1)S(1)}, u32[]{:S(2)}, u32[]{:S(2)}) collective-permute-start(bf16[512,128]{1,0:T(8,128)(2,1)S(1)} %last_kernel.1.refs_0_), channel_id=1, source_target_pairs={{0,2},{1,3},{2,0},{3,1},{4,6},{5,7},{6,4},{7,5},{8,10},{9,11},{10,... | collective-permute-start | bytes 393224 | tf_op jit(solution)/shard_map/ppermute | solution.py:22
  74.7 14.2 %collective-permute-start.28 = (bf16[512,128]{1,0:T(8,128)(2,1)S(1)}, bf16[512,128]{1,0:T(8,128)(2,1)S(1)}, u32[]{:S(2)}, u32[]{:S(2)}) collective-permute-start(bf16[512,128]{1,0:T(8,128)(2,1)S(1)} %last_kernel.1.refs_0_), channel_id=1, source_target_pairs={{0,4},{1,5},{2,6},{3,7},{4,0},{5,1},{6,2},{7,3},{8,12},{9,13},{10,... | collective-permute-start | bytes 393224 | tf_op jit(solution)/shard_map/ppermute | solution.py:22
  78.3 10.7 %collective-permute-start.29 = (bf16[512,128]{1,0:T(8,128)(2,1)S(1)}, bf16[512,128]{1,0:T(8,128)(2,1)S(1)}, u32[]{:S(2)}, u32[]{:S(2)}) collective-permute-start(bf16[512,128]{1,0:T(8,128)(2,1)S(1)} %last_kernel.1.refs_0_), channel_id=1, source_target_pairs={{0,6},{1,7},{2,4},{3,5},{4,2},{5,3},{6,0},{7,1},{8,14},{9,15},{10,... | collective-permute-start | bytes 393224 | tf_op jit(solution)/shard_map/ppermute | solution.py:22
  80.6 9.4 %collective-permute-start.34 = (bf16[128,1024]{1,0:T(8,128)(2,1)S(1)}, bf16[128,1024]{1,0:T(8,128)(2,1)S(1)}, u32[]{:S(2)}, u32[]{:S(2)}) collective-permute-start(bf16[128,1024]{1,0:T(8,128)(2,1)S(1)} %get-tuple-element.131), channel_id=1, source_target_pairs={{0,2},{1,3},{2,0},{3,1},{4,6},{5,7},{6,4},{7,5},{8,10},{9,11},{10,... | collective-permute-start | bytes 786440 | tf_op jit(solution)/shard_map/ppermute | solution.py:22
  (8 other events, 22.8 us)

commit v5 on v4

--- a/solution.py
+++ b/solution.py
@@ -30,7 +30,7 @@
     return pltpu.VMEM(shape, dtype)
 
 
-def run(body, outs, scalars, arrays, scratch=(), room=16):
+def run(body, outs, scalars, arrays, scratch=(), room=16, aliases={}):
     arrays = [pltpu.with_memory_space_constraint(v, pltpu.VMEM) for v in arrays]
     return pl.pallas_call(
         body,
@@ -41,6 +41,7 @@
             lambda _: pl.BlockSpec(memory_space=pltpu.VMEM), outs, is_leaf=lambda v: hasattr(v, "dtype")
         ),
         scratch_shapes=scratch,
+        input_output_aliases=aliases,
         compiler_params=pltpu.CompilerParams(vmem_limit_bytes=room << 20),
         name=getattr(body, "func", body).__name__,
     )(*scalars, *arrays)
@@ -141,32 +142,26 @@
     )(ids, *(both * 4))
 
 
-def attend_kernel(rels, docs, first_call, last_call, ids, lens, mine, got, *refs):
+def attend_kernel(rels, docs, first_call, last_call, ids, lens, *refs):
     count = len(rels)
-    qgs, refs = refs[:count], refs[count:]
-    if not first_call:
-        dk_in, dv_in = refs[:2]
-        refs = refs[2:]
-    outs, refs = refs[:count], refs[count:]
-    if last_call:
-        own, send, *refs = refs
-    dk, dv, key, val, key_t, val_t = refs
     m, c = ids[0], ids[1]
+    is_key = c == 0
+    if first_call:
+        mine, got, *refs = refs
+        qgs, outs, (dk, dv, key, val) = refs[:count], refs[count : 2 * count], refs[2 * count :]
+        key[...] = jnp.where(is_key, mine[...], got[...])
+        val[...] = jnp.where(is_key, got[...], mine[...])
+        dk[...] = jnp.zeros_like(dk)
+        dv[...] = jnp.zeros_like(dv)
+    elif last_call:
+        dk, dv, key, val, *refs = refs
+        qgs, outs, (own, keep, send) = refs[:count], refs[count : 2 * count], refs[2 * count :]
+    else:
+        _, _, key, val, *refs = refs
+        qgs, outs, (dk, dv) = refs[:count], refs[count : 2 * count], refs[2 * count :]
     rows = qgs[0].shape[1]
-    keys = mine.shape[0]
     heads = HEADS // KV_HEADS
     inv = HEAD_DIM ** (-0.5)
-    is_key = c == 0
-    key[...] = jnp.where(is_key, mine[...], got[...])
-    val[...] = jnp.where(is_key, got[...], mine[...])
-    key_t[...] = key[...].T
-    val_t[...] = val[...].T
-    if first_call:
-        dk[...] = jnp.zeros_like(dk)
-        dv[...] = jnp.zeros_like(dv)
-    else:
-        dk[...] = dk_in[...]
-        dv[...] = dv_in[...]
 
     def body(i, shard, begin, shards):
         span = shard_rows(begin, rows, shards)
@@ -181,30 +176,24 @@
             kdoc = kdoc + (kpos >= end).astype(jnp.int32)
             qdoc = qdoc + (qpos >= end).astype(jnp.int32)
         bias = jnp.where((kdoc == qdoc) & (kpos <= qpos), 0.0, NEG_FILL)
-        bias = jnp.concatenate([bias, bias], axis=1)
-        k, v, k_t, v_t = key[span, :], val[span, :], key_t[:, span], val_t[:, span]
-        grads_k, grads_v = [], []
-        for h in range(0, heads, 2):
-            cols = [slice((h + e) * HEAD_DIM, (h + e + 1) * HEAD_DIM) for e in range(2)]
-            q = jnp.concatenate([qgs[i][0, :, at] for at in cols], axis=0)
-            g = jnp.concatenate([qgs[i][1, :, at] for at in cols], axis=0)
-            s = dot(k, q, 1, 1) * inv + bias
-            p = jnp.exp(s - jnp.max(s, axis=0, keepdims=True))
-            p = p * (1.0 / jnp.sum(p, axis=0, keepdims=True))
-            low = p.astype(BF16)
-            out_t = dot(v_t, low, 1, 0).astype(BF16).astype(F32)
-            delta = jnp.sum(out_t * g.astype(F32).T, axis=0, keepdims=True)
-            ds = (p * (dot(v, g, 1, 1) - delta)).astype(BF16)
-            dq_t = dot(k_t, ds, 1, 0) * inv
-            grads_k.append(dot(ds, q, 1, 0))
-            grads_v.append(dot(low, g, 1, 0))
-            out = out_t.T.astype(BF16)
-            dq = dq_t.T.astype(BF16)
-            for e, at in enumerate(cols):
-                outs[i][0, :, at] = out[e * rows : (e + 1) * rows]
-                outs[i][1, :, at] = dq[e * rows : (e + 1) * rows]
-        dk[span, :] = dk[span, :] + (grads_k[0] + grads_k[1]) * inv
-        dv[span, :] = dv[span, :] + (grads_v[0] + grads_v[1])
+        bias = jnp.concatenate([bias] * heads, axis=1)
+        cols = [slice(h * HEAD_DIM, (h + 1) * HEAD_DIM) for h in range(heads)]
+        k, v = key[span, :], val[span, :]
+        q = jnp.concatenate([qgs[i][0, :, at] for at in cols], axis=0)
+        g = jnp.concatenate([qgs[i][1, :, at] for at in cols], axis=0)
+        s = dot(k, q, 1, 1) * inv + bias
+        p = jnp.exp(s - jnp.max(s, axis=0, keepdims=True))
+        p = p * (1.0 / jnp.sum(p, axis=0, keepdims=True))
+        low = p.astype(BF16)
+        out = dot(low, v, 0, 0).astype(BF16)
+        delta = jnp.sum(out.astype(F32).T * g.astype(F32).T, axis=0, keepdims=True)
+        ds = (p * (dot(v, g, 1, 1) - delta)).astype(BF16)
+        dq = (dot(ds, k, 0, 0) * inv).astype(BF16)
+        dk[span, :] = dk[span, :] + dot(ds, q, 1, 0) * inv
+        dv[span, :] = dv[span, :] + dot(low, g, 1, 0)
+        for h, at in enumerate(cols):
+            outs[i][0, :, at] = out[h * rows : (h + 1) * rows]
+            outs[i][1, :, at] = dq[h * rows : (h + 1) * rows]
 
     for i, r in enumerate(rels):
         chip = jnp.bitwise_xor(m, r)
@@ -220,23 +209,35 @@
 
     if last_call:
         own[...] = jnp.where(is_key, dk[...], dv[...])
-        send[...] = jnp.where(is_key, dv[...], dk[...]).astype(BF16)
-
-
-def attend(rels, ids, lens, mine, got, qgs, sums=(), last=False):
-    keys = mine.shape[0]
-    total = (keys, HEAD_DIM)
-    wide, tall = pltpu.VMEM(total, BF16), pltpu.VMEM((HEAD_DIM, keys), BF16)
-    sides = (on_chip(total, F32), on_chip(total) if last else on_chip(total, F32))
-    *outs, first, second = run(
-        functools.partial(attend_kernel, rels, lens.shape[1], not sums, last),
-        tuple(on_chip(v.shape) for v in qgs) + sides,
+        size = own.shape[0]
+        send[:size, :] = jnp.where(is_key, dv[...], dk[...]).astype(BF16)
+        for chip in range(4):
+            at = slice(chip * rows, (chip + 1) * rows)
+            mine, theirs = shard_rows(2 * chip + c, rows), shard_rows(2 * chip + 1 - c, rows)
+            keep[at, :] = jnp.where(is_key, dv[mine, :], dk[mine, :])
+            send[size + chip * rows : size + (chip + 1) * rows, :] = own[theirs, :].astype(BF16)
+
+
+def attend(rels, ids, lens, state, qgs, last=False):
+    first = len(state) == 2
+    total = (state[0].shape[0], HEAD_DIM)
+    sums = (on_chip(total, F32), on_chip(total, F32))
+    if last:
+        part = total[0] // 2
+        sums = (on_chip(total, F32), on_chip((part, HEAD_DIM), F32), on_chip((total[0] + part, HEAD_DIM)))
+    if first:
+        sums = sums + (on_chip(total), on_chip(total))
+    count = len(rels)
+    results = run(
+        functools.partial(attend_kernel, rels, lens.shape[1], first, last),
+        tuple(on_chip(v.shape) for v in qgs) + sums,
         (ids, lens),
-        (mine, got, *qgs, *sums),
-        scratch=([pltpu.VMEM(total, F32)] * 2 if last else []) + [wide, wide, tall, tall],
+        (*state, *qgs),
         room=24,
-    )
-    return outs, (first, second)
+        aliases={} if first or last else {2: count, 3: count + 1},
+    )
+    outs, state_out = results[:count], results[count:]
+    return outs, (state_out if first or last else (*state_out, *state[2:]))
 
 
 def place_kernel(ids, p0, p1, p2, p3, out, dq):
@@ -252,23 +253,16 @@
     return dot(g_t, x, 1, 0).T
 
 
-def sum_kernel(ids, mine, got, own, oth):
-    m, c = ids[0], ids[1]
-    rows = own.shape[1]
+def weight_kernel(ids, mine, got, *refs):
+    *xs, keep, send1, send2, send3, g_t = refs
+    m, c, z = ids[0], ids[1], ids[2]
+    rows = g_t.shape[1] // 8
     for r in range(4):
         chip = jnp.bitwise_xor(m, r)
-        for core, out in ((c, own), (1 - c, oth)):
+        for e, core in enumerate((c, 1 - c)):
             span = shard_rows(2 * chip + core, rows)
-            out[r] = (mine[span, :] + got[span, :].astype(F32)).astype(BF16)
-
-
-def weight_kernel(ids, own, oth, *refs):
-    *xs, keep, send1, send2, send3, g_t = refs
-    z = ids[2]
-    rows = own.shape[1]
-    for r in range(4):
-        g_t[:, 2 * r * rows : (2 * r + 1) * rows] = own[r].T
-        g_t[:, (2 * r + 1) * rows : (2 * r + 2) * rows] = oth[r].T
+            g = (mine[span, :] + got[span, :].astype(F32)).astype(BF16)
+            g_t[:, (2 * r + e) * rows : (2 * r + e + 1) * rows] = g.T
     for r, send in ((3, send3), (2, send2), (1, send1)):
         send[...] = weight_block(z, r, g_t[...], xs, send.shape[0]).astype(BF16)
     keep[...] = weight_block(z, 0, g_t[...], xs, keep.shape[0])
@@ -279,26 +273,36 @@
     later[...] = (keep[1] + got[1].astype(F32)).astype(BF16)
 
 
-def last_kernel(keep, got1, got2, got3, out):
-    got = (got1[...].astype(F32) + got2[...].astype(F32)) + got3[...].astype(F32)
-    out[...] = (keep[...] + got).astype(BF16)
+def add_kernel(keep, got, out):
+    out[...] = keep[...] + got[...].astype(F32)
+
+
+def last_kernel(keep, got1, got2, out):
+    out[...] = (keep[...] + (got1[...].astype(F32) + got2[...].astype(F32))).astype(BF16)
 
 
 def assemble_kernel(ids, *refs):
     m, c = ids[0], ids[1]
     out = refs[-1]
-    for side in range(2):
-        core = c if side == 0 else 1 - c
+    for side, core in enumerate((c, 1 - c)):
         for r in range(4):
             col = pl.multiple_of(column_of(jnp.bitwise_xor(m, r), core), HEAD_DIM)
             out[:, pl.ds(col, HEAD_DIM)] = refs[4 * side + r][...].astype(F32)
 
 
-def token_kernel(own, oth, w0, w1, w2, w3, u0, u1, u2, u3, send_a, send_b, keep_a, keep_b):
-    rows = own.shape[1]
-    g = jnp.concatenate(
-        [jnp.concatenate([own[r] for r in range(4)], axis=0),
-         jnp.concatenate([oth[r] for r in range(4)], axis=0)], axis=1)
+def token_kernel(ids, mine, kept, got, w0, w1, w2, w3, u0, u1, u2, u3,
+                 send_a, send_b, keep_a, keep_b):
+    m, c = ids[0], ids[1]
+    size = mine.shape[0]
+    rows = size // 8
+    parts = []
+    for r in range(4):
+        chip = jnp.bitwise_xor(m, r)
+        span = shard_rows(2 * chip + c, rows)
+        own = mine[span, :] + got[span, :].astype(F32)
+        oth = kept[shard_rows(chip, rows), :] + got[shard_rows(8 + chip, rows), :].astype(F32)
+        parts.append(jnp.concatenate([own, oth], axis=1).astype(BF16))
+    g = jnp.concatenate(parts, axis=0)
     ws = (w0[...], w1[...], w2[...], w3[...])
     us = (u0[...], u1[...], u2[...], u3[...])
     size = w0.shape[0]
@@ -344,61 +348,61 @@
     w3 = swap(w2, "fsdp", 1)
     ws = (w0, w1, w2, w3)
     half = on_chip((rows // 2, width))
+    p0, *away = cut_heads(ids, queries, out_grad)
+    x1, x2, *away = lax.optimization_barrier((x1, x2, *away))
+    p1, p2, p3 = away
     top, low = run(cut_kernel, (half, half), (), (x1, x2))
     x3 = [far(top), near(low)]
     flip = lambda vs: [pair(v) for v in vs]
     early = (x0, pair(x0), x1, pair(x1), x2, pair(x2))
+    p1, p2 = near(p1), far(p2)
     first = run(project_kernel, on_chip((6 * rows, HEAD_DIM)), (ids,), early + ws)
     *x3, first = lax.optimization_barrier((*x3, first))
     us = tuple(flip(ws))
-    p0, *away = cut_heads(ids, queries, out_grad)
-    p1, p2, p3 = away
-    p1, p2 = near(p1), far(p2)
     late = (*x3, *flip(x3))
     xs = early + late
     p1, p2, p3, first = lax.optimization_barrier((p1, p2, p3, first))
     mine = run(order_kernel, on_chip((8 * rows, HEAD_DIM)), (ids,), late + ws + (first,))
     p3 = cross(p3)
     got = pair(mine)
-    (o0,), sums = attend((0,), ids, doc_lengths, mine, got, (p0,))
-    p1, p2, *sums = lax.optimization_barrier((p1, p2, *sums))
-    (o1, o2), sums = attend((1, 2), ids, doc_lengths, mine, got, (p1, p2), sums)
+    (o0,), state = attend((0,), ids, doc_lengths, (mine, got), (p0,))
+    p1, p2, *state = lax.optimization_barrier((p1, p2, *state))
+    (o1, o2), state = attend((1, 2), ids, doc_lengths, state, (p1, p2))
     o1, o2 = near(o1), far(o2)
-    p3, *sums = lax.optimization_barrier((p3, *sums))
-    (o3,), (g_mine, g_send) = attend((3,), ids, doc_lengths, mine, got, (p3,), sums, True)
+    p3, *state = lax.optimization_barrier((p3, *state))
+    (o3,), (g_mine, g_keep, g_send) = attend((3,), ids, doc_lengths, state, (p3,), True)
     g_send, us = lax.optimization_barrier((g_send, us))
     g_got = pair(g_send)
     o3 = cross(o3)
 
-    block = on_chip((4, rows, HEAD_DIM))
     third = on_chip((size, HEAD_DIM))
-    g_own, g_oth = run(sum_kernel, (block, block), (ids,), (g_mine, g_got))
-    g_got = pair(g_oth)
     half = (rows, width // 2)
     send_a, send_b, keep_a, keep_b = run(
         token_kernel,
         (on_chip((2, *half)), on_chip((2, *half)), on_chip((2, *half), F32), on_chip((2, *half), F32)),
-        (),
-        (g_own, g_got) + ws + us,
+        (ids,),
+        (g_mine, g_keep, g_got) + ws + us,
     )
     got_a, got_b = near(send_a), far(send_b)
     keep, *sends = run(
         weight_kernel,
         (on_chip((size, HEAD_DIM), F32), third, third, third),
         (ids,),
-        (g_own, g_oth) + xs,
+        (g_mine, g_got) + xs,
         scratch=[pltpu.VMEM((HEAD_DIM, 8 * rows), BF16)],
     )
     gots = [swap(v, "fsdp", bit) for v, bit in zip(sends, (1, 2, 3))]
-    mine = run(last_kernel, on_chip((size, HEAD_DIM)), (), (keep, *gots))
+    keep = run(add_kernel, on_chip((size, HEAD_DIM), F32), (), (keep, gots[0]))
+    mine = run(last_kernel, on_chip((size, HEAD_DIM)), (), (keep, *gots[1:]))
     got_a, got_b, mine = lax.optimization_barrier((got_a, got_b, mine))
     fold = (on_chip(half, F32), on_chip(half))
     a, a_send, b, b_send = run(fold_both_kernel, fold + fold, (), (keep_a, got_a, keep_b, got_b))
     got_a, got_b = far(a_send), near(b_send)
     like = jax.ShapeDtypeStruct(queries.shape, BF16)
+    mine = [mine, near(mine), far(mine), cross(mine)]
+    mine[1], o1, o2, o3 = lax.optimization_barrier((mine[1], o1, o2, o3))
     attn_out, grad_queries = run(place_kernel, (like, like), (ids,), (o0, o1, o2, o3))
-    mine = [mine, near(mine), far(mine), cross(mine)]
-    *mine, attn_out, grad_queries = lax.optimization_barrier((*mine, attn_out, grad_queries))
+    mine[2], mine[3], attn_out, grad_queries = lax.optimization_barrier((mine[2], mine[3], attn_out, grad_queries))
     theirs = [pair(v) for v in mine]
     grad_weight = run(
         assemble_kernel,

time: 93.8 us -> 90.7 us (0.967)
  waiting for transfers between devices: 33.3 us -> 31.1 us
  Pallas kernels: 25.5 us -> 23.6 us
  starting transfers between devices: 34 us -> 35 us
    ppermute x39 -> x38, waiting for transfers between devices: 33.3 us -> 31.1 us  [swap(): return lax.ppermute(value, axis, [(i, i ^ bit) for i in range(count)])]
    pallas_call x14, Pallas kernels: 21.9 us -> 20 us  [run(): pl.pallas_call(body, out_shape=outs, in_specs=[pl.BlockSpec(memory_space=...]
    ppermute x39 -> x38, starting transfers between devices: 34 us -> 35 us  [swap(): return lax.ppermute(value, axis, [(i, i ^ bit) for i in range(count)])]
  transfers between devices with their start and end apart: 39 -> 38, of which waited for: 15 -> 14; matrix products, arithmetic and copies ran while one was open for 0% -> 0% of each run, Pallas kernels for 22% -> 21%
where the time goes in v5:
time: 90.7 us; the launch traced here: 90.6 us
  starting transfers between devices  35 us (39%)
  waiting for transfers between devices  31.1 us (34%)
  Pallas kernels  23.6 us (26%)
    ppermute x38, starting transfers between devices, swap(): return lax.ppermute(value, axis, [(i, i ^ bit) for i in range(count)])  35 us
    ppermute x38, waiting for transfers between devices, swap(): return lax.ppermute(value, axis, [(i, i ^ bit) for i in range(count)])  31.1 us
    pallas_call x14, Pallas kernels, run(): pl.pallas_call(body, out_shape=outs, in_specs=[pl.BlockSpec(memory_space=...  20 us
    pallas_call x1, Pallas kernels, cut_heads(): pl.pallas_call(cut_heads_kernel, out_shape=(on_chip((2, rows, width)),) *...  1.9 us
  transfers between devices with their start and end apart: 38, of which 14 were waited for; matrix products, arithmetic and copies ran while one was open for 0% of the time, Pallas kernels for 21%

profile of v5, /device:TPU:0, one launch (start us, length us, event | category | flops | bytes accessed | tf_op | source)
XLA Modules:
  0.0 90.6 jit_solution(3182165856877663038)
XLA Ops:
  0.6 3.0 %collective-permute-start = (bf16[128,2048]{1,0:T(8,128)(2,1)}, bf16[128,2048]{1,0:T(8,128)(2,1)S(1)}, u32[]{:S(2)}, u32[]{:S(2)}) collective-permute-start(bf16[128,2048]{1,0:T(8,128)(2,1)} %x.1), channel_id=1, source_target_pairs={{0,2},{1,3},{2,0},{3,1},{4,6},{5,7},{6,4},{7,5},{8,10},{9,11},{10,... | collective-permute-start | bytes 1572872 | tf_op jit(solution)/shard_map/ppermute | solution.py:22
  3.7 1.5 %collective-permute-start.1 = (bf16[128,2048]{1,0:T(8,128)(2,1)}, bf16[128,2048]{1,0:T(8,128)(2,1)S(1)}, u32[]{:S(2)}, u32[]{:S(2)}) collective-permute-start(bf16[128,2048]{1,0:T(8,128)(2,1)} %x.1), channel_id=1, source_target_pairs={{0,4},{1,5},{2,6},{3,7},{4,0},{5,1},{6,2},{7,3},{8,12},{9,13},{10,... | collective-permute-start | bytes 1572872 | tf_op jit(solution)/shard_map/ppermute | solution.py:22
  5.3 1.7 %prep_kernel.1 = (bf16[512,128]{1,0:T(8,128)(2,1)S(1)}, bf16[128,2048]{1,0:T(8,128)(2,1)S(1)}) custom-call(s32[3]{0:T(128)S(1)} %pad_add_fusion.ids, s32[1]{0:T(128)} %bitcast.3.block, bf16[512,1024]{1,0:T(8,128)(2,1)} %weight.1, bf16[128,2048]{1,0:T(8,128)(2,1)} %x.1), custom_call_target="tpu_custom_call" | custom-call | tf_op jit(solution)/shard_map/prep_kernel/pallas_call | solution.py:76
  7.0 1.6 %collective-permute-start.2 = (bf16[512,128]{1,0:T(8,128)(2,1)S(1)}, bf16[512,128]{1,0:T(8,128)(2,1)S(1)}, u32[]{:S(2)}, u32[]{:S(2)}) collective-permute-start(bf16[512,128]{1,0:T(8,128)(2,1)S(1)} %get-tuple-element.82.refs_6_.refs_4_.w0), channel_id=1, source_target_pairs={{0,8},{8,0},{16,24},{24,16},{1,9},{9,1},{17,25},{25,17},{2,10},{10... | collective-permute-start | bytes 393224 | tf_op jit(solution)/shard_map/ppermute | solution.py:22
  8.6 2.6 %collective-permute-start.3 = (bf16[512,128]{1,0:T(8,128)(2,1)S(1)}, bf16[512,128]{1,0:T(8,128)(2,1)S(1)}, u32[]{:S(2)}, u32[]{:S(2)}) collective-permute-start(bf16[512,128]{1,0:T(8,128)(2,1)S(1)} %get-tuple-element.82.refs_6_.refs_4_.w0), channel_id=1, source_target_pairs={{0,16},{8,24},{16,0},{24,8},{1,17},{9,25},{17,1},{25,9},{2,18},{10... | collective-permute-start | bytes 393224 | tf_op jit(solution)/shard_map/ppermute | solution.py:22
  11.2 1.9 %cut_heads_kernel.1 = (bf16[2,128,512]{2,1,0:T(8,128)(2,1)S(1)}, bf16[2,128,512]{2,1,0:T(8,128)(2,1)S(1)}, bf16[2,128,512]{2,1,0:T(8,128)(2,1)S(1)}, bf16[2,128,512]{2,1,0:T(8,128)(2,1)S(1)}) custom-call(s32[3]{0:T(128)S(1)} %pad_add_fusion.ids, bf16[128,2048]{1,0:T(8,128)(2,1)} %refs_6_.1, bf16[128,2048]{1,0:T(8,128)(2,1)} %refs_7_.1, ...), custom_call_target="tpu_custom_call" | custom-call | tf_op jit(solution)/shard_map/cut_heads_kernel/pallas_call | solution.py:128
  13.7 3.0 %collective-permute-done.3.refs_8_.refs_6_.w2 = bf16[512,128]{1,0:T(8,128)(2,1)S(1)} collective-permute-done((bf16[512,128]{1,0:T(8,128)(2,1)S(1)}, bf16[512,128]{1,0:T(8,128)(2,1)S(1)}, u32[]{:S(2)}, u32[]{:S(2)}) %collective-permute-start.3) | collective-permute-done | bytes 131104 | tf_op jit(solution)/shard_map/ppermute | solution.py:22
  17.8 1.6 %collective-permute-start.6 = (bf16[64,2048]{1,0:T(8,128)(2,1)S(1)}, bf16[64,2048]{1,0:T(8,128)(2,1)S(1)}, u32[]{:S(2)}, u32[]{:S(2)}) collective-permute-start(bf16[64,2048]{1,0:T(8,128)(2,1)S(1)} %get-tuple-element.93), channel_id=1, source_target_pairs={{0,4},{1,5},{2,6},{3,7},{4,0},{5,1},{6,2},{7,3},{8,12},{9,13},{10,... | collective-permute-start | bytes 786440 | tf_op jit(solution)/shard_map/ppermute | solution.py:22
  19.9 1.6 %collective-permute-start.11 = (bf16[512,128]{1,0:T(8,128)(2,1)S(1)}, bf16[512,128]{1,0:T(8,128)(2,1)S(1)}, u32[]{:S(2)}, u32[]{:S(2)}) collective-permute-start(bf16[512,128]{1,0:T(8,128)(2,1)S(1)} %collective-permute-done.3.refs_8_.refs_6_.w2), channel_id=1, source_target_pairs={{0,8},{8,0},{16,24},{24,16},{1,9},{9,1},{17,25},{25,17},{2,10},{10... | collective-permute-start | bytes 393224 | tf_op jit(solution)/shard_map/ppermute | solution.py:22
  21.5 3.4 %collective-permute-done.11.refs_9_.refs_7_.w3 = bf16[512,128]{1,0:T(8,128)(2,1)S(1)} collective-permute-done((bf16[512,128]{1,0:T(8,128)(2,1)S(1)}, bf16[512,128]{1,0:T(8,128)(2,1)S(1)}, u32[]{:S(2)}, u32[]{:S(2)}) %collective-permute-start.11) | collective-permute-done | bytes 131104 | tf_op jit(solution)/shard_map/ppermute | solution.py:22
  24.9 1.5 %collective-permute-start.4 = (bf16[2,128,512]{2,1,0:T(8,128)(2,1)S(1)}, bf16[2,128,512]{2,1,0:T(8,128)(2,1)S(1)}, u32[]{:S(2)}, u32[]{:S(2)}) collective-permute-start(bf16[2,128,512]{2,1,0:T(8,128)(2,1)S(1)} %get-tuple-element.88), channel_id=1, source_target_pairs={{0,2},{1,3},{2,0},{3,1},{4,6},{5,7},{6,4},{7,5},{8,10},{9,11},{10,... | collective-permute-start | bytes 786440 | tf_op jit(solution)/shard_map/ppermute | solution.py:22
  26.9 1.5 %project_kernel.1.refs_8_ = bf16[768,128]{1,0:T(8,128)(2,1)S(1)} custom-call(s32[3]{0:T(128)S(1)} %pad_add_fusion.ids, bf16[128,2048]{1,0:T(8,128)(2,1)S(1)} %get-tuple-element.95.refs_0_, bf16[128,2048]{1,0:T(8,128)(2,1)S(1)} %collective-permute-done.8.refs_1_, bf16[128,2048]{1,0:T(8,128)(2,1)S(1)} %collective-permute-done.x1.refs_2_, ...), custom_call_target="tpu_custom_call" | custom-call | tf_op jit(solution)/shard_map/project_kernel/pallas_call | solution.py:35
  29.1 3.9 %collective-permute-done.4.refs_4_ = bf16[2,128,512]{2,1,0:T(8,128)(2,1)S(1)} collective-permute-done((bf16[2,128,512]{2,1,0:T(8,128)(2,1)S(1)}, bf16[2,128,512]{2,1,0:T(8,128)(2,1)S(1)}, u32[]{:S(2)}, u32[]{:S(2)}) %collective-permute-start.4) | collective-permute-done | bytes 262176 | tf_op jit(solution)/shard_map/ppermute | solution.py:22
  35.7 1.8 %attend_kernel.3 = (bf16[2,128,512]{2,1,0:T(8,128)(2,1)S(1)}, f32[1024,128]{1,0:T(8,128)S(1)}, f32[1024,128]{1,0:T(8,128)S(1)}, bf16[1024,128]{1,0:T(8,128)(2,1)S(1)}, bf16[1024,128]{1,0:T(8,128)(2,1)S(1)}) custom-call(s32[3]{0:T(128)S(1)} %pad_add_fusion.ids, s32[1,4]{1,0:T(1,128)S(1)} %copy-done, bf16[1024,128]{1,0:T(8,128)(2,1)S(1)} %order_kernel.1.refs_0_, ...), custom_call_target="tpu_custom_call" | custom-call | tf_op jit(solution)/shard_map/attend_kernel/pallas_call | solution.py:35
  37.5 4.6 %attend_kernel.4 = (bf16[2,128,512]{2,1,0:T(8,128)(2,1)S(1)}, bf16[2,128,512]{2,1,0:T(8,128)(2,1)S(1)}, f32[1024,128]{1,0:T(8,128)S(1)}, f32[1024,128]{1,0:T(8,128)S(1)}) custom-call(s32[3]{0:T(128)S(1)} %pad_add_fusion.ids, s32[1,4]{1,0:T(1,128)S(1)} %copy-done, ...), custom_call_target="tpu_custom_call", output_to_operand_aliasing={{2}: (2, {}), {3}: (3, {})} | custom-call | tf_op jit(solution)/shard_map/attend_kernel/pallas_call | solution.py:35
  42.1 1.5 %collective-permute-done.12.refs_4_ = bf16[2,128,512]{2,1,0:T(8,128)(2,1)S(1)} collective-permute-done((bf16[2,128,512]{2,1,0:T(8,128)(2,1)S(1)}, bf16[2,128,512]{2,1,0:T(8,128)(2,1)S(1)}, u32[]{:S(2)}, u32[]{:S(2)}) %collective-permute-start.12) | collective-permute-done | bytes 262176 | tf_op jit(solution)/shard_map/ppermute | solution.py:22
  43.6 2.9 %attend_kernel.5 = (bf16[2,128,512]{2,1,0:T(8,128)(2,1)S(1)}, f32[1024,128]{1,0:T(8,128)S(1)}, f32[512,128]{1,0:T(8,128)S(1)}, bf16[1536,128]{1,0:T(8,128)(2,1)S(1)}) custom-call(s32[3]{0:T(128)S(1)} %pad_add_fusion.ids, s32[1,4]{1,0:T(1,128)S(1)} %copy-done, f32[1024,128]{1,0:T(8,128)S(1)} %get-tuple-element.118.refs_0_, ...), custom_call_target="tpu_custom_call" | custom-call | tf_op jit(solution)/shard_map/attend_kernel/pallas_call | solution.py:35
  46.7 1.7 %collective-permute-done.20.got = bf16[1536,128]{1,0:T(8,128)(2,1)S(1)} collective-permute-done((bf16[1536,128]{1,0:T(8,128)(2,1)S(1)}, bf16[1536,128]{1,0:T(8,128)(2,1)S(1)}, u32[]{:S(2)}, u32[]{:S(2)}) %collective-permute-start.20) | collective-permute-done | bytes 393248 | tf_op jit(solution)/shard_map/ppermute | solution.py:22
  52.6 1.7 %collective-permute-start.23 = (bf16[512,128]{1,0:T(8,128)(2,1)S(1)}, bf16[512,128]{1,0:T(8,128)(2,1)S(1)}, u32[]{:S(2)}, u32[]{:S(2)}) collective-permute-start(bf16[512,128]{1,0:T(8,128)(2,1)S(1)} %get-tuple-element.134), channel_id=1, source_target_pairs={{0,8},{8,0},{16,24},{24,16},{1,9},{9,1},{17,25},{25,17},{2,10},{10... | collective-permute-start | bytes 393224 | tf_op jit(solution)/shard_map/ppermute | solution.py:22
  54.2 2.6 %collective-permute-start.24 = (bf16[512,128]{1,0:T(8,128)(2,1)S(1)}, bf16[512,128]{1,0:T(8,128)(2,1)S(1)}, u32[]{:S(2)}, u32[]{:S(2)}) collective-permute-start(bf16[512,128]{1,0:T(8,128)(2,1)S(1)} %get-tuple-element.135), channel_id=1, source_target_pairs={{0,16},{8,24},{16,0},{24,8},{1,17},{9,25},{17,1},{25,9},{2,18},{10... | collective-permute-start | bytes 393224 | tf_op jit(solution)/shard_map/ppermute | solution.py:22
  57.0 2.2 %collective-permute-done.23.got = bf16[512,128]{1,0:T(8,128)(2,1)S(1)} collective-permute-done((bf16[512,128]{1,0:T(8,128)(2,1)S(1)}, bf16[512,128]{1,0:T(8,128)(2,1)S(1)}, u32[]{:S(2)}, u32[]{:S(2)}) %collective-permute-start.23) | collective-permute-done | bytes 131104 | tf_op jit(solution)/shard_map/ppermute | solution.py:22
  59.2 2.1 %collective-permute-start.31 = (bf16[2,128,512]{2,1,0:T(8,128)(2,1)S(1)}, bf16[2,128,512]{2,1,0:T(8,128)(2,1)S(1)}, u32[]{:S(2)}, u32[]{:S(2)}) collective-permute-start(bf16[2,128,512]{2,1,0:T(8,128)(2,1)S(1)} %get-tuple-element.141), channel_id=1, source_target_pairs={{0,6},{1,7},{2,4},{3,5},{4,2},{5,3},{6,0},{7,1},{8,14},{9,15},{10,... | collective-permute-start | bytes 786440 | tf_op jit(solution)/shard_map/ppermute | solution.py:22
  61.3 5.7 %collective-permute-done.24.got1 = bf16[512,128]{1,0:T(8,128)(2,1)S(1)} collective-permute-done((bf16[512,128]{1,0:T(8,128)(2,1)S(1)}, bf16[512,128]{1,0:T(8,128)(2,1)S(1)}, u32[]{:S(2)}, u32[]{:S(2)}) %collective-permute-start.24) | collective-permute-done | bytes 131104 | tf_op jit(solution)/shard_map/ppermute | solution.py:22
  68.0 1.5 %collective-permute-start.30 = (bf16[2,128,512]{2,1,0:T(8,128)(2,1)S(1)}, bf16[2,128,512]{2,1,0:T(8,128)(2,1)S(1)}, u32[]{:S(2)}, u32[]{:S(2)}) collective-permute-start(bf16[2,128,512]{2,1,0:T(8,128)(2,1)S(1)} %get-tuple-element.140), channel_id=1, source_target_pairs={{0,4},{1,5},{2,6},{3,7},{4,0},{5,1},{6,2},{7,3},{8,12},{9,13},{10,... | collective-permute-start | bytes 786440 | tf_op jit(solution)/shard_map/ppermute | solution.py:22
  70.4 1.8 %collective-permute-start.28 = (bf16[512,128]{1,0:T(8,128)(2,1)S(1)}, bf16[512,128]{1,0:T(8,128)(2,1)S(1)}, u32[]{:S(2)}, u32[]{:S(2)}) collective-permute-start(bf16[512,128]{1,0:T(8,128)(2,1)S(1)} %last_kernel.1.refs_0_), channel_id=1, source_target_pairs={{0,2},{1,3},{2,0},{3,1},{4,6},{5,7},{6,4},{7,5},{8,10},{9,11},{10,... | collective-permute-start | bytes 393224 | tf_op jit(solution)/shard_map/ppermute | solution.py:22
  72.2 1.9 %collective-permute-start.26 = (bf16[512,128]{1,0:T(8,128)(2,1)S(1)}, bf16[512,128]{1,0:T(8,128)(2,1)S(1)}, u32[]{:S(2)}, u32[]{:S(2)}) collective-permute-start(bf16[512,128]{1,0:T(8,128)(2,1)S(1)} %last_kernel.1.refs_0_), channel_id=1, source_target_pairs={{0,4},{1,5},{2,6},{3,7},{4,0},{5,1},{6,2},{7,3},{8,12},{9,13},{10,... | collective-permute-start | bytes 393224 | tf_op jit(solution)/shard_map/ppermute | solution.py:22
  74.1 2.0 %collective-permute-done.29.p1 = bf16[2,128,512]{2,1,0:T(8,128)(2,1)S(1)} collective-permute-done((bf16[2,128,512]{2,1,0:T(8,128)(2,1)S(1)}, bf16[2,128,512]{2,1,0:T(8,128)(2,1)S(1)}, u32[]{:S(2)}, u32[]{:S(2)}) %collective-permute-start.29) | collective-permute-done | bytes 262176 | tf_op jit(solution)/shard_map/ppermute | solution.py:22
  77.3 1.6 %collective-permute-start.33 = (bf16[128,1024]{1,0:T(8,128)(2,1)S(1)}, bf16[128,1024]{1,0:T(8,128)(2,1)S(1)}, u32[]{:S(2)}, u32[]{:S(2)}) collective-permute-start(bf16[128,1024]{1,0:T(8,128)(2,1)S(1)} %get-tuple-element.156), channel_id=1, source_target_pairs={{0,2},{1,3},{2,0},{3,1},{4,6},{5,7},{6,4},{7,5},{8,10},{9,11},{10,... | collective-permute-start | bytes 786440 | tf_op jit(solution)/shard_map/ppermute | solution.py:22
  78.9 1.6 %place_kernel.1 = (bf16[128,2048]{1,0:T(8,128)(2,1)}, bf16[128,2048]{1,0:T(8,128)(2,1)}) custom-call(s32[3]{0:T(128)S(1)} %pad_add_fusion.ids, bf16[2,128,512]{2,1,0:T(8,128)(2,1)S(1)} %get-tuple-element.138.p0, bf16[2,128,512]{2,1,0:T(8,128)(2,1)S(1)} %collective-permute-done.29.p1, bf16[2,128,512]{2,1,0:T(8,128)(2,1)S(1)} %collective-permute-done.30.p2, ...), custom_call_target="tpu_custom_call" | custom-call | tf_op jit(solution)/shard_map/place_kernel/pallas_call | solution.py:35
  80.5 5.9 %collective-permute-done.26.refs_2_ = bf16[512,128]{1,0:T(8,128)(2,1)S(1)} collective-permute-done((bf16[512,128]{1,0:T(8,128)(2,1)S(1)}, bf16[512,128]{1,0:T(8,128)(2,1)S(1)}, u32[]{:S(2)}, u32[]{:S(2)}) %collective-permute-start.26) | collective-permute-done | bytes 131104 | tf_op jit(solution)/shard_map/ppermute | solution.py:22
  87.0 1.4 %token_last_kernel.1 = bf16[128,2048]{1,0:T(8,128)(2,1)} custom-call(s32[3]{0:T(128)S(1)} %pad_add_fusion.ids, f32[128,1024]{1,0:T(8,128)S(1)} %get-tuple-element.153.a, bf16[128,1024]{1,0:T(8,128)(2,1)S(1)} %collective-permute-done.32.got_a, f32[128,1024]{1,0:T(8,128)S(1)} %get-tuple-element.155.b, bf16[128,1024]{1,0:T(8,128)(2,1)S(1)} %collective-permute-done.33.got_b), custom_call_target="tpu_custom_call" | custom-call | tf_op jit(solution)/shard_map/token_last_kernel/pallas_call | solution.py:35
  88.4 2.1 %assemble_kernel.1 = f32[512,1024]{1,0:T(8,128)} custom-call(s32[3]{0:T(128)S(1)} %pad_add_fusion.ids, bf16[512,128]{1,0:T(8,128)(2,1)S(1)} %last_kernel.1.refs_0_, bf16[512,128]{1,0:T(8,128)(2,1)S(1)} %collective-permute-done.28.refs_1_, bf16[512,128]{1,0:T(8,128)(2,1)S(1)} %collective-permute-done.26.refs_2_, ...), custom_call_target="tpu_custom_call" | custom-call | tf_op jit(solution)/shard_map/assemble_kernel/pallas_call | solution.py:35
  (63 shorter events, 14.4 us)
Async XLA Ops:
  0.6 16.1 %collective-permute-start = (bf16[128,2048]{1,0:T(8,128)(2,1)}, bf16[128,2048]{1,0:T(8,128)(2,1)S(1)}, u32[]{:S(2)}, u32[]{:S(2)}) collective-permute-start(bf16[128,2048]{1,0:T(8,128)(2,1)} %x.1), channel_id=1, source_target_pairs={{0,2},{1,3},{2,0},{3,1},{4,6},{5,7},{6,4},{7,5},{8,10},{9,11},{10,... | collective-permute-start | bytes 1572872 | tf_op jit(solution)/shard_map/ppermute | solution.py:22
  3.7 13.6 %collective-permute-start.1 = (bf16[128,2048]{1,0:T(8,128)(2,1)}, bf16[128,2048]{1,0:T(8,128)(2,1)S(1)}, u32[]{:S(2)}, u32[]{:S(2)}) collective-permute-start(bf16[128,2048]{1,0:T(8,128)(2,1)} %x.1), channel_id=1, source_target_pairs={{0,4},{1,5},{2,6},{3,7},{4,0},{5,1},{6,2},{7,3},{8,12},{9,13},{10,... | collective-permute-start | bytes 1572872 | tf_op jit(solution)/shard_map/ppermute | solution.py:22
  7.0 6.8 %collective-permute-start.2 = (bf16[512,128]{1,0:T(8,128)(2,1)S(1)}, bf16[512,128]{1,0:T(8,128)(2,1)S(1)}, u32[]{:S(2)}, u32[]{:S(2)}) collective-permute-start(bf16[512,128]{1,0:T(8,128)(2,1)S(1)} %get-tuple-element.82.refs_6_.refs_4_.w0), channel_id=1, source_target_pairs={{0,8},{8,0},{16,24},{24,16},{1,9},{9,1},{17,25},{25,17},{2,10},{10... | collective-permute-start | bytes 393224 | tf_op jit(solution)/shard_map/ppermute | solution.py:22
  8.6 8.2 %collective-permute-start.3 = (bf16[512,128]{1,0:T(8,128)(2,1)S(1)}, bf16[512,128]{1,0:T(8,128)(2,1)S(1)}, u32[]{:S(2)}, u32[]{:S(2)}) collective-permute-start(bf16[512,128]{1,0:T(8,128)(2,1)S(1)} %get-tuple-element.82.refs_6_.refs_4_.w0), channel_id=1, source_target_pairs={{0,16},{8,24},{16,0},{24,8},{1,17},{9,25},{17,1},{25,9},{2,18},{10... | collective-permute-start | bytes 393224 | tf_op jit(solution)/shard_map/ppermute | solution.py:22
  11.2 8.7 %collective-permute-start.8 = (bf16[128,2048]{1,0:T(8,128)(2,1)S(1)}, bf16[128,2048]{1,0:T(8,128)(2,1)S(1)}, u32[]{:S(2)}, u32[]{:S(2)}) collective-permute-start(bf16[128,2048]{1,0:T(8,128)(2,1)S(1)} %get-tuple-element.95.refs_0_), channel_id=1, source_target_pairs={{0,1},{1,0},{2,3},{3,2},{4,5},{5,4},{6,7},{7,6},{8,9},{9,8},{10,11... | collective-permute-start | bytes 1572872 | tf_op jit(solution)/shard_map/ppermute | solution.py:22
  17.3 9.1 %collective-permute-start.10 = (bf16[128,2048]{1,0:T(8,128)(2,1)S(1)}, bf16[128,2048]{1,0:T(8,128)(2,1)S(1)}, u32[]{:S(2)}, u32[]{:S(2)}) collective-permute-start(bf16[128,2048]{1,0:T(8,128)(2,1)S(1)} %collective-permute-done.1.x2.refs_4_), channel_id=1, source_target_pairs={{0,1},{1,0},{2,3},{3,2},{4,5},{5,4},{6,7},{7,6},{8,9},{9,8},{10,11... | collective-permute-start | bytes 1572872 | tf_op jit(solution)/shard_map/ppermute | solution.py:22
  17.3 9.6 %collective-permute-start.9 = (bf16[128,2048]{1,0:T(8,128)(2,1)S(1)}, bf16[128,2048]{1,0:T(8,128)(2,1)S(1)}, u32[]{:S(2)}, u32[]{:S(2)}) collective-permute-start(bf16[128,2048]{1,0:T(8,128)(2,1)S(1)} %collective-permute-done.x1.refs_2_), channel_id=1, source_target_pairs={{0,1},{1,0},{2,3},{3,2},{4,5},{5,4},{6,7},{7,6},{8,9},{9,8},{10,11... | collective-permute-start | bytes 1572872 | tf_op jit(solution)/shard_map/ppermute | solution.py:22
  17.8 10.6 %collective-permute-start.6 = (bf16[64,2048]{1,0:T(8,128)(2,1)S(1)}, bf16[64,2048]{1,0:T(8,128)(2,1)S(1)}, u32[]{:S(2)}, u32[]{:S(2)}) collective-permute-start(bf16[64,2048]{1,0:T(8,128)(2,1)S(1)} %get-tuple-element.93), channel_id=1, source_target_pairs={{0,4},{1,5},{2,6},{3,7},{4,0},{5,1},{6,2},{7,3},{8,12},{9,13},{10,... | collective-permute-start | bytes 786440 | tf_op jit(solution)/shard_map/ppermute | solution.py:22
  19.4 9.2 %collective-permute-start.7 = (bf16[64,2048]{1,0:T(8,128)(2,1)S(1)}, bf16[64,2048]{1,0:T(8,128)(2,1)S(1)}, u32[]{:S(2)}, u32[]{:S(2)}) collective-permute-start(bf16[64,2048]{1,0:T(8,128)(2,1)S(1)} %get-tuple-element.94), channel_id=1, source_target_pairs={{0,2},{1,3},{2,0},{3,1},{4,6},{5,7},{6,4},{7,5},{8,10},{9,11},{10,... | collective-permute-start | bytes 786440 | tf_op jit(solution)/shard_map/ppermute | solution.py:22
  19.9 5.0 %collective-permute-start.11 = (bf16[512,128]{1,0:T(8,128)(2,1)S(1)}, bf16[512,128]{1,0:T(8,128)(2,1)S(1)}, u32[]{:S(2)}, u32[]{:S(2)}) collective-permute-start(bf16[512,128]{1,0:T(8,128)(2,1)S(1)} %collective-permute-done.3.refs_8_.refs_6_.w2), channel_id=1, source_target_pairs={{0,8},{8,0},{16,24},{24,16},{1,9},{9,1},{17,25},{25,17},{2,10},{10... | collective-permute-start | bytes 393224 | tf_op jit(solution)/shard_map/ppermute | solution.py:22
  24.9 8.0 %collective-permute-start.4 = (bf16[2,128,512]{2,1,0:T(8,128)(2,1)S(1)}, bf16[2,128,512]{2,1,0:T(8,128)(2,1)S(1)}, u32[]{:S(2)}, u32[]{:S(2)}) collective-permute-start(bf16[2,128,512]{2,1,0:T(8,128)(2,1)S(1)} %get-tuple-element.88), channel_id=1, source_target_pairs={{0,2},{1,3},{2,0},{3,1},{4,6},{5,7},{6,4},{7,5},{8,10},{9,11},{10,... | collective-permute-start | bytes 786440 | tf_op jit(solution)/shard_map/ppermute | solution.py:22
  26.4 6.6 %collective-permute-start.5 = (bf16[2,128,512]{2,1,0:T(8,128)(2,1)S(1)}, bf16[2,128,512]{2,1,0:T(8,128)(2,1)S(1)}, u32[]{:S(2)}, u32[]{:S(2)}) collective-permute-start(bf16[2,128,512]{2,1,0:T(8,128)(2,1)S(1)} %get-tuple-element.89), channel_id=1, source_target_pairs={{0,4},{1,5},{2,6},{3,7},{4,0},{5,1},{6,2},{7,3},{8,12},{9,13},{10,... | collective-permute-start | bytes 786440 | tf_op jit(solution)/shard_map/ppermute | solution.py:22
  28.6 4.4 %collective-permute-start.13 = (bf16[64,2048]{1,0:T(8,128)(2,1)S(1)}, bf16[64,2048]{1,0:T(8,128)(2,1)S(1)}, u32[]{:S(2)}, u32[]{:S(2)}) collective-permute-start(bf16[64,2048]{1,0:T(8,128)(2,1)S(1)} %collective-permute-done.6.refs_0_.refs_6_), channel_id=1, source_target_pairs={{0,1},{1,0},{2,3},{3,2},{4,5},{5,4},{6,7},{7,6},{8,9},{9,8},{10,11... | collective-permute-start | bytes 786440 | tf_op jit(solution)/shard_map/ppermute | solution.py:22
  34.0 9.6 %collective-permute-start.12 = (bf16[2,128,512]{2,1,0:T(8,128)(2,1)S(1)}, bf16[2,128,512]{2,1,0:T(8,128)(2,1)S(1)}, u32[]{:S(2)}, u32[]{:S(2)}) collective-permute-start(bf16[2,128,512]{2,1,0:T(8,128)(2,1)S(1)} %get-tuple-element.99), channel_id=1, source_target_pairs={{0,6},{1,7},{2,4},{3,5},{4,2},{5,3},{6,0},{7,1},{8,14},{9,15},{10,... | collective-permute-start | bytes 786440 | tf_op jit(solution)/shard_map/ppermute | solution.py:22
  34.4 12.1 %collective-permute-start.16 = (bf16[512,128]{1,0:T(8,128)(2,1)S(1)}, bf16[512,128]{1,0:T(8,128)(2,1)S(1)}, u32[]{:S(2)}, u32[]{:S(2)}) collective-permute-start(bf16[512,128]{1,0:T(8,128)(2,1)S(1)} %get-tuple-element.82.refs_6_.refs_4_.w0), channel_id=1, source_target_pairs={{0,1},{1,0},{2,3},{3,2},{4,5},{5,4},{6,7},{7,6},{8,9},{9,8},{10,11... | collective-permute-start | bytes 393224 | tf_op jit(solution)/shard_map/ppermute | solution.py:22
  34.6 12.0 %collective-permute-start.17 = (bf16[512,128]{1,0:T(8,128)(2,1)S(1)}, bf16[512,128]{1,0:T(8,128)(2,1)S(1)}, u32[]{:S(2)}, u32[]{:S(2)}) collective-permute-start(bf16[512,128]{1,0:T(8,128)(2,1)S(1)} %collective-permute-done.2.refs_7_.refs_5_.w1), channel_id=1, source_target_pairs={{0,1},{1,0},{2,3},{3,2},{4,5},{5,4},{6,7},{7,6},{8,9},{9,8},{10,11... | collective-permute-start | bytes 393224 | tf_op jit(solution)/shard_map/ppermute | solution.py:22
  34.9 11.6 %collective-permute-start.18 = (bf16[512,128]{1,0:T(8,128)(2,1)S(1)}, bf16[512,128]{1,0:T(8,128)(2,1)S(1)}, u32[]{:S(2)}, u32[]{:S(2)}) collective-permute-start(bf16[512,128]{1,0:T(8,128)(2,1)S(1)} %collective-permute-done.3.refs_8_.refs_6_.w2), channel_id=1, source_target_pairs={{0,1},{1,0},{2,3},{3,2},{4,5},{5,4},{6,7},{7,6},{8,9},{9,8},{10,11... | collective-permute-start | bytes 393224 | tf_op jit(solution)/shard_map/ppermute | solution.py:22
  35.5 11.1 %collective-permute-start.19 = (bf16[512,128]{1,0:T(8,128)(2,1)S(1)}, bf16[512,128]{1,0:T(8,128)(2,1)S(1)}, u32[]{:S(2)}, u32[]{:S(2)}) collective-permute-start(bf16[512,128]{1,0:T(8,128)(2,1)S(1)} %collective-permute-done.11.refs_9_.refs_7_.w3), channel_id=1, source_target_pairs={{0,1},{1,0},{2,3},{3,2},{4,5},{5,4},{6,7},{7,6},{8,9},{9,8},{10,11... | collective-permute-start | bytes 393224 | tf_op jit(solution)/shard_map/ppermute | solution.py:22
  49.7 19.9 %collective-permute-start.21 = (bf16[2,128,1024]{2,1,0:T(8,128)(2,1)S(1)}, bf16[2,128,1024]{2,1,0:T(8,128)(2,1)S(1)}, u32[]{:S(2)}, u32[]{:S(2)}) collective-permute-start(bf16[2,128,1024]{2,1,0:T(8,128)(2,1)S(1)} %get-tuple-element.131), channel_id=1, source_target_pairs={{0,2},{1,3},{2,0},{3,1},{4,6},{5,7},{6,4},{7,5},{8,10},{9,11},{10,... | collective-permute-start | bytes 1572872 | tf_op jit(solution)/shard_map/ppermute | solution.py:22
  50.3 19.4 %collective-permute-start.22 = (bf16[2,128,1024]{2,1,0:T(8,128)(2,1)S(1)}, bf16[2,128,1024]{2,1,0:T(8,128)(2,1)S(1)}, u32[]{:S(2)}, u32[]{:S(2)}) collective-permute-start(bf16[2,128,1024]{2,1,0:T(8,128)(2,1)S(1)} %get-tuple-element.132), channel_id=1, source_target_pairs={{0,4},{1,5},{2,6},{3,7},{4,0},{5,1},{6,2},{7,3},{8,12},{9,13},{10,... | collective-permute-start | bytes 1572872 | tf_op jit(solution)/shard_map/ppermute | solution.py:22
  52.6 6.6 %collective-permute-start.23 = (bf16[512,128]{1,0:T(8,128)(2,1)S(1)}, bf16[512,128]{1,0:T(8,128)(2,1)S(1)}, u32[]{:S(2)}, u32[]{:S(2)}) collective-permute-start(bf16[512,128]{1,0:T(8,128)(2,1)S(1)} %get-tuple-element.134), channel_id=1, source_target_pairs={{0,8},{8,0},{16,24},{24,16},{1,9},{9,1},{17,25},{25,17},{2,10},{10... | collective-permute-start | bytes 393224 | tf_op jit(solution)/shard_map/ppermute | solution.py:22
  54.2 12.7 %collective-permute-start.24 = (bf16[512,128]{1,0:T(8,128)(2,1)S(1)}, bf16[512,128]{1,0:T(8,128)(2,1)S(1)}, u32[]{:S(2)}, u32[]{:S(2)}) collective-permute-start(bf16[512,128]{1,0:T(8,128)(2,1)S(1)} %get-tuple-element.135), channel_id=1, source_target_pairs={{0,16},{8,24},{16,0},{24,8},{1,17},{9,25},{17,1},{25,9},{2,18},{10... | collective-permute-start | bytes 393224 | tf_op jit(solution)/shard_map/ppermute | solution.py:22
  56.8 11.2 %collective-permute-start.25 = (bf16[512,128]{1,0:T(8,128)(2,1)S(1)}, bf16[512,128]{1,0:T(8,128)(2,1)S(1)}, u32[]{:S(2)}, u32[]{:S(2)}) collective-permute-start(bf16[512,128]{1,0:T(8,128)(2,1)S(1)} %get-tuple-element.136), channel_id=1, source_target_pairs={{0,24},{8,16},{16,8},{24,0},{1,25},{9,17},{17,9},{25,1},{2,26},{10... | collective-permute-start | bytes 393224 | tf_op jit(solution)/shard_map/ppermute | solution.py:22
  59.2 13.0 %collective-permute-start.31 = (bf16[2,128,512]{2,1,0:T(8,128)(2,1)S(1)}, bf16[2,128,512]{2,1,0:T(8,128)(2,1)S(1)}, u32[]{:S(2)}, u32[]{:S(2)}) collective-permute-start(bf16[2,128,512]{2,1,0:T(8,128)(2,1)S(1)} %get-tuple-element.141), channel_id=1, source_target_pairs={{0,6},{1,7},{2,4},{3,5},{4,2},{5,3},{6,0},{7,1},{8,14},{9,15},{10,... | collective-permute-start | bytes 786440 | tf_op jit(solution)/shard_map/ppermute | solution.py:22
  66.9 9.2 %collective-permute-start.29 = (bf16[2,128,512]{2,1,0:T(8,128)(2,1)S(1)}, bf16[2,128,512]{2,1,0:T(8,128)(2,1)S(1)}, u32[]{:S(2)}, u32[]{:S(2)}) collective-permute-start(bf16[2,128,512]{2,1,0:T(8,128)(2,1)S(1)} %get-tuple-element.139), channel_id=1, source_target_pairs={{0,2},{1,3},{2,0},{3,1},{4,6},{5,7},{6,4},{7,5},{8,10},{9,11},{10,... | collective-permute-start | bytes 786440 | tf_op jit(solution)/shard_map/ppermute | solution.py:22
  68.0 9.2 %collective-permute-start.30 = (bf16[2,128,512]{2,1,0:T(8,128)(2,1)S(1)}, bf16[2,128,512]{2,1,0:T(8,128)(2,1)S(1)}, u32[]{:S(2)}, u32[]{:S(2)}) collective-permute-start(bf16[2,128,512]{2,1,0:T(8,128)(2,1)S(1)} %get-tuple-element.140), channel_id=1, source_target_pairs={{0,4},{1,5},{2,6},{3,7},{4,0},{5,1},{6,2},{7,3},{8,12},{9,13},{10,... | collective-permute-start | bytes 786440 | tf_op jit(solution)/shard_map/ppermute | solution.py:22
  69.8 17.1 %collective-permute-start.32 = (bf16[128,1024]{1,0:T(8,128)(2,1)S(1)}, bf16[128,1024]{1,0:T(8,128)(2,1)S(1)}, u32[]{:S(2)}, u32[]{:S(2)}) collective-permute-start(bf16[128,1024]{1,0:T(8,128)(2,1)S(1)} %get-tuple-element.154), channel_id=1, source_target_pairs={{0,4},{1,5},{2,6},{3,7},{4,0},{5,1},{6,2},{7,3},{8,12},{9,13},{10,... | collective-permute-start | bytes 786440 | tf_op jit(solution)/shard_map/ppermute | solution.py:22
  70.4 8.5 %collective-permute-start.28 = (bf16[512,128]{1,0:T(8,128)(2,1)S(1)}, bf16[512,128]{1,0:T(8,128)(2,1)S(1)}, u32[]{:S(2)}, u32[]{:S(2)}) collective-permute-start(bf16[512,128]{1,0:T(8,128)(2,1)S(1)} %last_kernel.1.refs_0_), channel_id=1, source_target_pairs={{0,2},{1,3},{2,0},{3,1},{4,6},{5,7},{6,4},{7,5},{8,10},{9,11},{10,... | collective-permute-start | bytes 393224 | tf_op jit(solution)/shard_map/ppermute | solution.py:22
  72.2 14.2 %collective-permute-start.26 = (bf16[512,128]{1,0:T(8,128)(2,1)S(1)}, bf16[512,128]{1,0:T(8,128)(2,1)S(1)}, u32[]{:S(2)}, u32[]{:S(2)}) collective-permute-start(bf16[512,128]{1,0:T(8,128)(2,1)S(1)} %last_kernel.1.refs_0_), channel_id=1, source_target_pairs={{0,4},{1,5},{2,6},{3,7},{4,0},{5,1},{6,2},{7,3},{8,12},{9,13},{10,... | collective-permute-start | bytes 393224 | tf_op jit(solution)/shard_map/ppermute | solution.py:22
  76.1 10.3 %collective-permute-start.27 = (bf16[512,128]{1,0:T(8,128)(2,1)S(1)}, bf16[512,128]{1,0:T(8,128)(2,1)S(1)}, u32[]{:S(2)}, u32[]{:S(2)}) collective-permute-start(bf16[512,128]{1,0:T(8,128)(2,1)S(1)} %last_kernel.1.refs_0_), channel_id=1, source_target_pairs={{0,6},{1,7},{2,4},{3,5},{4,2},{5,3},{6,0},{7,1},{8,14},{9,15},{10,... | collective-permute-start | bytes 393224 | tf_op jit(solution)/shard_map/ppermute | solution.py:22
  77.3 9.7 %collective-permute-start.33 = (bf16[128,1024]{1,0:T(8,128)(2,1)S(1)}, bf16[128,1024]{1,0:T(8,128)(2,1)S(1)}, u32[]{:S(2)}, u32[]{:S(2)}) collective-permute-start(bf16[128,1024]{1,0:T(8,128)(2,1)S(1)} %get-tuple-element.156), channel_id=1, source_target_pairs={{0,2},{1,3},{2,0},{3,1},{4,6},{5,7},{6,4},{7,5},{8,10},{9,11},{10,... | collective-permute-start | bytes 786440 | tf_op jit(solution)/shard_map/ppermute | solution.py:22
  78.9 9.5 %collective-permute-start.34 = (bf16[512,128]{1,0:T(8,128)(2,1)S(1)}, bf16[512,128]{1,0:T(8,128)(2,1)S(1)}, u32[]{:S(2)}, u32[]{:S(2)}) collective-permute-start(bf16[512,128]{1,0:T(8,128)(2,1)S(1)} %last_kernel.1.refs_0_), channel_id=1, source_target_pairs={{0,1},{1,0},{2,3},{3,2},{4,5},{5,4},{6,7},{7,6},{8,9},{9,8},{10,11... | collective-permute-start | bytes 393224 | tf_op jit(solution)/shard_map/ppermute | solution.py:22
  (7 other events, 29.5 us)

commit v6 on v5

--- a/solution.py
+++ b/solution.py
@@ -328,6 +328,12 @@
         now, got = (a, got_a) if i < 2 else (b, got_b)
         at = slice((i % 2) * size, (i % 2 + 1) * size)
         out[:, quarter(ids[2], i, size)] = (now[:, at] + got[:, at].astype(F32)).astype(BF16)
+
+
+def final_kernel(ids, *refs):
+    *blocks, a, got_a, b, got_b, weight_out, token_out = refs
+    token_last_kernel(ids, a, got_a, b, got_b, token_out)
+    assemble_kernel(ids, *blocks, weight_out)
 
 
 def plane_local(tokens, kv_weight, queries, out_grad, doc_lengths):
@@ -404,14 +410,14 @@
     attn_out, grad_queries = run(place_kernel, (like, like), (ids,), (o0, o1, o2, o3))
     mine[2], mine[3], attn_out, grad_queries = lax.optimization_barrier((mine[2], mine[3], attn_out, grad_queries))
     theirs = [pair(v) for v in mine]
-    grad_weight = run(
-        assemble_kernel,
-        jax.ShapeDtypeStruct((size, kv_weight.shape[1]), F32),
+    grad_weight, grad_tokens = run(
+        final_kernel,
+        (
+            jax.ShapeDtypeStruct((size, kv_weight.shape[1]), F32),
+            jax.ShapeDtypeStruct(tokens.shape, BF16),
+        ),
         (ids,),
-        mine + theirs,
-    )
-    grad_tokens = run(
-        token_last_kernel, jax.ShapeDtypeStruct(tokens.shape, BF16), (ids,), (a, got_a, b, got_b)
+        (*mine, *theirs, a, got_a, b, got_b),
     )
     return attn_out, grad_queries, grad_tokens, grad_weight
 

time: 90.7 us -> 89 us (0.981)
  Pallas kernels: 23.6 us -> 22.4 us
    pallas_call x14 -> x13, Pallas kernels: 20 us -> 18.8 us  [run(): pl.pallas_call(body, out_shape=outs, in_specs=[pl.BlockSpec(memory_space=...]
  transfers between devices with their start and end apart: 38 -> 38, of which waited for: 14 -> 15; matrix products, arithmetic and copies ran while one was open for 0% -> 0% of each run, Pallas kernels for 21% -> 20%
where the time goes in v6:
time: 89 us; the launch traced here: 88.8 us
  starting transfers between devices  34.5 us (39%)
  waiting for transfers between devices  31 us (35%)
  Pallas kernels  22.4 us (25%)
    ppermute x38, starting transfers between devices, swap(): return lax.ppermute(value, axis, [(i, i ^ bit) for i in range(count)])  34.5 us
    ppermute x38, waiting for transfers between devices, swap(): return lax.ppermute(value, axis, [(i, i ^ bit) for i in range(count)])  31 us
    pallas_call x13, Pallas kernels, run(): pl.pallas_call(body, out_shape=outs, in_specs=[pl.BlockSpec(memory_space=...  18.8 us
    pallas_call x1, Pallas kernels, cut_heads(): pl.pallas_call(cut_heads_kernel, out_shape=(on_chip((2, rows, width)),) *...  1.9 us
  transfers between devices with their start and end apart: 38, of which 15 were waited for; matrix products, arithmetic and copies ran while one was open for 0% of the time, Pallas kernels for 20%

profile of v6, /device:TPU:0, one launch (start us, length us, event | category | flops | bytes accessed | tf_op | source)
XLA Modules:
  0.0 88.8 jit_solution(2197437608243982016)
XLA Ops:
  0.6 3.0 %collective-permute-start = (bf16[128,2048]{1,0:T(8,128)(2,1)}, bf16[128,2048]{1,0:T(8,128)(2,1)S(1)}, u32[]{:S(2)}, u32[]{:S(2)}) collective-permute-start(bf16[128,2048]{1,0:T(8,128)(2,1)} %x.1), channel_id=1, source_target_pairs={{0,2},{1,3},{2,0},{3,1},{4,6},{5,7},{6,4},{7,5},{8,10},{9,11},{10,... | collective-permute-start | bytes 1572872 | tf_op jit(solution)/shard_map/ppermute | solution.py:22
  3.7 1.5 %collective-permute-start.1 = (bf16[128,2048]{1,0:T(8,128)(2,1)}, bf16[128,2048]{1,0:T(8,128)(2,1)S(1)}, u32[]{:S(2)}, u32[]{:S(2)}) collective-permute-start(bf16[128,2048]{1,0:T(8,128)(2,1)} %x.1), channel_id=1, source_target_pairs={{0,4},{1,5},{2,6},{3,7},{4,0},{5,1},{6,2},{7,3},{8,12},{9,13},{10,... | collective-permute-start | bytes 1572872 | tf_op jit(solution)/shard_map/ppermute | solution.py:22
  5.3 1.7 %prep_kernel.1 = (bf16[512,128]{1,0:T(8,128)(2,1)S(1)}, bf16[128,2048]{1,0:T(8,128)(2,1)S(1)}) custom-call(s32[3]{0:T(128)S(1)} %pad_add_fusion.ids, s32[1]{0:T(128)} %bitcast.3.block, bf16[512,1024]{1,0:T(8,128)(2,1)} %weight.1, bf16[128,2048]{1,0:T(8,128)(2,1)} %x.1), custom_call_target="tpu_custom_call" | custom-call | tf_op jit(solution)/shard_map/prep_kernel/pallas_call | solution.py:76
  7.0 1.6 %collective-permute-start.2 = (bf16[512,128]{1,0:T(8,128)(2,1)S(1)}, bf16[512,128]{1,0:T(8,128)(2,1)S(1)}, u32[]{:S(2)}, u32[]{:S(2)}) collective-permute-start(bf16[512,128]{1,0:T(8,128)(2,1)S(1)} %get-tuple-element.84.refs_6_.refs_4_.w0), channel_id=1, source_target_pairs={{0,8},{8,0},{16,24},{24,16},{1,9},{9,1},{17,25},{25,17},{2,10},{10... | collective-permute-start | bytes 393224 | tf_op jit(solution)/shard_map/ppermute | solution.py:22
  8.6 2.6 %collective-permute-start.3 = (bf16[512,128]{1,0:T(8,128)(2,1)S(1)}, bf16[512,128]{1,0:T(8,128)(2,1)S(1)}, u32[]{:S(2)}, u32[]{:S(2)}) collective-permute-start(bf16[512,128]{1,0:T(8,128)(2,1)S(1)} %get-tuple-element.84.refs_6_.refs_4_.w0), channel_id=1, source_target_pairs={{0,16},{8,24},{16,0},{24,8},{1,17},{9,25},{17,1},{25,9},{2,18},{10... | collective-permute-start | bytes 393224 | tf_op jit(solution)/shard_map/ppermute | solution.py:22
  11.2 1.9 %cut_heads_kernel.1 = (bf16[2,128,512]{2,1,0:T(8,128)(2,1)S(1)}, bf16[2,128,512]{2,1,0:T(8,128)(2,1)S(1)}, bf16[2,128,512]{2,1,0:T(8,128)(2,1)S(1)}, bf16[2,128,512]{2,1,0:T(8,128)(2,1)S(1)}) custom-call(s32[3]{0:T(128)S(1)} %pad_add_fusion.ids, bf16[128,2048]{1,0:T(8,128)(2,1)} %refs_6_.1, bf16[128,2048]{1,0:T(8,128)(2,1)} %refs_7_.1, ...), custom_call_target="tpu_custom_call" | custom-call | tf_op jit(solution)/shard_map/cut_heads_kernel/pallas_call | solution.py:128
  13.7 3.0 %collective-permute-done.3.refs_8_.refs_6_.w2 = bf16[512,128]{1,0:T(8,128)(2,1)S(1)} collective-permute-done((bf16[512,128]{1,0:T(8,128)(2,1)S(1)}, bf16[512,128]{1,0:T(8,128)(2,1)S(1)}, u32[]{:S(2)}, u32[]{:S(2)}) %collective-permute-start.3) | collective-permute-done | bytes 131104 | tf_op jit(solution)/shard_map/ppermute | solution.py:22
  17.8 1.6 %collective-permute-start.6 = (bf16[64,2048]{1,0:T(8,128)(2,1)S(1)}, bf16[64,2048]{1,0:T(8,128)(2,1)S(1)}, u32[]{:S(2)}, u32[]{:S(2)}) collective-permute-start(bf16[64,2048]{1,0:T(8,128)(2,1)S(1)} %get-tuple-element.95), channel_id=1, source_target_pairs={{0,4},{1,5},{2,6},{3,7},{4,0},{5,1},{6,2},{7,3},{8,12},{9,13},{10,... | collective-permute-start | bytes 786440 | tf_op jit(solution)/shard_map/ppermute | solution.py:22
  19.9 1.6 %collective-permute-start.11 = (bf16[512,128]{1,0:T(8,128)(2,1)S(1)}, bf16[512,128]{1,0:T(8,128)(2,1)S(1)}, u32[]{:S(2)}, u32[]{:S(2)}) collective-permute-start(bf16[512,128]{1,0:T(8,128)(2,1)S(1)} %collective-permute-done.3.refs_8_.refs_6_.w2), channel_id=1, source_target_pairs={{0,8},{8,0},{16,24},{24,16},{1,9},{9,1},{17,25},{25,17},{2,10},{10... | collective-permute-start | bytes 393224 | tf_op jit(solution)/shard_map/ppermute | solution.py:22
  21.5 3.4 %collective-permute-done.11.refs_9_.refs_7_.w3 = bf16[512,128]{1,0:T(8,128)(2,1)S(1)} collective-permute-done((bf16[512,128]{1,0:T(8,128)(2,1)S(1)}, bf16[512,128]{1,0:T(8,128)(2,1)S(1)}, u32[]{:S(2)}, u32[]{:S(2)}) %collective-permute-start.11) | collective-permute-done | bytes 131104 | tf_op jit(solution)/shard_map/ppermute | solution.py:22
  24.9 1.5 %collective-permute-start.4 = (bf16[2,128,512]{2,1,0:T(8,128)(2,1)S(1)}, bf16[2,128,512]{2,1,0:T(8,128)(2,1)S(1)}, u32[]{:S(2)}, u32[]{:S(2)}) collective-permute-start(bf16[2,128,512]{2,1,0:T(8,128)(2,1)S(1)} %get-tuple-element.90), channel_id=1, source_target_pairs={{0,2},{1,3},{2,0},{3,1},{4,6},{5,7},{6,4},{7,5},{8,10},{9,11},{10,... | collective-permute-start | bytes 786440 | tf_op jit(solution)/shard_map/ppermute | solution.py:22
  26.9 1.5 %project_kernel.1.refs_8_ = bf16[768,128]{1,0:T(8,128)(2,1)S(1)} custom-call(s32[3]{0:T(128)S(1)} %pad_add_fusion.ids, bf16[128,2048]{1,0:T(8,128)(2,1)S(1)} %get-tuple-element.97.refs_0_, bf16[128,2048]{1,0:T(8,128)(2,1)S(1)} %collective-permute-done.8.refs_1_, bf16[128,2048]{1,0:T(8,128)(2,1)S(1)} %collective-permute-done.x1.refs_2_, ...), custom_call_target="tpu_custom_call" | custom-call | tf_op jit(solution)/shard_map/project_kernel/pallas_call | solution.py:35
  29.1 3.9 %collective-permute-done.4.refs_4_ = bf16[2,128,512]{2,1,0:T(8,128)(2,1)S(1)} collective-permute-done((bf16[2,128,512]{2,1,0:T(8,128)(2,1)S(1)}, bf16[2,128,512]{2,1,0:T(8,128)(2,1)S(1)}, u32[]{:S(2)}, u32[]{:S(2)}) %collective-permute-start.4) | collective-permute-done | bytes 262176 | tf_op jit(solution)/shard_map/ppermute | solution.py:22
  35.7 1.8 %attend_kernel.3 = (bf16[2,128,512]{2,1,0:T(8,128)(2,1)S(1)}, f32[1024,128]{1,0:T(8,128)S(1)}, f32[1024,128]{1,0:T(8,128)S(1)}, bf16[1024,128]{1,0:T(8,128)(2,1)S(1)}, bf16[1024,128]{1,0:T(8,128)(2,1)S(1)}) custom-call(s32[3]{0:T(128)S(1)} %pad_add_fusion.ids, s32[1,4]{1,0:T(1,128)S(1)} %copy-done, bf16[1024,128]{1,0:T(8,128)(2,1)S(1)} %order_kernel.1.refs_0_, ...), custom_call_target="tpu_custom_call" | custom-call | tf_op jit(solution)/shard_map/attend_kernel/pallas_call | solution.py:35
  37.5 4.6 %attend_kernel.4 = (bf16[2,128,512]{2,1,0:T(8,128)(2,1)S(1)}, bf16[2,128,512]{2,1,0:T(8,128)(2,1)S(1)}, f32[1024,128]{1,0:T(8,128)S(1)}, f32[1024,128]{1,0:T(8,128)S(1)}) custom-call(s32[3]{0:T(128)S(1)} %pad_add_fusion.ids, s32[1,4]{1,0:T(1,128)S(1)} %copy-done, ...), custom_call_target="tpu_custom_call", output_to_operand_aliasing={{2}: (2, {}), {3}: (3, {})} | custom-call | tf_op jit(solution)/shard_map/attend_kernel/pallas_call | solution.py:35
  42.1 1.5 %collective-permute-done.12.refs_4_ = bf16[2,128,512]{2,1,0:T(8,128)(2,1)S(1)} collective-permute-done((bf16[2,128,512]{2,1,0:T(8,128)(2,1)S(1)}, bf16[2,128,512]{2,1,0:T(8,128)(2,1)S(1)}, u32[]{:S(2)}, u32[]{:S(2)}) %collective-permute-start.12) | collective-permute-done | bytes 262176 | tf_op jit(solution)/shard_map/ppermute | solution.py:22
  43.6 2.9 %attend_kernel.5 = (bf16[2,128,512]{2,1,0:T(8,128)(2,1)S(1)}, f32[1024,128]{1,0:T(8,128)S(1)}, f32[512,128]{1,0:T(8,128)S(1)}, bf16[1536,128]{1,0:T(8,128)(2,1)S(1)}) custom-call(s32[3]{0:T(128)S(1)} %pad_add_fusion.ids, s32[1,4]{1,0:T(1,128)S(1)} %copy-done, f32[1024,128]{1,0:T(8,128)S(1)} %get-tuple-element.120.refs_0_, ...), custom_call_target="tpu_custom_call" | custom-call | tf_op jit(solution)/shard_map/attend_kernel/pallas_call | solution.py:35
  46.7 1.7 %collective-permute-done.20.got = bf16[1536,128]{1,0:T(8,128)(2,1)S(1)} collective-permute-done((bf16[1536,128]{1,0:T(8,128)(2,1)S(1)}, bf16[1536,128]{1,0:T(8,128)(2,1)S(1)}, u32[]{:S(2)}, u32[]{:S(2)}) %collective-permute-start.20) | collective-permute-done | bytes 393248 | tf_op jit(solution)/shard_map/ppermute | solution.py:22
  51.1 1.4 %weight_kernel.1 = (f32[512,128]{1,0:T(8,128)S(1)}, bf16[512,128]{1,0:T(8,128)(2,1)S(1)}, bf16[512,128]{1,0:T(8,128)(2,1)S(1)}, bf16[512,128]{1,0:T(8,128)(2,1)S(1)}) custom-call(s32[3]{0:T(128)S(1)} %pad_add_fusion.ids, f32[1024,128]{1,0:T(8,128)S(1)} %get-tuple-element.125.mine, bf16[1536,128]{1,0:T(8,128)(2,1)S(1)} %collective-permute-done.20.got, ...), custom_call_target="tpu_custom_call" | custom-call | tf_op jit(solution)/shard_map/weight_kernel/pallas_call | solution.py:35
  52.6 1.7 %collective-permute-start.23 = (bf16[512,128]{1,0:T(8,128)(2,1)S(1)}, bf16[512,128]{1,0:T(8,128)(2,1)S(1)}, u32[]{:S(2)}, u32[]{:S(2)}) collective-permute-start(bf16[512,128]{1,0:T(8,128)(2,1)S(1)} %get-tuple-element.136), channel_id=1, source_target_pairs={{0,8},{8,0},{16,24},{24,16},{1,9},{9,1},{17,25},{25,17},{2,10},{10... | collective-permute-start | bytes 393224 | tf_op jit(solution)/shard_map/ppermute | solution.py:22
  54.2 2.6 %collective-permute-start.24 = (bf16[512,128]{1,0:T(8,128)(2,1)S(1)}, bf16[512,128]{1,0:T(8,128)(2,1)S(1)}, u32[]{:S(2)}, u32[]{:S(2)}) collective-permute-start(bf16[512,128]{1,0:T(8,128)(2,1)S(1)} %get-tuple-element.137), channel_id=1, source_target_pairs={{0,16},{8,24},{16,0},{24,8},{1,17},{9,25},{17,1},{25,9},{2,18},{10... | collective-permute-start | bytes 393224 | tf_op jit(solution)/shard_map/ppermute | solution.py:22
  57.0 2.2 %collective-permute-done.23.got = bf16[512,128]{1,0:T(8,128)(2,1)S(1)} collective-permute-done((bf16[512,128]{1,0:T(8,128)(2,1)S(1)}, bf16[512,128]{1,0:T(8,128)(2,1)S(1)}, u32[]{:S(2)}, u32[]{:S(2)}) %collective-permute-start.23) | collective-permute-done | bytes 131104 | tf_op jit(solution)/shard_map/ppermute | solution.py:22
  59.2 2.1 %collective-permute-start.31 = (bf16[2,128,512]{2,1,0:T(8,128)(2,1)S(1)}, bf16[2,128,512]{2,1,0:T(8,128)(2,1)S(1)}, u32[]{:S(2)}, u32[]{:S(2)}) collective-permute-start(bf16[2,128,512]{2,1,0:T(8,128)(2,1)S(1)} %get-tuple-element.143), channel_id=1, source_target_pairs={{0,6},{1,7},{2,4},{3,5},{4,2},{5,3},{6,0},{7,1},{8,14},{9,15},{10,... | collective-permute-start | bytes 786440 | tf_op jit(solution)/shard_map/ppermute | solution.py:22
  61.3 5.7 %collective-permute-done.24.got1 = bf16[512,128]{1,0:T(8,128)(2,1)S(1)} collective-permute-done((bf16[512,128]{1,0:T(8,128)(2,1)S(1)}, bf16[512,128]{1,0:T(8,128)(2,1)S(1)}, u32[]{:S(2)}, u32[]{:S(2)}) %collective-permute-start.24) | collective-permute-done | bytes 131104 | tf_op jit(solution)/shard_map/ppermute | solution.py:22
  68.0 1.5 %collective-permute-start.30 = (bf16[2,128,512]{2,1,0:T(8,128)(2,1)S(1)}, bf16[2,128,512]{2,1,0:T(8,128)(2,1)S(1)}, u32[]{:S(2)}, u32[]{:S(2)}) collective-permute-start(bf16[2,128,512]{2,1,0:T(8,128)(2,1)S(1)} %get-tuple-element.142), channel_id=1, source_target_pairs={{0,4},{1,5},{2,6},{3,7},{4,0},{5,1},{6,2},{7,3},{8,12},{9,13},{10,... | collective-permute-start | bytes 786440 | tf_op jit(solution)/shard_map/ppermute | solution.py:22
  69.6 2.2 %collective-permute-start.28 = (bf16[512,128]{1,0:T(8,128)(2,1)S(1)}, bf16[512,128]{1,0:T(8,128)(2,1)S(1)}, u32[]{:S(2)}, u32[]{:S(2)}) collective-permute-start(bf16[512,128]{1,0:T(8,128)(2,1)S(1)} %last_kernel.1.refs_0_), channel_id=1, source_target_pairs={{0,2},{1,3},{2,0},{3,1},{4,6},{5,7},{6,4},{7,5},{8,10},{9,11},{10,... | collective-permute-start | bytes 393224 | tf_op jit(solution)/shard_map/ppermute | solution.py:22
  71.9 1.5 %collective-permute-start.27 = (bf16[512,128]{1,0:T(8,128)(2,1)S(1)}, bf16[512,128]{1,0:T(8,128)(2,1)S(1)}, u32[]{:S(2)}, u32[]{:S(2)}) collective-permute-start(bf16[512,128]{1,0:T(8,128)(2,1)S(1)} %last_kernel.1.refs_0_), channel_id=1, source_target_pairs={{0,6},{1,7},{2,4},{3,5},{4,2},{5,3},{6,0},{7,1},{8,14},{9,15},{10,... | collective-permute-start | bytes 393224 | tf_op jit(solution)/shard_map/ppermute | solution.py:22
  73.5 2.6 %collective-permute-done.29.p1 = bf16[2,128,512]{2,1,0:T(8,128)(2,1)S(1)} collective-permute-done((bf16[2,128,512]{2,1,0:T(8,128)(2,1)S(1)}, bf16[2,128,512]{2,1,0:T(8,128)(2,1)S(1)}, u32[]{:S(2)}, u32[]{:S(2)}) %collective-permute-start.29) | collective-permute-done | bytes 262176 | tf_op jit(solution)/shard_map/ppermute | solution.py:22
  77.8 1.8 %collective-permute-start.37 = (bf16[128,1024]{1,0:T(8,128)(2,1)S(1)}, bf16[128,1024]{1,0:T(8,128)(2,1)S(1)}, u32[]{:S(2)}, u32[]{:S(2)}) collective-permute-start(bf16[128,1024]{1,0:T(8,128)(2,1)S(1)} %get-tuple-element.161), channel_id=1, source_target_pairs={{0,2},{1,3},{2,0},{3,1},{4,6},{5,7},{6,4},{7,5},{8,10},{9,11},{10,... | collective-permute-start | bytes 786440 | tf_op jit(solution)/shard_map/ppermute | solution.py:22
  79.5 1.6 %place_kernel.1 = (bf16[128,2048]{1,0:T(8,128)(2,1)}, bf16[128,2048]{1,0:T(8,128)(2,1)}) custom-call(s32[3]{0:T(128)S(1)} %pad_add_fusion.ids, bf16[2,128,512]{2,1,0:T(8,128)(2,1)S(1)} %get-tuple-element.140.p0, bf16[2,128,512]{2,1,0:T(8,128)(2,1)S(1)} %collective-permute-done.29.p1, bf16[2,128,512]{2,1,0:T(8,128)(2,1)S(1)} %collective-permute-done.30.p2, ...), custom_call_target="tpu_custom_call" | custom-call | tf_op jit(solution)/shard_map/place_kernel/pallas_call | solution.py:35
  83.0 3.4 %collective-permute-done.36.refs_9_ = bf16[128,1024]{1,0:T(8,128)(2,1)S(1)} collective-permute-done((bf16[128,1024]{1,0:T(8,128)(2,1)S(1)}, bf16[128,1024]{1,0:T(8,128)(2,1)S(1)}, u32[]{:S(2)}, u32[]{:S(2)}) %collective-permute-start.36) | collective-permute-done | bytes 262176 | tf_op jit(solution)/shard_map/ppermute | solution.py:22
  86.5 2.4 %final_kernel.1 = (f32[512,1024]{1,0:T(8,128)}, bf16[128,2048]{1,0:T(8,128)(2,1)}) custom-call(s32[3]{0:T(128)S(1)} %pad_add_fusion.ids, bf16[512,128]{1,0:T(8,128)(2,1)S(1)} %last_kernel.1.refs_0_, bf16[512,128]{1,0:T(8,128)(2,1)S(1)} %collective-permute-done.28.refs_1_, bf16[512,128]{1,0:T(8,128)(2,1)S(1)} %collective-permute-done.26.refs_2_, ...), custom_call_target="tpu_custom_call" | custom-call | tf_op jit(solution)/shard_map/final_kernel/pallas_call | solution.py:35
  (62 shorter events, 14.2 us)
Async XLA Ops:
  0.6 16.1 %collective-permute-start = (bf16[128,2048]{1,0:T(8,128)(2,1)}, bf16[128,2048]{1,0:T(8,128)(2,1)S(1)}, u32[]{:S(2)}, u32[]{:S(2)}) collective-permute-start(bf16[128,2048]{1,0:T(8,128)(2,1)} %x.1), channel_id=1, source_target_pairs={{0,2},{1,3},{2,0},{3,1},{4,6},{5,7},{6,4},{7,5},{8,10},{9,11},{10,... | collective-permute-start | bytes 1572872 | tf_op jit(solution)/shard_map/ppermute | solution.py:22
  3.7 13.6 %collective-permute-start.1 = (bf16[128,2048]{1,0:T(8,128)(2,1)}, bf16[128,2048]{1,0:T(8,128)(2,1)S(1)}, u32[]{:S(2)}, u32[]{:S(2)}) collective-permute-start(bf16[128,2048]{1,0:T(8,128)(2,1)} %x.1), channel_id=1, source_target_pairs={{0,4},{1,5},{2,6},{3,7},{4,0},{5,1},{6,2},{7,3},{8,12},{9,13},{10,... | collective-permute-start | bytes 1572872 | tf_op jit(solution)/shard_map/ppermute | solution.py:22
  7.0 6.8 %collective-permute-start.2 = (bf16[512,128]{1,0:T(8,128)(2,1)S(1)}, bf16[512,128]{1,0:T(8,128)(2,1)S(1)}, u32[]{:S(2)}, u32[]{:S(2)}) collective-permute-start(bf16[512,128]{1,0:T(8,128)(2,1)S(1)} %get-tuple-element.84.refs_6_.refs_4_.w0), channel_id=1, source_target_pairs={{0,8},{8,0},{16,24},{24,16},{1,9},{9,1},{17,25},{25,17},{2,10},{10... | collective-permute-start | bytes 393224 | tf_op jit(solution)/shard_map/ppermute | solution.py:22
  8.6 8.2 %collective-permute-start.3 = (bf16[512,128]{1,0:T(8,128)(2,1)S(1)}, bf16[512,128]{1,0:T(8,128)(2,1)S(1)}, u32[]{:S(2)}, u32[]{:S(2)}) collective-permute-start(bf16[512,128]{1,0:T(8,128)(2,1)S(1)} %get-tuple-element.84.refs_6_.refs_4_.w0), channel_id=1, source_target_pairs={{0,16},{8,24},{16,0},{24,8},{1,17},{9,25},{17,1},{25,9},{2,18},{10... | collective-permute-start | bytes 393224 | tf_op jit(solution)/shard_map/ppermute | solution.py:22
  11.2 8.7 %collective-permute-start.8 = (bf16[128,2048]{1,0:T(8,128)(2,1)S(1)}, bf16[128,2048]{1,0:T(8,128)(2,1)S(1)}, u32[]{:S(2)}, u32[]{:S(2)}) collective-permute-start(bf16[128,2048]{1,0:T(8,128)(2,1)S(1)} %get-tuple-element.97.refs_0_), channel_id=1, source_target_pairs={{0,1},{1,0},{2,3},{3,2},{4,5},{5,4},{6,7},{7,6},{8,9},{9,8},{10,11... | collective-permute-start | bytes 1572872 | tf_op jit(solution)/shard_map/ppermute | solution.py:22
  17.3 9.1 %collective-permute-start.10 = (bf16[128,2048]{1,0:T(8,128)(2,1)S(1)}, bf16[128,2048]{1,0:T(8,128)(2,1)S(1)}, u32[]{:S(2)}, u32[]{:S(2)}) collective-permute-start(bf16[128,2048]{1,0:T(8,128)(2,1)S(1)} %collective-permute-done.1.x2.refs_4_), channel_id=1, source_target_pairs={{0,1},{1,0},{2,3},{3,2},{4,5},{5,4},{6,7},{7,6},{8,9},{9,8},{10,11... | collective-permute-start | bytes 1572872 | tf_op jit(solution)/shard_map/ppermute | solution.py:22
  17.3 9.6 %collective-permute-start.9 = (bf16[128,2048]{1,0:T(8,128)(2,1)S(1)}, bf16[128,2048]{1,0:T(8,128)(2,1)S(1)}, u32[]{:S(2)}, u32[]{:S(2)}) collective-permute-start(bf16[128,2048]{1,0:T(8,128)(2,1)S(1)} %collective-permute-done.x1.refs_2_), channel_id=1, source_target_pairs={{0,1},{1,0},{2,3},{3,2},{4,5},{5,4},{6,7},{7,6},{8,9},{9,8},{10,11... | collective-permute-start | bytes 1572872 | tf_op jit(solution)/shard_map/ppermute | solution.py:22
  17.8 10.6 %collective-permute-start.6 = (bf16[64,2048]{1,0:T(8,128)(2,1)S(1)}, bf16[64,2048]{1,0:T(8,128)(2,1)S(1)}, u32[]{:S(2)}, u32[]{:S(2)}) collective-permute-start(bf16[64,2048]{1,0:T(8,128)(2,1)S(1)} %get-tuple-element.95), channel_id=1, source_target_pairs={{0,4},{1,5},{2,6},{3,7},{4,0},{5,1},{6,2},{7,3},{8,12},{9,13},{10,... | collective-permute-start | bytes 786440 | tf_op jit(solution)/shard_map/ppermute | solution.py:22
  19.4 9.2 %collective-permute-start.7 = (bf16[64,2048]{1,0:T(8,128)(2,1)S(1)}, bf16[64,2048]{1,0:T(8,128)(2,1)S(1)}, u32[]{:S(2)}, u32[]{:S(2)}) collective-permute-start(bf16[64,2048]{1,0:T(8,128)(2,1)S(1)} %get-tuple-element.96), channel_id=1, source_target_pairs={{0,2},{1,3},{2,0},{3,1},{4,6},{5,7},{6,4},{7,5},{8,10},{9,11},{10,... | collective-permute-start | bytes 786440 | tf_op jit(solution)/shard_map/ppermute | solution.py:22
  19.9 5.0 %collective-permute-start.11 = (bf16[512,128]{1,0:T(8,128)(2,1)S(1)}, bf16[512,128]{1,0:T(8,128)(2,1)S(1)}, u32[]{:S(2)}, u32[]{:S(2)}) collective-permute-start(bf16[512,128]{1,0:T(8,128)(2,1)S(1)} %collective-permute-done.3.refs_8_.refs_6_.w2), channel_id=1, source_target_pairs={{0,8},{8,0},{16,24},{24,16},{1,9},{9,1},{17,25},{25,17},{2,10},{10... | collective-permute-start | bytes 393224 | tf_op jit(solution)/shard_map/ppermute | solution.py:22
  24.9 8.0 %collective-permute-start.4 = (bf16[2,128,512]{2,1,0:T(8,128)(2,1)S(1)}, bf16[2,128,512]{2,1,0:T(8,128)(2,1)S(1)}, u32[]{:S(2)}, u32[]{:S(2)}) collective-permute-start(bf16[2,128,512]{2,1,0:T(8,128)(2,1)S(1)} %get-tuple-element.90), channel_id=1, source_target_pairs={{0,2},{1,3},{2,0},{3,1},{4,6},{5,7},{6,4},{7,5},{8,10},{9,11},{10,... | collective-permute-start | bytes 786440 | tf_op jit(solution)/shard_map/ppermute | solution.py:22
  26.4 6.6 %collective-permute-start.5 = (bf16[2,128,512]{2,1,0:T(8,128)(2,1)S(1)}, bf16[2,128,512]{2,1,0:T(8,128)(2,1)S(1)}, u32[]{:S(2)}, u32[]{:S(2)}) collective-permute-start(bf16[2,128,512]{2,1,0:T(8,128)(2,1)S(1)} %get-tuple-element.91), channel_id=1, source_target_pairs={{0,4},{1,5},{2,6},{3,7},{4,0},{5,1},{6,2},{7,3},{8,12},{9,13},{10,... | collective-permute-start | bytes 786440 | tf_op jit(solution)/shard_map/ppermute | solution.py:22
  28.6 4.4 %collective-permute-start.13 = (bf16[64,2048]{1,0:T(8,128)(2,1)S(1)}, bf16[64,2048]{1,0:T(8,128)(2,1)S(1)}, u32[]{:S(2)}, u32[]{:S(2)}) collective-permute-start(bf16[64,2048]{1,0:T(8,128)(2,1)S(1)} %collective-permute-done.6.refs_0_.refs_6_), channel_id=1, source_target_pairs={{0,1},{1,0},{2,3},{3,2},{4,5},{5,4},{6,7},{7,6},{8,9},{9,8},{10,11... | collective-permute-start | bytes 786440 | tf_op jit(solution)/shard_map/ppermute | solution.py:22
  28.6 4.4 %collective-permute-start.14 = (bf16[64,2048]{1,0:T(8,128)(2,1)S(1)}, bf16[64,2048]{1,0:T(8,128)(2,1)S(1)}, u32[]{:S(2)}, u32[]{:S(2)}) collective-permute-start(bf16[64,2048]{1,0:T(8,128)(2,1)S(1)} %collective-permute-done.7.refs_1_.refs_7_), channel_id=1, source_target_pairs={{0,1},{1,0},{2,3},{3,2},{4,5},{5,4},{6,7},{7,6},{8,9},{9,8},{10,11... | collective-permute-start | bytes 786440 | tf_op jit(solution)/shard_map/ppermute | solution.py:22
  34.0 9.6 %collective-permute-start.12 = (bf16[2,128,512]{2,1,0:T(8,128)(2,1)S(1)}, bf16[2,128,512]{2,1,0:T(8,128)(2,1)S(1)}, u32[]{:S(2)}, u32[]{:S(2)}) collective-permute-start(bf16[2,128,512]{2,1,0:T(8,128)(2,1)S(1)} %get-tuple-element.101), channel_id=1, source_target_pairs={{0,6},{1,7},{2,4},{3,5},{4,2},{5,3},{6,0},{7,1},{8,14},{9,15},{10,... | collective-permute-start | bytes 786440 | tf_op jit(solution)/shard_map/ppermute | solution.py:22
  34.4 12.1 %collective-permute-start.16 = (bf16[512,128]{1,0:T(8,128)(2,1)S(1)}, bf16[512,128]{1,0:T(8,128)(2,1)S(1)}, u32[]{:S(2)}, u32[]{:S(2)}) collective-permute-start(bf16[512,128]{1,0:T(8,128)(2,1)S(1)} %get-tuple-element.84.refs_6_.refs_4_.w0), channel_id=1, source_target_pairs={{0,1},{1,0},{2,3},{3,2},{4,5},{5,4},{6,7},{7,6},{8,9},{9,8},{10,11... | collective-permute-start | bytes 393224 | tf_op jit(solution)/shard_map/ppermute | solution.py:22
  34.6 12.0 %collective-permute-start.17 = (bf16[512,128]{1,0:T(8,128)(2,1)S(1)}, bf16[512,128]{1,0:T(8,128)(2,1)S(1)}, u32[]{:S(2)}, u32[]{:S(2)}) collective-permute-start(bf16[512,128]{1,0:T(8,128)(2,1)S(1)} %collective-permute-done.2.refs_7_.refs_5_.w1), channel_id=1, source_target_pairs={{0,1},{1,0},{2,3},{3,2},{4,5},{5,4},{6,7},{7,6},{8,9},{9,8},{10,11... | collective-permute-start | bytes 393224 | tf_op jit(solution)/shard_map/ppermute | solution.py:22
  34.9 11.6 %collective-permute-start.18 = (bf16[512,128]{1,0:T(8,128)(2,1)S(1)}, bf16[512,128]{1,0:T(8,128)(2,1)S(1)}, u32[]{:S(2)}, u32[]{:S(2)}) collective-permute-start(bf16[512,128]{1,0:T(8,128)(2,1)S(1)} %collective-permute-done.3.refs_8_.refs_6_.w2), channel_id=1, source_target_pairs={{0,1},{1,0},{2,3},{3,2},{4,5},{5,4},{6,7},{7,6},{8,9},{9,8},{10,11... | collective-permute-start | bytes 393224 | tf_op jit(solution)/shard_map/ppermute | solution.py:22
  35.5 11.1 %collective-permute-start.19 = (bf16[512,128]{1,0:T(8,128)(2,1)S(1)}, bf16[512,128]{1,0:T(8,128)(2,1)S(1)}, u32[]{:S(2)}, u32[]{:S(2)}) collective-permute-start(bf16[512,128]{1,0:T(8,128)(2,1)S(1)} %collective-permute-done.11.refs_9_.refs_7_.w3), channel_id=1, source_target_pairs={{0,1},{1,0},{2,3},{3,2},{4,5},{5,4},{6,7},{7,6},{8,9},{9,8},{10,11... | collective-permute-start | bytes 393224 | tf_op jit(solution)/shard_map/ppermute | solution.py:22
  49.7 19.9 %collective-permute-start.21 = (bf16[2,128,1024]{2,1,0:T(8,128)(2,1)S(1)}, bf16[2,128,1024]{2,1,0:T(8,128)(2,1)S(1)}, u32[]{:S(2)}, u32[]{:S(2)}) collective-permute-start(bf16[2,128,1024]{2,1,0:T(8,128)(2,1)S(1)} %get-tuple-element.133), channel_id=1, source_target_pairs={{0,2},{1,3},{2,0},{3,1},{4,6},{5,7},{6,4},{7,5},{8,10},{9,11},{10,... | collective-permute-start | bytes 1572872 | tf_op jit(solution)/shard_map/ppermute | solution.py:22
  50.3 19.4 %collective-permute-start.22 = (bf16[2,128,1024]{2,1,0:T(8,128)(2,1)S(1)}, bf16[2,128,1024]{2,1,0:T(8,128)(2,1)S(1)}, u32[]{:S(2)}, u32[]{:S(2)}) collective-permute-start(bf16[2,128,1024]{2,1,0:T(8,128)(2,1)S(1)} %get-tuple-element.134), channel_id=1, source_target_pairs={{0,4},{1,5},{2,6},{3,7},{4,0},{5,1},{6,2},{7,3},{8,12},{9,13},{10,... | collective-permute-start | bytes 1572872 | tf_op jit(solution)/shard_map/ppermute | solution.py:22
  52.6 6.6 %collective-permute-start.23 = (bf16[512,128]{1,0:T(8,128)(2,1)S(1)}, bf16[512,128]{1,0:T(8,128)(2,1)S(1)}, u32[]{:S(2)}, u32[]{:S(2)}) collective-permute-start(bf16[512,128]{1,0:T(8,128)(2,1)S(1)} %get-tuple-element.136), channel_id=1, source_target_pairs={{0,8},{8,0},{16,24},{24,16},{1,9},{9,1},{17,25},{25,17},{2,10},{10... | collective-permute-start | bytes 393224 | tf_op jit(solution)/shard_map/ppermute | solution.py:22
  54.2 12.7 %collective-permute-start.24 = (bf16[512,128]{1,0:T(8,128)(2,1)S(1)}, bf16[512,128]{1,0:T(8,128)(2,1)S(1)}, u32[]{:S(2)}, u32[]{:S(2)}) collective-permute-start(bf16[512,128]{1,0:T(8,128)(2,1)S(1)} %get-tuple-element.137), channel_id=1, source_target_pairs={{0,16},{8,24},{16,0},{24,8},{1,17},{9,25},{17,1},{25,9},{2,18},{10... | collective-permute-start | bytes 393224 | tf_op jit(solution)/shard_map/ppermute | solution.py:22
  56.8 11.2 %collective-permute-start.25 = (bf16[512,128]{1,0:T(8,128)(2,1)S(1)}, bf16[512,128]{1,0:T(8,128)(2,1)S(1)}, u32[]{:S(2)}, u32[]{:S(2)}) collective-permute-start(bf16[512,128]{1,0:T(8,128)(2,1)S(1)} %get-tuple-element.138), channel_id=1, source_target_pairs={{0,24},{8,16},{16,8},{24,0},{1,25},{9,17},{17,9},{25,1},{2,26},{10... | collective-permute-start | bytes 393224 | tf_op jit(solution)/shard_map/ppermute | solution.py:22
  59.2 12.7 %collective-permute-start.31 = (bf16[2,128,512]{2,1,0:T(8,128)(2,1)S(1)}, bf16[2,128,512]{2,1,0:T(8,128)(2,1)S(1)}, u32[]{:S(2)}, u32[]{:S(2)}) collective-permute-start(bf16[2,128,512]{2,1,0:T(8,128)(2,1)S(1)} %get-tuple-element.143), channel_id=1, source_target_pairs={{0,6},{1,7},{2,4},{3,5},{4,2},{5,3},{6,0},{7,1},{8,14},{9,15},{10,... | collective-permute-start | bytes 786440 | tf_op jit(solution)/shard_map/ppermute | solution.py:22
  66.9 9.2 %collective-permute-start.29 = (bf16[2,128,512]{2,1,0:T(8,128)(2,1)S(1)}, bf16[2,128,512]{2,1,0:T(8,128)(2,1)S(1)}, u32[]{:S(2)}, u32[]{:S(2)}) collective-permute-start(bf16[2,128,512]{2,1,0:T(8,128)(2,1)S(1)} %get-tuple-element.141), channel_id=1, source_target_pairs={{0,2},{1,3},{2,0},{3,1},{4,6},{5,7},{6,4},{7,5},{8,10},{9,11},{10,... | collective-permute-start | bytes 786440 | tf_op jit(solution)/shard_map/ppermute | solution.py:22
  68.0 9.8 %collective-permute-start.30 = (bf16[2,128,512]{2,1,0:T(8,128)(2,1)S(1)}, bf16[2,128,512]{2,1,0:T(8,128)(2,1)S(1)}, u32[]{:S(2)}, u32[]{:S(2)}) collective-permute-start(bf16[2,128,512]{2,1,0:T(8,128)(2,1)S(1)} %get-tuple-element.142), channel_id=1, source_target_pairs={{0,4},{1,5},{2,6},{3,7},{4,0},{5,1},{6,2},{7,3},{8,12},{9,13},{10,... | collective-permute-start | bytes 786440 | tf_op jit(solution)/shard_map/ppermute | solution.py:22
  69.6 9.9 %collective-permute-start.28 = (bf16[512,128]{1,0:T(8,128)(2,1)S(1)}, bf16[512,128]{1,0:T(8,128)(2,1)S(1)}, u32[]{:S(2)}, u32[]{:S(2)}) collective-permute-start(bf16[512,128]{1,0:T(8,128)(2,1)S(1)} %last_kernel.1.refs_0_), channel_id=1, source_target_pairs={{0,2},{1,3},{2,0},{3,1},{4,6},{5,7},{6,4},{7,5},{8,10},{9,11},{10,... | collective-permute-start | bytes 393224 | tf_op jit(solution)/shard_map/ppermute | solution.py:22
  71.8 10.7 %collective-permute-start.26 = (bf16[512,128]{1,0:T(8,128)(2,1)S(1)}, bf16[512,128]{1,0:T(8,128)(2,1)S(1)}, u32[]{:S(2)}, u32[]{:S(2)}) collective-permute-start(bf16[512,128]{1,0:T(8,128)(2,1)S(1)} %last_kernel.1.refs_0_), channel_id=1, source_target_pairs={{0,4},{1,5},{2,6},{3,7},{4,0},{5,1},{6,2},{7,3},{8,12},{9,13},{10,... | collective-permute-start | bytes 393224 | tf_op jit(solution)/shard_map/ppermute | solution.py:22
  71.9 10.7 %collective-permute-start.27 = (bf16[512,128]{1,0:T(8,128)(2,1)S(1)}, bf16[512,128]{1,0:T(8,128)(2,1)S(1)}, u32[]{:S(2)}, u32[]{:S(2)}) collective-permute-start(bf16[512,128]{1,0:T(8,128)(2,1)S(1)} %last_kernel.1.refs_0_), channel_id=1, source_target_pairs={{0,6},{1,7},{2,4},{3,5},{4,2},{5,3},{6,0},{7,1},{8,14},{9,15},{10,... | collective-permute-start | bytes 393224 | tf_op jit(solution)/shard_map/ppermute | solution.py:22
  76.1 10.3 %collective-permute-start.36 = (bf16[128,1024]{1,0:T(8,128)(2,1)S(1)}, bf16[128,1024]{1,0:T(8,128)(2,1)S(1)}, u32[]{:S(2)}, u32[]{:S(2)}) collective-permute-start(bf16[128,1024]{1,0:T(8,128)(2,1)S(1)} %get-tuple-element.159), channel_id=1, source_target_pairs={{0,4},{1,5},{2,6},{3,7},{4,0},{5,1},{6,2},{7,3},{8,12},{9,13},{10,... | collective-permute-start | bytes 786440 | tf_op jit(solution)/shard_map/ppermute | solution.py:22
  77.8 8.6 %collective-permute-start.37 = (bf16[128,1024]{1,0:T(8,128)(2,1)S(1)}, bf16[128,1024]{1,0:T(8,128)(2,1)S(1)}, u32[]{:S(2)}, u32[]{:S(2)}) collective-permute-start(bf16[128,1024]{1,0:T(8,128)(2,1)S(1)} %get-tuple-element.161), channel_id=1, source_target_pairs={{0,2},{1,3},{2,0},{3,1},{4,6},{5,7},{6,4},{7,5},{8,10},{9,11},{10,... | collective-permute-start | bytes 786440 | tf_op jit(solution)/shard_map/ppermute | solution.py:22
  (7 other events, 34.4 us)
